TPU v7x, 512 devices: a whole 4x4x16 slice. The times are simulated.
512 devices in a mesh: grp: 16 (over z), seq: 32 (over y, x, core).
Axes of the slice: x: 4, y: 4, z: 16, core: 2. Of those that a mesh axis runs over, the one named last changes fastest.
Arguments:
- queries: bfloat16 [32, 1024, 128], P('seq'), may hold values from -8 to 8
- scene_keys: bfloat16 [65536, 2048], P(('grp', 'seq')), may hold values from -8 to 8
- scene_values: bfloat16 [65536, 2048], P(('grp', 'seq')), may hold values from -6 to 6
- grad_output: bfloat16 [32, 1024, 128], P('seq'), may hold values from -6 to 6
- tile_list: int32 [16, 32, 9, 2], P('grp', 'seq'), may hold values from 0 to 7, as said below
- tile_counts: int32 [16, 32], P('grp', 'seq'), may hold values from 2 to 9, as said below
Outputs:
- attended: bfloat16 [32, 1024, 128], P('seq')
- grad_queries: bfloat16 [32, 1024, 128], P('seq')
- grad_keys: bfloat16 [65536, 2048], P(('grp', 'seq'))
- grad_values: bfloat16 [65536, 2048], P(('grp', 'seq'))
Inputs may be any that keep to these rules, and one draw needn't show every extreme that they name: For each group g and item i: every one of the 2 query blocks appears in at least one of the first tile_counts[g, i] entries; some group and item list 9 tiles and some list 2. The first tile_counts[g, i] entries of tile_list[g, i] are distinct pairs (query block below 2, key block below 8) in no particular order; the later entries are unused.
All inputs are finite; a program needn't handle non-finite values.
Results may differ from a plain program's by a relative error of at most 0.024.
Values may be sent and summed in bfloat16 or wider, within the bound.
A program may use at most 64 MiB of HBM per device.

v0:
```python
import jax
import jax.numpy as jnp
from jax import lax
from jax.sharding import PartitionSpec as P

QPARTS = 2
QBLK = 512
KBLK = 512


NEG_START = -1e30


def tile_scores(query_block, key_block, softmax_scale):
    return (
        lax.dot_general(
            query_block, key_block, (((1,), (1,)), ((), ())), preferred_element_type=jnp.float32
        )
        * softmax_scale
    )


def forward_item(query_item, key_head, value_head, listing, live_tiles, softmax_scale):
    query_rows = query_item.shape[0]
    head_width = query_item.shape[1]

    def forward_visit_tile(position, running):
        run_max, run_total, run_accum = running
        query_start = listing[position, 0] * QBLK
        key_start = listing[position, 1] * KBLK
        query_block = lax.dynamic_slice_in_dim(query_item, query_start, QBLK, 0)
        key_block = lax.dynamic_slice_in_dim(key_head, key_start, KBLK, 0)
        value_block = lax.dynamic_slice_in_dim(value_head, key_start, KBLK, 0)
        scores = tile_scores(query_block, key_block, softmax_scale)
        old_max = lax.dynamic_slice_in_dim(run_max, query_start, QBLK, 0)
        old_total = lax.dynamic_slice_in_dim(run_total, query_start, QBLK, 0)
        old_accum = lax.dynamic_slice_in_dim(run_accum, query_start, QBLK, 0)
        new_max = jnp.maximum(old_max, jnp.max(scores, axis=1))
        weights = jnp.exp(scores - new_max[:, None])
        shrink = jnp.exp(old_max - new_max)
        new_total = old_total * shrink + jnp.sum(weights, axis=1)
        new_accum = old_accum * shrink[:, None] + jnp.dot(
            weights.astype(jnp.bfloat16), value_block, preferred_element_type=jnp.float32
        )
        run_max = lax.dynamic_update_slice_in_dim(run_max, new_max, query_start, 0)
        run_total = lax.dynamic_update_slice_in_dim(run_total, new_total, query_start, 0)
        run_accum = lax.dynamic_update_slice_in_dim(run_accum, new_accum, query_start, 0)
        return (run_max, run_total, run_accum)

    initial = (
        jnp.full((query_rows,), NEG_START, jnp.float32),
        jnp.zeros((query_rows,), jnp.float32),
        jnp.zeros((query_rows, head_width), jnp.float32),
    )
    return lax.fori_loop(0, live_tiles, forward_visit_tile, initial)


def backward_item(
    query_item,
    key_head,
    value_head,
    grad_item,
    log_total,
    deltas,
    listing,
    live_tiles,
    softmax_scale,
):
    query_rows = query_item.shape[0]
    head_width = query_item.shape[1]
    key_rows = key_head.shape[0]

    def backward_visit_tile(position, running):
        query_grad, key_grad, value_grad = running
        query_start = listing[position, 0] * QBLK
        key_start = listing[position, 1] * KBLK
        query_block = lax.dynamic_slice_in_dim(query_item, query_start, QBLK, 0)
        grad_block = lax.dynamic_slice_in_dim(grad_item, query_start, QBLK, 0)
        key_block = lax.dynamic_slice_in_dim(key_head, key_start, KBLK, 0)
        value_block = lax.dynamic_slice_in_dim(value_head, key_start, KBLK, 0)
        log_block = lax.dynamic_slice_in_dim(log_total, query_start, QBLK, 0)
        delta_block = lax.dynamic_slice_in_dim(deltas, query_start, QBLK, 0)
        scores = tile_scores(query_block, key_block, softmax_scale)
        probs = jnp.exp(scores - log_block[:, None])
        probs_half = probs.astype(jnp.bfloat16)
        value_term = lax.dot_general(
            probs_half, grad_block, (((0,), (0,)), ((), ())), preferred_element_type=jnp.float32
        )
        prob_grad = lax.dot_general(
            grad_block, value_block, (((1,), (1,)), ((), ())), preferred_element_type=jnp.float32
        )
        score_grad = (probs * (prob_grad - delta_block[:, None])).astype(jnp.bfloat16)
        query_term = (
            jnp.dot(score_grad, key_block, preferred_element_type=jnp.float32) * softmax_scale
        )
        key_term = (
            lax.dot_general(
                score_grad,
                query_block,
                (((0,), (0,)), ((), ())),
                preferred_element_type=jnp.float32,
            )
            * softmax_scale
        )
        query_grad = lax.dynamic_update_slice_in_dim(
            query_grad,
            lax.dynamic_slice_in_dim(query_grad, query_start, QBLK, 0) + query_term,
            query_start,
            0,
        )
        key_grad = lax.dynamic_update_slice_in_dim(
            key_grad,
            lax.dynamic_slice_in_dim(key_grad, key_start, KBLK, 0) + key_term,
            key_start,
            0,
        )
        value_grad = lax.dynamic_update_slice_in_dim(
            value_grad,
            lax.dynamic_slice_in_dim(value_grad, key_start, KBLK, 0) + value_term,
            key_start,
            0,
        )
        return (query_grad, key_grad, value_grad)

    initial = (
        jnp.zeros((query_rows, head_width), jnp.float32),
        jnp.zeros((key_rows, head_width), jnp.float32),
        jnp.zeros((key_rows, head_width), jnp.float32),
    )
    return lax.fori_loop(0, live_tiles, backward_visit_tile, initial)


def per_device(queries, scene_keys, scene_values, grad_output, tile_list, tile_counts):
    items_here = queries.shape[0]
    head_width = queries.shape[2]
    scene_here = scene_keys.shape[0]
    heads_total = scene_keys.shape[1] // head_width
    seq_devices = lax.axis_size("seq")
    group_keys = scene_here * seq_devices
    copies = max(1, QPARTS // items_here)
    heads_here = max(1, items_here // QPARTS)
    softmax_scale = head_width ** (-0.5)
    key_wide = jnp.repeat(
        scene_keys.reshape(scene_here, heads_total, head_width), copies, axis=1
    ).reshape(scene_here, -1)
    value_wide = jnp.repeat(
        scene_values.reshape(scene_here, heads_total, head_width), copies, axis=1
    ).reshape(scene_here, -1)
    key_group, value_group = (
        lax.all_to_all(key_wide, "seq", split_axis=1, concat_axis=0, tiled=True),
        lax.all_to_all(value_wide, "seq", split_axis=1, concat_axis=0, tiled=True),
    )
    key_group = key_group.reshape(group_keys, heads_here, head_width)
    value_group = value_group.reshape(group_keys, heads_here, head_width)
    maxima, totals, accums = ([], [], [])
    item_index = 0
    local_head = item_index // QPARTS
    part_max, part_total, part_accum = forward_item(
        queries[item_index],
        key_group[:, local_head, :],
        value_group[:, local_head, :],
        tile_list[0, item_index],
        tile_counts[0, item_index],
        softmax_scale,
    )
    maxima.append(part_max)
    totals.append(part_total)
    accums.append(part_accum)
    local_max = jnp.stack(maxima)
    local_total = jnp.stack(totals)
    local_accum = jnp.stack(accums)
    global_max = lax.pmax(local_max, "grp")
    shrink = jnp.exp(local_max - global_max)
    global_total, global_accum = lax.psum(
        (local_total * shrink, local_accum * shrink[..., None]), "grp"
    )
    attended = (global_accum / global_total[..., None]).astype(jnp.bfloat16)
    log_total = global_max + jnp.log(global_total)
    deltas = jnp.sum(attended.astype(jnp.float32) * grad_output.astype(jnp.float32), axis=2)
    query_grads, key_parts, value_parts = ([], [], [])
    item_index = 0
    local_head = item_index // QPARTS
    query_grad, key_grad, value_grad = backward_item(
        queries[item_index],
        key_group[:, local_head, :],
        value_group[:, local_head, :],
        grad_output[item_index],
        log_total[item_index],
        deltas[item_index],
        tile_list[0, item_index],
        tile_counts[0, item_index],
        softmax_scale,
    )
    query_grads.append(query_grad)
    key_parts.append(key_grad.astype(jnp.bfloat16))
    value_parts.append(value_grad.astype(jnp.bfloat16))
    key_heads, value_heads = ([], [])
    members = [index_one for index_one in range(items_here) if index_one // QPARTS == 0]
    key_sum = key_parts[members[0]].astype(jnp.float32)
    value_sum = value_parts[members[0]].astype(jnp.float32)
    key_heads.append(key_sum.astype(jnp.bfloat16))
    value_heads.append(value_sum.astype(jnp.bfloat16))
    key_stack = jnp.stack(key_heads, axis=1)
    value_stack = jnp.stack(value_heads, axis=1)
    key_back, value_back = (
        lax.all_to_all(
            key_stack.reshape(group_keys, -1), "seq", split_axis=0, concat_axis=1, tiled=True
        ),
        lax.all_to_all(
            value_stack.reshape(group_keys, -1), "seq", split_axis=0, concat_axis=1, tiled=True
        ),
    )
    grad_keys = (
        jnp.sum(
            key_back.reshape(scene_here, heads_total, copies, head_width).astype(jnp.float32),
            axis=2,
        )
        .astype(jnp.bfloat16)
        .reshape(scene_here, -1)
    )
    grad_values = (
        jnp.sum(
            value_back.reshape(scene_here, heads_total, copies, head_width).astype(jnp.float32),
            axis=2,
        )
        .astype(jnp.bfloat16)
        .reshape(scene_here, -1)
    )
    grad_queries = lax.psum(jnp.stack(query_grads), "grp").astype(jnp.bfloat16)
    return (attended, grad_queries, grad_keys, grad_values)


def solution(mesh):
    in_specs = (
        P("seq", None, None),
        P(("grp", "seq"), None),
        P(("grp", "seq"), None),
        P("seq", None, None),
        P("grp", "seq", None, None),
        P("grp", "seq"),
    )
    out_specs = (
        P("seq", None, None),
        P("seq", None, None),
        P(("grp", "seq"), None),
        P(("grp", "seq"), None),
    )
    return jax.shard_map(
        per_device, mesh=mesh, in_specs=in_specs, out_specs=out_specs, check_vma=False
    )
```

profile of v0, /device:TPU:6, one launch (start us, length us, event | category | flops | bytes accessed | tf_op | source)
XLA Modules:
  0.0 428.1 jit_solution(13124028591319190804)
XLA Ops:
  9.6 9.5 %all-to-all-start = ((bf16[128,32,128]{2,0,1:T(8,128)(2,1)}), bf16[128,32,128]{2,0,1:T(8,128)(2,1)S(1)}, u32[]{:S(2)}, u32[]{:S(2)}) async-start(bf16[128,32,128]{2,0,1:T(8,128)(2,1)} %bitcast.67), calls=%async_computation | async-start | bytes 2097152 | tf_op jit(solution)/shard_map/all_to_all | solution.py:150
  19.2 14.5 %all-to-all-done = bf16[128,32,128]{2,0,1:T(8,128)(2,1)S(1)} async-done(((bf16[128,32,128]{2,0,1:T(8,128)(2,1)}), bf16[128,32,128]{2,0,1:T(8,128)(2,1)S(1)}, u32[]{:S(2)}, u32[]{:S(2)}) %all-to-all-start) | async-done | bytes 1048608 | tf_op jit(solution)/shard_map/all_to_all | solution.py:150
  35.0 7.2 %all-to-all-start.1 = ((bf16[128,32,128]{2,0,1:T(8,128)(2,1)}), bf16[128,32,128]{2,0,1:T(8,128)(2,1)}, u32[]{:S(2)}, u32[]{:S(2)}) async-start(bf16[128,32,128]{2,0,1:T(8,128)(2,1)} %bitcast.66), calls=%async_computation.1 | async-start | bytes 2097152 | tf_op jit(solution)/shard_map/all_to_all | solution.py:151
  42.2 14.7 %all-to-all-done.1 = bf16[128,32,128]{2,0,1:T(8,128)(2,1)} async-done(((bf16[128,32,128]{2,0,1:T(8,128)(2,1)}), bf16[128,32,128]{2,0,1:T(8,128)(2,1)}, u32[]{:S(2)}, u32[]{:S(2)}) %all-to-all-start.1) | async-done | bytes 1048608 | tf_op jit(solution)/shard_map/all_to_all | solution.py:151
  57.0 19.6 %while.28 = (s32[]{:T(128)}, f32[1024]{0:T(1024)S(1)}, f32[1024]{0:T(1024)S(1)}, f32[1024,128]{1,0:T(8,128)S(1)}, s32[]{:T(128)}, /*index=5*/s32[9,2]{0,1:T(2,12...) while((s32[]{:T(128)}, f32[1024]{0:T(1024)S(1)}, ...), condition=%wide.region_3.0_spmd, body=%wide.region_0.0_spmd.sunk | while | flops 135922704 | bytes 4110655 | solution.py:55
  76.7 47.5 %pmax.7 = f32[1,1024]{1,0:T(1,128)S(1)} all-reduce(f32[1,1024]{1,0:T(1,128)S(1)} %bitcast.70), channel_id=1, replica_groups=mesh['grp'=16,'seq'=32] {'grp'}, use_global_device_ids=true, to_apply=%region_4.0 | all-reduce | flops 1024 | bytes 8192 | tf_op jit(solution)/shard_map/pmax | solution.py:172
  125.2 27.1 %psum.22 = f32[1,1024]{1,0:T(1,128)S(1)} all-reduce(f32[1,1024]{1,0:T(1,128)S(1)} %get-tuple-element.177), channel_id=1, replica_groups=mesh['grp'=16,'seq'=32] {'grp'}, use_global_device_ids=true, to_apply=%region_6.0 | all-reduce | flops 1024 | bytes 8192 | tf_op jit(solution)/shard_map/psum | solution.py:174
  152.3 102.9 %all-reduce.3.cloned.1.call-done = f32[1,1024,128]{2,1,0:T(8,128)} async-done(((f32[1,1024,128]{2,1,0:T(8,128)}), f32[1,1024,128]{2,1,0:T(8,128)}) %all-reduce.3.cloned.1.call-update) | async-done | bytes 524304 | tf_op jit(solution)/shard_map/psum | solution.py:174
  255.2 2.0 multiply_reduce_fusion
  257.3 1.5 broadcast.23
  258.8 36.1 %while.29 = (s32[]{:T(128)}, f32[1024,128]{1,0:T(8,128)S(1)}, f32[4096,128]{1,0:T(8,128)}, f32[4096,128]{1,0:T(8,128)S(1)}, s32[]{:T(128)}, /*index=5*/s32[9,2]{...) while((s32[]{:T(128)}, f32[1024,128]{1,0:T(8,128)S(1)}, ...), condition=%wide.region_9.0_spmd, body=%wide.region_8.0_spmd.sunk | while | flops 337444864 | bytes 8270219 | solution.py:130
  262.8 1.3 fusion.77
  265.6 2.0 fusion.79
  271.6 1.3 fusion.77
  274.5 2.0 fusion.79
  280.5 1.3 fusion.77
  283.4 2.0 fusion.79
  289.4 1.3 fusion.77
  292.2 2.0 fusion.79
  296.0 16.2 %all-to-all-start.3 = ((bf16[32,128,128]{2,1,0:T(8,128)(2,1)}), bf16[32,128,128]{2,1,0:T(8,128)(2,1)}, u32[]{:S(2)}, u32[]{:S(2)}) async-start(bf16[32,128,128]{2,1,0:T(8,128)(2,1)} %bitcast.65), calls=%async_computation.3 | async-start | bytes 2097152 | tf_op jit(solution)/shard_map/all_to_all | solution.py:209
  313.3 13.6 %all-to-all-done.3 = bf16[32,128,128]{2,1,0:T(8,128)(2,1)} async-done(((bf16[32,128,128]{2,1,0:T(8,128)(2,1)}), bf16[32,128,128]{2,1,0:T(8,128)(2,1)}, u32[]{:S(2)}, u32[]{:S(2)}) %all-to-all-start.3) | async-done | bytes 1048608 | tf_op jit(solution)/shard_map/all_to_all | solution.py:209
  326.9 6.6 %all-to-all-start.2 = ((bf16[32,128,128]{2,1,0:T(8,128)(2,1)}), bf16[32,128,128]{2,1,0:T(8,128)(2,1)S(1)}, u32[]{:S(2)}, u32[]{:S(2)}) async-start(bf16[32,128,128]{2,1,0:T(8,128)(2,1)} %bitcast.64), calls=%async_computation.2 | async-start | bytes 2097152 | tf_op jit(solution)/shard_map/all_to_all | solution.py:206
  333.4 83.7 %all-reduce.4 = bf16[1,1024,128]{2,1,0:T(8,128)(2,1)} all-reduce(f32[1,1024,128]{2,1,0:T(8,128)S(1)} %bitcast.61), channel_id=1, replica_groups=mesh['grp'=16,'seq'=32] {'grp'}, use_global_device_ids=true, to_apply=%region_10.0 | all-reduce | flops 131072 | bytes 786432 | tf_op jit(solution)/shard_map/psum | solution.py:229
  417.1 1.4 bitcast_reduce_fusion
  (100 shorter events, 35.2 us)
Async XLA Ops:
  7.2 1.0 copy-start
  8.3 10.7 %copy-start.6 = (bf16[128,2048]{1,0:T(8,128)(2,1)S(1)}, bf16[128,2048]{1,0:T(8,128)(2,1)}, u32[]{:S(2)}) copy-start(bf16[128,2048]{1,0:T(8,128)(2,1)} %param.12) | copy-start | bytes 1572868
  9.6 24.2 %all-to-all-start = ((bf16[128,32,128]{2,0,1:T(8,128)(2,1)}), bf16[128,32,128]{2,0,1:T(8,128)(2,1)S(1)}, u32[]{:S(2)}, u32[]{:S(2)}) async-start(bf16[128,32,128]{2,0,1:T(8,128)(2,1)} %bitcast.67), calls=%async_computation | async-start | bytes 2097152 | tf_op jit(solution)/shard_map/all_to_all | solution.py:150
  19.2 37.8 %copy-start.1 = (bf16[1,1024,128]{2,1,0:T(8,128)(2,1)S(1)}, bf16[1,1024,128]{2,1,0:T(8,128)(2,1)}, u32[]{:S(2)}) copy-start(bf16[1,1024,128]{2,1,0:T(8,128)(2,1)} %param.10) | copy-start | bytes 786436
  19.2 37.8 %copy-start.7 = (s32[1,1,9,2]{2,3,1,0:T(2,128)S(1)}, s32[1,1,9,2]{2,3,1,0:T(2,128)}, u32[]{:S(2)}) copy-start(s32[1,1,9,2]{2,3,1,0:T(2,128)} %param.14) | copy-start | bytes 220
  35.0 22.0 %all-to-all-start.1 = ((bf16[128,32,128]{2,0,1:T(8,128)(2,1)}), bf16[128,32,128]{2,0,1:T(8,128)(2,1)}, u32[]{:S(2)}, u32[]{:S(2)}) async-start(bf16[128,32,128]{2,0,1:T(8,128)(2,1)} %bitcast.66), calls=%async_computation.1 | async-start | bytes 2097152 | tf_op jit(solution)/shard_map/all_to_all | solution.py:151
  42.2 213.0 %all-reduce.3.cloned.1.call-start = ((), (), s32[]{:S(2)}) async-start(), calls=%async_computation.4 | async-start | bytes 1048576 | tf_op jit(solution)/shard_map/psum | solution.py:174
  57.0 198.1 %copy-start.3 = (bf16[1,1024,128]{2,1,0:T(8,128)(2,1)S(1)}, bf16[1,1024,128]{2,1,0:T(8,128)(2,1)}, u32[]{:S(2)}) copy-start(bf16[1,1024,128]{2,1,0:T(8,128)(2,1)} %param.13) | copy-start | bytes 786436
  76.6 180.5 %copy-start.5 = (bf16[4096,128]{1,0:T(8,128)(2,1)}, bf16[4096,128]{1,0:T(8,128)(2,1)S(1)}, u32[]{:S(2)}) copy-start(bf16[4096,128]{1,0:T(8,128)(2,1)S(1)} %get-tuple-element.437) | copy-start | bytes 3145732
  261.5 3.8 copy-start.4
  270.3 3.8 copy-start.4
  279.2 3.8 copy-start.4
  288.1 3.8 copy-start.4
  296.0 16.2 %copy-start.2 = (f32[4096,128]{1,0:T(8,128)S(1)}, f32[4096,128]{1,0:T(8,128)}, u32[]{:S(2)}) copy-start(f32[4096,128]{1,0:T(8,128)} %get-tuple-element.123) | copy-start | bytes 6291460
  296.0 30.9 %all-to-all-start.3 = ((bf16[32,128,128]{2,1,0:T(8,128)(2,1)}), bf16[32,128,128]{2,1,0:T(8,128)(2,1)}, u32[]{:S(2)}, u32[]{:S(2)}) async-start(bf16[32,128,128]{2,1,0:T(8,128)(2,1)} %bitcast.65), calls=%async_computation.3 | async-start | bytes 2097152 | tf_op jit(solution)/shard_map/all_to_all | solution.py:209
  326.9 93.0 %all-to-all-start.2 = ((bf16[32,128,128]{2,1,0:T(8,128)(2,1)}), bf16[32,128,128]{2,1,0:T(8,128)(2,1)S(1)}, u32[]{:S(2)}, u32[]{:S(2)}) async-start(bf16[32,128,128]{2,1,0:T(8,128)(2,1)} %bitcast.64), calls=%async_computation.2 | async-start | bytes 2097152 | tf_op jit(solution)/shard_map/all_to_all | solution.py:206
Sparse Core Ops, SparseCore 0:
  125.3 129.8 all-reduce.2
where the time goes:
time: 430 us; the launch traced here: 428 us
  blocking collectives  158 us (37%)
  waiting for transfers between devices  146 us (34%)
  starting transfers between devices  39.5 us (9%)
  matrix products  30.8 us (7%)
  loops' own time  17.4 us (4%)
  between operations  14.2 us (3%)
  local copies, waits for them, and re-layouts  13.4 us (3%)
  other arithmetic  8.93 us (2%)
    psum x1, waiting for transfers between devices, per_device(): lax.psum((local_total * shrink, local_accum * shrink[..., None]), 'grp')  103 us
    psum x1, blocking collectives, per_device(): grad_queries = lax.psum(jnp.stack(query_grads), 'grp').astype(jnp.bfloat16)  83.7 us
    pmax x1, blocking collectives, per_device(): global_max = lax.pmax(local_max, 'grp')  47.5 us
    psum x1, blocking collectives, per_device(): lax.psum((local_total * shrink, local_accum * shrink[..., None]), 'grp')  27.1 us
    all_to_all x1, starting transfers between devices, per_device(): lax.all_to_all(value_stack.reshape(group_keys, -1), 'seq', split_axis=0,...  16.2 us
    all_to_all x1, waiting for transfers between devices, per_device(): lax.all_to_all(value_wide, 'seq', split_axis=1, concat_axis=0, tiled=True)  14.7 us
    all_to_all x1, waiting for transfers between devices, per_device(): lax.all_to_all(key_wide, 'seq', split_axis=1, concat_axis=0, tiled=True)  14.5 us
    all_to_all x1, waiting for transfers between devices, per_device(): lax.all_to_all(value_stack.reshape(group_keys, -1), 'seq', split_axis=0,...  13.6 us
  transfers between devices with their start and end apart: 5, of which 4 were waited for; matrix products, arithmetic and copies ran while one was open for 1% of the time, Pallas kernels for 0%

commit v1 on v0

--- a/solution.py
+++ b/solution.py
@@ -130,12 +130,31 @@
     return lax.fori_loop(0, live_tiles, backward_visit_tile, initial)
 
 
+def scatter_rows(rows, parts):
+    return lax.all_to_all(
+        rows.reshape(parts, rows.shape[0] // parts, rows.shape[1]),
+        "grp",
+        split_axis=0,
+        concat_axis=0,
+        tiled=True,
+    )
+
+
+def broadcast_rows(chunk, parts):
+    spread = jnp.broadcast_to(chunk[None], (parts,) + chunk.shape)
+    gathered = lax.all_to_all(spread, "grp", split_axis=0, concat_axis=0, tiled=True)
+    return gathered.reshape(parts * chunk.shape[0], chunk.shape[1])
+
+
 def per_device(queries, scene_keys, scene_values, grad_output, tile_list, tile_counts):
     items_here = queries.shape[0]
     head_width = queries.shape[2]
+    query_rows = queries.shape[1]
     scene_here = scene_keys.shape[0]
     heads_total = scene_keys.shape[1] // head_width
     seq_devices = lax.axis_size("seq")
+    groups = lax.axis_size("grp")
+    chunk_rows = query_rows // groups
     group_keys = scene_here * seq_devices
     copies = max(1, QPARTS // items_here)
     heads_here = max(1, items_here // QPARTS)
@@ -152,56 +171,50 @@
     )
     key_group = key_group.reshape(group_keys, heads_here, head_width)
     value_group = value_group.reshape(group_keys, heads_here, head_width)
-    maxima, totals, accums = ([], [], [])
-    item_index = 0
-    local_head = item_index // QPARTS
     part_max, part_total, part_accum = forward_item(
-        queries[item_index],
-        key_group[:, local_head, :],
-        value_group[:, local_head, :],
-        tile_list[0, item_index],
-        tile_counts[0, item_index],
+        queries[0],
+        key_group[:, 0, :],
+        value_group[:, 0, :],
+        tile_list[0, 0],
+        tile_counts[0, 0],
         softmax_scale,
     )
-    maxima.append(part_max)
-    totals.append(part_total)
-    accums.append(part_accum)
-    local_max = jnp.stack(maxima)
-    local_total = jnp.stack(totals)
-    local_accum = jnp.stack(accums)
-    global_max = lax.pmax(local_max, "grp")
-    shrink = jnp.exp(local_max - global_max)
-    global_total, global_accum = lax.psum(
-        (local_total * shrink, local_accum * shrink[..., None]), "grp"
-    )
-    attended = (global_accum / global_total[..., None]).astype(jnp.bfloat16)
-    log_total = global_max + jnp.log(global_total)
+    stats = jnp.concatenate(
+        [part_max.reshape(groups, 1, chunk_rows), part_total.reshape(groups, 1, chunk_rows)],
+        axis=2,
+    )
+    packed = jnp.concatenate([part_accum.reshape(groups, chunk_rows, head_width), stats], axis=1)
+    arrived = scatter_rows(packed.reshape(groups * (chunk_rows + 1), head_width), groups)
+    arrived = arrived.reshape(groups, chunk_rows + 1, head_width)
+    got_accum = arrived[:, :chunk_rows, :]
+    got_max = arrived[:, chunk_rows, :chunk_rows]
+    got_total = arrived[:, chunk_rows, chunk_rows:]
+    top = jnp.max(got_max, axis=0)
+    shrink = jnp.exp(got_max - top[None, :])
+    chunk_total = jnp.sum(got_total * shrink, axis=0)
+    chunk_accum = jnp.sum(got_accum * shrink[:, :, None], axis=0)
+    chunk_out = (chunk_accum / chunk_total[:, None]).astype(jnp.bfloat16)
+    chunk_log = top + jnp.log(chunk_total)
+    log_row = jnp.concatenate([chunk_log, jnp.zeros((chunk_rows,), jnp.float32)])
+    back = broadcast_rows(
+        jnp.concatenate([chunk_out.astype(jnp.float32), log_row[None, :]], axis=0), groups
+    ).reshape(groups, chunk_rows + 1, head_width)
+    attended = back[:, :chunk_rows, :].reshape(1, query_rows, head_width).astype(jnp.bfloat16)
+    log_total = back[:, chunk_rows, :chunk_rows].reshape(1, query_rows)
     deltas = jnp.sum(attended.astype(jnp.float32) * grad_output.astype(jnp.float32), axis=2)
-    query_grads, key_parts, value_parts = ([], [], [])
-    item_index = 0
-    local_head = item_index // QPARTS
     query_grad, key_grad, value_grad = backward_item(
-        queries[item_index],
-        key_group[:, local_head, :],
-        value_group[:, local_head, :],
-        grad_output[item_index],
-        log_total[item_index],
-        deltas[item_index],
-        tile_list[0, item_index],
-        tile_counts[0, item_index],
+        queries[0],
+        key_group[:, 0, :],
+        value_group[:, 0, :],
+        grad_output[0],
+        log_total[0],
+        deltas[0],
+        tile_list[0, 0],
+        tile_counts[0, 0],
         softmax_scale,
     )
-    query_grads.append(query_grad)
-    key_parts.append(key_grad.astype(jnp.bfloat16))
-    value_parts.append(value_grad.astype(jnp.bfloat16))
-    key_heads, value_heads = ([], [])
-    members = [index_one for index_one in range(items_here) if index_one // QPARTS == 0]
-    key_sum = key_parts[members[0]].astype(jnp.float32)
-    value_sum = value_parts[members[0]].astype(jnp.float32)
-    key_heads.append(key_sum.astype(jnp.bfloat16))
-    value_heads.append(value_sum.astype(jnp.bfloat16))
-    key_stack = jnp.stack(key_heads, axis=1)
-    value_stack = jnp.stack(value_heads, axis=1)
+    key_stack = key_grad.astype(jnp.bfloat16)[:, None, :]
+    value_stack = value_grad.astype(jnp.bfloat16)[:, None, :]
     key_back, value_back = (
         lax.all_to_all(
             key_stack.reshape(group_keys, -1), "seq", split_axis=0, concat_axis=1, tiled=True
@@ -226,7 +239,9 @@
         .astype(jnp.bfloat16)
         .reshape(scene_here, -1)
     )
-    grad_queries = lax.psum(jnp.stack(query_grads), "grp").astype(jnp.bfloat16)
+    query_parts = scatter_rows(query_grad, groups)
+    query_chunk = jnp.sum(query_parts, axis=0).astype(jnp.bfloat16)
+    grad_queries = broadcast_rows(query_chunk, groups).reshape(1, query_rows, head_width)
     return (attended, grad_queries, grad_keys, grad_values)
 
 

time: 430 us -> 367 us (0.85)
  the two profiles are of different devices: /device:TPU:6 before, /device:TPU:1 now
where the time goes in v1:
time: 367 us; the launch traced here: 361 us
  blocking collectives  144 us (39%)
  waiting for transfers between devices  109 us (30%)
  starting transfers between devices  61.2 us (17%)
  matrix products  18.6 us (5%)
  local copies, waits for them, and re-layouts  14.4 us (4%)
  loops' own time  9.24 us (3%)
    all_to_all x1, blocking collectives, per_device(): lax.all_to_all(key_stack.reshape(group_keys, -1), 'seq', split_axis=0, co...  83.7 us
    all_to_all x1, blocking collectives, scatter_rows(): lax.all_to_all(rows.reshape(parts, rows.shape[0] // parts, rows.shape[1])...  60.5 us
    all_to_all x2, waiting for transfers between devices, broadcast_rows(): lax.all_to_all(spread, 'grp', split_axis=0, concat_axis=0, tiled=True)  35.7 us
    all_to_all x1, waiting for transfers between devices, scatter_rows(): lax.all_to_all(rows.reshape(parts, rows.shape[0] // parts, rows.shape[1])...  21.6 us
    all_to_all x1, starting transfers between devices, scatter_rows(): lax.all_to_all(rows.reshape(parts, rows.shape[0] // parts, rows.shape[1])...  20.3 us
    all_to_all x1, waiting for transfers between devices, per_device(): lax.all_to_all(key_wide, 'seq', split_axis=1, concat_axis=0, tiled=True)  17.3 us
    all_to_all x1, waiting for transfers between devices, per_device(): lax.all_to_all(value_stack.reshape(group_keys, -1), 'seq', split_axis=0,...  17.2 us
    all_to_all x1, waiting for transfers between devices, per_device(): lax.all_to_all(value_wide, 'seq', split_axis=1, concat_axis=0, tiled=True)  17.2 us
  transfers between devices with their start and end apart: 6, of which 6 were waited for; matrix products, arithmetic and copies ran while one was open for 1% of the time, Pallas kernels for 0%

profile of v1, /device:TPU:1, one launch (start us, length us, event | category | flops | bytes accessed | tf_op | source)
XLA Modules:
  0.0 360.9 jit_solution(12899739702436949643)
XLA Ops:
  1.8 1.3 broadcast_in_dim.21
  3.1 11.1 %all-to-all-start.1 = ((bf16[128,32,128]{2,0,1:T(8,128)(2,1)}), bf16[128,32,128]{2,0,1:T(8,128)(2,1)}, u32[]{:S(2)}, u32[]{:S(2)}) async-start(bf16[128,32,128]{2,0,1:T(8,128)(2,1)} %bitcast.10), calls=%async_computation.1 | async-start | bytes 2097152 | tf_op jit(solution)/shard_map/all_to_all | solution.py:170
  14.4 17.2 %all-to-all-done.1 = bf16[128,32,128]{2,0,1:T(8,128)(2,1)} async-done(((bf16[128,32,128]{2,0,1:T(8,128)(2,1)}), bf16[128,32,128]{2,0,1:T(8,128)(2,1)}, u32[]{:S(2)}, u32[]{:S(2)}) %all-to-all-start.1) | async-done | bytes 1048608 | tf_op jit(solution)/shard_map/all_to_all | solution.py:170
  31.6 1.3 broadcast_in_dim.18
  32.9 4.6 %all-to-all-start = ((bf16[128,32,128]{2,0,1:T(8,128)(2,1)}), bf16[128,32,128]{2,0,1:T(8,128)(2,1)}, u32[]{:S(2)}, u32[]{:S(2)}) async-start(bf16[128,32,128]{2,0,1:T(8,128)(2,1)} %bitcast.7), calls=%async_computation | async-start | bytes 2097152 | tf_op jit(solution)/shard_map/all_to_all | solution.py:169
  37.5 17.3 %all-to-all-done = bf16[128,32,128]{2,0,1:T(8,128)(2,1)} async-done(((bf16[128,32,128]{2,0,1:T(8,128)(2,1)}), bf16[128,32,128]{2,0,1:T(8,128)(2,1)}, u32[]{:S(2)}, u32[]{:S(2)}) %all-to-all-start) | async-done | bytes 1048608 | tf_op jit(solution)/shard_map/all_to_all | solution.py:169
  54.9 11.9 %while.28 = (s32[]{:T(128)}, f32[1024]{0:T(1024)S(1)}, f32[1024]{0:T(1024)S(1)}, f32[1024,128]{1,0:T(8,128)S(1)}, s32[]{:T(128)}, /*index=5*/s32[9,2]{0,1:T(2,12...) while((s32[]{:T(128)}, f32[1024]{0:T(1024)S(1)}, ...), condition=%wide.region_3.0_spmd, body=%wide.region_0.0_spmd.sunk | while | flops 135922704 | bytes 4110647 | solution.py:55
  64.9 1.3 fusion.67
  67.1 60.5 %all_to_all.90 = f32[16,65,128]{2,1,0:T(8,128)S(1)} all-to-all(f32[16,65,128]{2,1,0:T(8,128)S(1)} %maximum_maximum_fusion), channel_id=1, replica_groups=mesh['grp'=16,'seq'=32] {'grp'}, dimensions={0} | all-to-all | bytes 1064960 | tf_op jit(solution)/shard_map/all_to_all | solution.py:134
  128.9 8.3 %all-to-all-start.3 = ((f32[16,65,128]{2,1,0:T(8,128)}), f32[16,65,128]{2,1,0:T(8,128)S(1)}, u32[]{:S(2)}, u32[]{:S(2)}) async-start(f32[16,65,128]{2,1,0:T(8,128)} %broadcast_in_dim.23), calls=%async_computation.3 | async-start | bytes 1179648 | tf_op jit(solution)/shard_map/all_to_all | solution.py:145
  137.2 24.7 %all-to-all-done.3 = f32[16,65,128]{2,1,0:T(8,128)S(1)} async-done(((f32[16,65,128]{2,1,0:T(8,128)}), f32[16,65,128]{2,1,0:T(8,128)S(1)}, u32[]{:S(2)}, u32[]{:S(2)}) %all-to-all-start.3) | async-done | bytes 532512 | tf_op jit(solution)/shard_map/all_to_all | solution.py:145
  162.5 1.5 broadcast.31.clone
  164.8 19.7 %while.29 = (s32[]{:T(128)}, f32[1024,128]{1,0:T(8,128)}, f32[4096,128]{1,0:T(8,128)S(1)}, f32[4096,128]{1,0:T(8,128)}, s32[]{:T(128)}, /*index=5*/s32[9,2]{0,1:...) while((s32[]{:T(128)}, f32[1024,128]{1,0:T(8,128)}, ...), condition=%wide.region_9.0_spmd, body=%wide.region_8.0_spmd.sunk | while | flops 337444864 | bytes 7221607 | solution.py:130
  170.3 2.0 fusion.82
  172.3 2.0 fusion.80
  179.8 2.0 fusion.82
  181.8 2.0 fusion.80
  184.6 83.7 %all_to_all.91 = bf16[32,128,128]{2,1,0:T(8,128)(2,1)} all-to-all(bf16[32,128,128]{2,1,0:T(8,128)(2,1)S(1)} %bitcast.68), channel_id=1, replica_groups=mesh['grp'=16,'seq'=32] {'seq'}, dimensions={0} | all-to-all | bytes 2097152 | tf_op jit(solution)/shard_map/all_to_all | solution.py:219
  268.4 20.3 %all-to-all-start.4 = ((f32[16,64,128]{2,1,0:T(8,128)}), f32[16,64,128]{2,1,0:T(8,128)S(1)}, u32[]{:S(2)}, u32[]{:S(2)}) async-start(f32[16,64,128]{2,1,0:T(8,128)} %bitcast.21), calls=%async_computation.4 | async-start | bytes 1048576 | tf_op jit(solution)/shard_map/all_to_all | solution.py:134
  289.7 21.6 %all-to-all-done.4 = f32[16,64,128]{2,1,0:T(8,128)S(1)} async-done(((f32[16,64,128]{2,1,0:T(8,128)}), f32[16,64,128]{2,1,0:T(8,128)S(1)}, u32[]{:S(2)}, u32[]{:S(2)}) %all-to-all-start.4) | async-done | bytes 524320 | tf_op jit(solution)/shard_map/all_to_all | solution.py:134
  311.4 10.7 %all-to-all-start.7 = ((bf16[32,128,128]{2,1,0:T(8,128)(2,1)}), bf16[32,128,128]{2,1,0:T(8,128)(2,1)S(1)}, u32[]{:S(2)}, u32[]{:S(2)}) async-start(bf16[32,128,128]{2,1,0:T(8,128)(2,1)} %bitcast.67), calls=%async_computation.7 | async-start | bytes 2097152 | tf_op jit(solution)/shard_map/all_to_all | solution.py:222
  322.2 17.2 %all-to-all-done.7 = bf16[32,128,128]{2,1,0:T(8,128)(2,1)S(1)} async-done(((bf16[32,128,128]{2,1,0:T(8,128)(2,1)}), bf16[32,128,128]{2,1,0:T(8,128)(2,1)S(1)}, u32[]{:S(2)}, u32[]{:S(2)}) %all-to-all-start.7) | async-done | bytes 1048608 | tf_op jit(solution)/shard_map/all_to_all | solution.py:222
  340.2 6.1 %all-to-all-start.5 = ((bf16[16,64,128]{2,1,0:T(8,128)(2,1)}), bf16[16,64,128]{2,1,0:T(8,128)(2,1)S(1)}, u32[]{:S(2)}, u32[]{:S(2)}) async-start(bf16[16,64,128]{2,1,0:T(8,128)(2,1)} %broadcast_in_dim.24), calls=%async_computation.5 | async-start | bytes 524288 | tf_op jit(solution)/shard_map/all_to_all | solution.py:145
  349.3 10.9 %all-to-all-done.5 = bf16[16,64,128]{2,1,0:T(8,128)(2,1)S(1)} async-done(((bf16[16,64,128]{2,1,0:T(8,128)(2,1)}), bf16[16,64,128]{2,1,0:T(8,128)(2,1)S(1)}, u32[]{:S(2)}, u32[]{:S(2)}) %all-to-all-start.5) | async-done | bytes 262176 | tf_op jit(solution)/shard_map/all_to_all | solution.py:145
  (77 shorter events, 22.9 us)
Async XLA Ops:
  0.6 1.0 copy-start
  1.8 12.4 %copy-start.6 = (bf16[128,2048]{1,0:T(8,128)(2,1)S(1)}, bf16[128,2048]{1,0:T(8,128)(2,1)}, u32[]{:S(2)}) copy-start(bf16[128,2048]{1,0:T(8,128)(2,1)} %param.11) | copy-start | bytes 1572868
  3.1 28.5 %all-to-all-start.1 = ((bf16[128,32,128]{2,0,1:T(8,128)(2,1)}), bf16[128,32,128]{2,0,1:T(8,128)(2,1)}, u32[]{:S(2)}, u32[]{:S(2)}) async-start(bf16[128,32,128]{2,0,1:T(8,128)(2,1)} %bitcast.10), calls=%async_computation.1 | async-start | bytes 2097152 | tf_op jit(solution)/shard_map/all_to_all | solution.py:170
  14.4 40.5 %copy-start.1 = (bf16[1,1024,128]{2,1,0:T(8,128)(2,1)S(1)}, bf16[1,1024,128]{2,1,0:T(8,128)(2,1)}, u32[]{:S(2)}) copy-start(bf16[1,1024,128]{2,1,0:T(8,128)(2,1)} %param.10) | copy-start | bytes 786436
  14.4 40.5 %copy-start.7 = (s32[1,1,9,2]{2,3,1,0:T(2,128)S(1)}, s32[1,1,9,2]{2,3,1,0:T(2,128)}, u32[]{:S(2)}) copy-start(s32[1,1,9,2]{2,3,1,0:T(2,128)} %param.14) | copy-start | bytes 220
  32.9 22.0 %all-to-all-start = ((bf16[128,32,128]{2,0,1:T(8,128)(2,1)}), bf16[128,32,128]{2,0,1:T(8,128)(2,1)}, u32[]{:S(2)}, u32[]{:S(2)}) async-start(bf16[128,32,128]{2,0,1:T(8,128)(2,1)} %bitcast.7), calls=%async_computation | async-start | bytes 2097152 | tf_op jit(solution)/shard_map/all_to_all | solution.py:169
  67.1 95.0 %copy-start.3 = (bf16[1,1024,128]{2,1,0:T(8,128)(2,1)S(1)}, bf16[1,1024,128]{2,1,0:T(8,128)(2,1)}, u32[]{:S(2)}) copy-start(bf16[1,1024,128]{2,1,0:T(8,128)(2,1)} %param.13) | copy-start | bytes 786436
  128.9 33.0 %all-to-all-start.3 = ((f32[16,65,128]{2,1,0:T(8,128)}), f32[16,65,128]{2,1,0:T(8,128)S(1)}, u32[]{:S(2)}, u32[]{:S(2)}) async-start(f32[16,65,128]{2,1,0:T(8,128)} %broadcast_in_dim.23), calls=%async_computation.3 | async-start | bytes 1179648 | tf_op jit(solution)/shard_map/all_to_all | solution.py:145
  162.1 1.9 copy-start.5
  184.6 104.0 %copy-start.2 = (f32[4096,128]{1,0:T(8,128)S(1)}, f32[4096,128]{1,0:T(8,128)}, u32[]{:S(2)}) copy-start(f32[4096,128]{1,0:T(8,128)} %get-tuple-element.124) | copy-start | bytes 6291460
  268.4 43.0 %all-to-all-start.4 = ((f32[16,64,128]{2,1,0:T(8,128)}), f32[16,64,128]{2,1,0:T(8,128)S(1)}, u32[]{:S(2)}, u32[]{:S(2)}) async-start(f32[16,64,128]{2,1,0:T(8,128)} %bitcast.21), calls=%async_computation.4 | async-start | bytes 1048576 | tf_op jit(solution)/shard_map/all_to_all | solution.py:134
  289.7 56.6 %copy-start.4 = (bf16[32,128,128]{2,1,0:T(8,128)(2,1)S(1)}, bf16[32,128,128]{2,1,0:T(8,128)(2,1)}, u32[]{:S(2)}) copy-start(bf16[32,128,128]{2,1,0:T(8,128)(2,1)} %all_to_all.91) | copy-start | bytes 3145732
  311.4 28.0 %all-to-all-start.7 = ((bf16[32,128,128]{2,1,0:T(8,128)(2,1)}), bf16[32,128,128]{2,1,0:T(8,128)(2,1)S(1)}, u32[]{:S(2)}, u32[]{:S(2)}) async-start(bf16[32,128,128]{2,1,0:T(8,128)(2,1)} %bitcast.67), calls=%async_computation.7 | async-start | bytes 2097152 | tf_op jit(solution)/shard_map/all_to_all | solution.py:222
  340.2 20.0 %all-to-all-start.5 = ((bf16[16,64,128]{2,1,0:T(8,128)(2,1)}), bf16[16,64,128]{2,1,0:T(8,128)(2,1)S(1)}, u32[]{:S(2)}, u32[]{:S(2)}) async-start(bf16[16,64,128]{2,1,0:T(8,128)(2,1)} %broadcast_in_dim.24), calls=%async_computation.5 | async-start | bytes 524288 | tf_op jit(solution)/shard_map/all_to_all | solution.py:145

commit v2 on v1

--- a/solution.py
+++ b/solution.py
@@ -36,6 +36,7 @@
         old_total = lax.dynamic_slice_in_dim(run_total, query_start, QBLK, 0)
         old_accum = lax.dynamic_slice_in_dim(run_accum, query_start, QBLK, 0)
         new_max = jnp.maximum(old_max, jnp.max(scores, axis=1))
+        new_max = new_max.astype(jnp.bfloat16).astype(jnp.float32)
         weights = jnp.exp(scores - new_max[:, None])
         shrink = jnp.exp(old_max - new_max)
         new_total = old_total * shrink + jnp.sum(weights, axis=1)
@@ -179,28 +180,49 @@
         tile_counts[0, 0],
         softmax_scale,
     )
-    stats = jnp.concatenate(
-        [part_max.reshape(groups, 1, chunk_rows), part_total.reshape(groups, 1, chunk_rows)],
-        axis=2,
-    )
-    packed = jnp.concatenate([part_accum.reshape(groups, chunk_rows, head_width), stats], axis=1)
-    arrived = scatter_rows(packed.reshape(groups * (chunk_rows + 1), head_width), groups)
-    arrived = arrived.reshape(groups, chunk_rows + 1, head_width)
+    total_hi = part_total.astype(jnp.bfloat16)
+    total_lo = (part_total - total_hi.astype(jnp.float32)).astype(jnp.bfloat16)
+    stats = jnp.stack(
+        [
+            jnp.concatenate(
+                [part_max.astype(jnp.bfloat16).reshape(groups, chunk_rows), total_hi.reshape(groups, chunk_rows)],
+                axis=1,
+            ),
+            jnp.concatenate(
+                [total_lo.reshape(groups, chunk_rows), jnp.zeros((groups, chunk_rows), jnp.bfloat16)],
+                axis=1,
+            ),
+        ],
+        axis=1,
+    )
+    packed = jnp.concatenate(
+        [part_accum.astype(jnp.bfloat16).reshape(groups, chunk_rows, head_width), stats], axis=1
+    )
+    arrived = scatter_rows(packed.reshape(groups * (chunk_rows + 2), head_width), groups)
+    arrived = arrived.reshape(groups, chunk_rows + 2, head_width).astype(jnp.float32)
     got_accum = arrived[:, :chunk_rows, :]
     got_max = arrived[:, chunk_rows, :chunk_rows]
-    got_total = arrived[:, chunk_rows, chunk_rows:]
+    got_total = arrived[:, chunk_rows, chunk_rows:] + arrived[:, chunk_rows + 1, :chunk_rows]
     top = jnp.max(got_max, axis=0)
     shrink = jnp.exp(got_max - top[None, :])
     chunk_total = jnp.sum(got_total * shrink, axis=0)
     chunk_accum = jnp.sum(got_accum * shrink[:, :, None], axis=0)
     chunk_out = (chunk_accum / chunk_total[:, None]).astype(jnp.bfloat16)
-    chunk_log = top + jnp.log(chunk_total)
-    log_row = jnp.concatenate([chunk_log, jnp.zeros((chunk_rows,), jnp.float32)])
-    back = broadcast_rows(
-        jnp.concatenate([chunk_out.astype(jnp.float32), log_row[None, :]], axis=0), groups
-    ).reshape(groups, chunk_rows + 1, head_width)
-    attended = back[:, :chunk_rows, :].reshape(1, query_rows, head_width).astype(jnp.bfloat16)
-    log_total = back[:, chunk_rows, :chunk_rows].reshape(1, query_rows)
+    chunk_hi = chunk_total.astype(jnp.bfloat16)
+    chunk_lo = (chunk_total - chunk_hi.astype(jnp.float32)).astype(jnp.bfloat16)
+    chunk_stats = jnp.stack(
+        [
+            jnp.concatenate([top.astype(jnp.bfloat16), chunk_hi]),
+            jnp.concatenate([chunk_lo, jnp.zeros((chunk_rows,), jnp.bfloat16)]),
+        ]
+    )
+    back = broadcast_rows(jnp.concatenate([chunk_out, chunk_stats], axis=0), groups)
+    back = back.reshape(groups, chunk_rows + 2, head_width)
+    attended = back[:, :chunk_rows, :].reshape(1, query_rows, head_width)
+    back_stats = back[:, chunk_rows:, :].astype(jnp.float32)
+    row_top = back_stats[:, 0, :chunk_rows].reshape(1, query_rows)
+    row_total = (back_stats[:, 0, chunk_rows:] + back_stats[:, 1, :chunk_rows]).reshape(1, query_rows)
+    log_total = row_top + jnp.log(row_total)
     deltas = jnp.sum(attended.astype(jnp.float32) * grad_output.astype(jnp.float32), axis=2)
     query_grad, key_grad, value_grad = backward_item(
         queries[0],
@@ -239,8 +261,8 @@
         .astype(jnp.bfloat16)
         .reshape(scene_here, -1)
     )
-    query_parts = scatter_rows(query_grad, groups)
-    query_chunk = jnp.sum(query_parts, axis=0).astype(jnp.bfloat16)
+    query_parts = scatter_rows(query_grad.astype(jnp.bfloat16), groups)
+    query_chunk = jnp.sum(query_parts.astype(jnp.float32), axis=0).astype(jnp.bfloat16)
     grad_queries = broadcast_rows(query_chunk, groups).reshape(1, query_rows, head_width)
     return (attended, grad_queries, grad_keys, grad_values)
 

time: 367 us -> 315 us (0.86)
  blocking collectives: 144 us -> 49.1 us
  starting transfers between devices: 61.2 us -> 91.7 us
  matrix products: 18.6 us -> 23.1 us
  loops' own time: 9.24 us -> 13.3 us
    all_to_all x1 -> x0, blocking collectives: 83.7 us -> none  [per_device(): lax.all_to_all(key_stack.reshape(group_keys, -1), 'seq', split_axis=0, co...]
    all_to_all x1, starting transfers between devices: 20.3 us -> 48.3 us  [scatter_rows(): lax.all_to_all(rows.reshape(parts, rows.shape[0] // parts, rows.shape[1])...]
    all_to_all x0 -> x1, waiting for transfers between devices: none -> 17.2 us  [per_device(): lax.all_to_all(key_stack.reshape(group_keys, -1), 'seq', split_axis=0, co...]
    all_to_all x1, blocking collectives: 60.5 us -> 49.1 us  [scatter_rows(): lax.all_to_all(rows.reshape(parts, rows.shape[0] // parts, rows.shape[1])...]
    all_to_all x1, waiting for transfers between devices: 21.6 us -> 11.7 us  [scatter_rows(): lax.all_to_all(rows.reshape(parts, rows.shape[0] // parts, rows.shape[1])...]
    all_to_all x2, waiting for transfers between devices: 35.7 us -> 27.6 us  [broadcast_rows(): lax.all_to_all(spread, 'grp', split_axis=0, concat_axis=0, tiled=True)]
    all_to_all x1, starting transfers between devices: 11.1 us -> 3.97 us  [per_device(): lax.all_to_all(value_wide, 'seq', split_axis=1, concat_axis=0, tiled=True)]
    all_to_all x1, starting transfers between devices: 4.63 us -> 10.5 us  [per_device(): lax.all_to_all(key_wide, 'seq', split_axis=1, concat_axis=0, tiled=True)]
  transfers between devices with their start and end apart: 6 -> 7, of which waited for: 6 -> 7; matrix products, arithmetic and copies ran while one was open for 1% -> 2% of each run, Pallas kernels for 0% -> 0%
where the time goes in v2:
time: 315 us; the launch traced here: 309 us
  waiting for transfers between devices  107 us (34%)
  starting transfers between devices  91.7 us (29%)
  blocking collectives  49.1 us (16%)
  matrix products  23.1 us (7%)
  local copies, waits for them, and re-layouts  16.9 us (5%)
  loops' own time  13.3 us (4%)
  other arithmetic  6.88 us (2%)
    all_to_all x1, blocking collectives, scatter_rows(): lax.all_to_all(rows.reshape(parts, rows.shape[0] // parts, rows.shape[1])...  49.1 us
    all_to_all x1, starting transfers between devices, scatter_rows(): lax.all_to_all(rows.reshape(parts, rows.shape[0] // parts, rows.shape[1])...  48.3 us
    all_to_all x2, waiting for transfers between devices, broadcast_rows(): lax.all_to_all(spread, 'grp', split_axis=0, concat_axis=0, tiled=True)  27.6 us
    all_to_all x1, waiting for transfers between devices, per_device(): lax.all_to_all(value_wide, 'seq', split_axis=1, concat_axis=0, tiled=True)  17.3 us
    all_to_all x1, waiting for transfers between devices, per_device(): lax.all_to_all(key_stack.reshape(group_keys, -1), 'seq', split_axis=0, co...  17.2 us
    all_to_all x1, waiting for transfers between devices, per_device(): lax.all_to_all(key_wide, 'seq', split_axis=1, concat_axis=0, tiled=True)  17.1 us
    all_to_all x1, waiting for transfers between devices, per_device(): lax.all_to_all(value_stack.reshape(group_keys, -1), 'seq', split_axis=0,...  16.1 us
    all_to_all x1, starting transfers between devices, per_device(): lax.all_to_all(value_stack.reshape(group_keys, -1), 'seq', split_axis=0,...  14 us
  transfers between devices with their start and end apart: 7, of which 7 were waited for; matrix products, arithmetic and copies ran while one was open for 2% of the time, Pallas kernels for 0%

profile of v2, /device:TPU:1, one launch (start us, length us, event | category | flops | bytes accessed | tf_op | source)
XLA Modules:
  0.0 309.0 jit_solution(10869238558518240139)
XLA Ops:
  3.1 10.5 %all-to-all-start = ((bf16[128,32,128]{2,0,1:T(8,128)(2,1)}), bf16[128,32,128]{2,0,1:T(8,128)(2,1)S(1)}, u32[]{:S(2)}, u32[]{:S(2)}) async-start(bf16[128,32,128]{2,0,1:T(8,128)(2,1)} %bitcast.7), calls=%async_computation | async-start | bytes 2097152 | tf_op jit(solution)/shard_map/all_to_all | solution.py:170
  13.7 17.1 %all-to-all-done = bf16[128,32,128]{2,0,1:T(8,128)(2,1)S(1)} async-done(((bf16[128,32,128]{2,0,1:T(8,128)(2,1)}), bf16[128,32,128]{2,0,1:T(8,128)(2,1)S(1)}, u32[]{:S(2)}, u32[]{:S(2)}) %all-to-all-start) | async-done | bytes 1048608 | tf_op jit(solution)/shard_map/all_to_all | solution.py:170
  32.1 4.0 %all-to-all-start.1 = ((bf16[128,32,128]{2,0,1:T(8,128)(2,1)}), bf16[128,32,128]{2,0,1:T(8,128)(2,1)S(1)}, u32[]{:S(2)}, u32[]{:S(2)}) async-start(bf16[128,32,128]{2,0,1:T(8,128)(2,1)} %bitcast.76), calls=%async_computation.1 | async-start | bytes 2097152 | tf_op jit(solution)/shard_map/all_to_all | solution.py:171
  36.1 17.3 %all-to-all-done.1 = bf16[128,32,128]{2,0,1:T(8,128)(2,1)S(1)} async-done(((bf16[128,32,128]{2,0,1:T(8,128)(2,1)}), bf16[128,32,128]{2,0,1:T(8,128)(2,1)S(1)}, u32[]{:S(2)}, u32[]{:S(2)}) %all-to-all-start.1) | async-done | bytes 1048608 | tf_op jit(solution)/shard_map/all_to_all | solution.py:171
  54.4 15.3 %while.28 = (s32[]{:T(128)}, f32[1024]{0:T(1024)S(1)}, f32[1024]{0:T(1024)S(1)}, f32[1024,128]{1,0:T(8,128)S(1)}, s32[]{:T(128)}, /*index=5*/s32[9,2]{0,1:T(2,12...) while((s32[]{:T(128)}, f32[1024]{0:T(1024)S(1)}, ...), condition=%wide.region_3.0_spmd, body=%wide.region_0.0_spmd.sunk | while | flops 135924240 | bytes 4093251 | solution.py:56
  70.2 49.1 %all_to_all.90 = bf16[16,66,128]{2,1,0:T(8,128)(2,1)S(1)} all-to-all(bf16[16,66,128]{2,1,0:T(8,128)(2,1)S(1)} %pad_maximum_fusion), channel_id=1, replica_groups=mesh['grp'=16,'seq'=32] {'grp'}, dimensions={0} | all-to-all | bytes 540672 | tf_op jit(solution)/shard_map/all_to_all | solution.py:135
  120.7 4.6 %all-to-all-start.3 = ((bf16[16,66,128]{2,1,0:T(8,128)(2,1)}), bf16[16,66,128]{2,1,0:T(8,128)(2,1)S(1)}, u32[]{:S(2)}, u32[]{:S(2)}) async-start(bf16[16,66,128]{2,1,0:T(8,128)(2,1)} %broadcast_in_dim.18), calls=%async_computation.3 | async-start | bytes 589824 | tf_op jit(solution)/shard_map/all_to_all | solution.py:146
  125.3 17.9 %all-to-all-done.3 = bf16[16,66,128]{2,1,0:T(8,128)(2,1)S(1)} async-done(((bf16[16,66,128]{2,1,0:T(8,128)(2,1)}), bf16[16,66,128]{2,1,0:T(8,128)(2,1)S(1)}, u32[]{:S(2)}, u32[]{:S(2)}) %all-to-all-start.3) | async-done | bytes 270368 | tf_op jit(solution)/shard_map/all_to_all | solution.py:146
  144.2 1.5 broadcast.34
  145.7 27.3 %while.29 = (s32[]{:T(128)}, f32[1024,128]{1,0:T(8,128)S(1)}, f32[4096,128]{1,0:T(8,128)}, f32[4096,128]{1,0:T(8,128)S(1)}, s32[]{:T(128)}, /*index=5*/s32[9,2]{...) while((s32[]{:T(128)}, f32[1024,128]{1,0:T(8,128)S(1)}, ...), condition=%wide.region_9.0_spmd, body=%wide.region_8.0_spmd.sunk | while | flops 337444864 | bytes 8270219 | solution.py:131
  149.7 1.3 fusion.81
  152.6 2.0 fusion.83
  158.6 1.3 fusion.81
  161.5 2.0 fusion.83
  170.3 2.0 fusion.83
  173.7 48.3 %all-to-all-start.4 = ((bf16[16,64,128]{2,1,0:T(8,128)(2,1)}), bf16[16,64,128]{2,1,0:T(8,128)(2,1)S(1)}, u32[]{:S(2)}, u32[]{:S(2)}) async-start(bf16[16,64,128]{2,1,0:T(8,128)(2,1)} %bitcast.24), calls=%async_computation.4 | async-start | bytes 524288 | tf_op jit(solution)/shard_map/all_to_all | solution.py:135
  223.1 11.7 %all-to-all-done.4 = bf16[16,64,128]{2,1,0:T(8,128)(2,1)S(1)} async-done(((bf16[16,64,128]{2,1,0:T(8,128)(2,1)}), bf16[16,64,128]{2,1,0:T(8,128)(2,1)S(1)}, u32[]{:S(2)}, u32[]{:S(2)}) %all-to-all-start.4) | async-done | bytes 262176 | tf_op jit(solution)/shard_map/all_to_all | solution.py:135
  234.7 14.0 %all-to-all-start.7 = ((bf16[32,128,128]{2,1,0:T(8,128)(2,1)}), bf16[32,128,128]{2,1,0:T(8,128)(2,1)}, u32[]{:S(2)}, u32[]{:S(2)}) async-start(bf16[32,128,128]{2,1,0:T(8,128)(2,1)} %bitcast.74), calls=%async_computation.7 | async-start | bytes 2097152 | tf_op jit(solution)/shard_map/all_to_all | solution.py:244
  249.9 16.1 %all-to-all-done.7 = bf16[32,128,128]{2,1,0:T(8,128)(2,1)} async-done(((bf16[32,128,128]{2,1,0:T(8,128)(2,1)}), bf16[32,128,128]{2,1,0:T(8,128)(2,1)}, u32[]{:S(2)}, u32[]{:S(2)}) %all-to-all-start.7) | async-done | bytes 1048608 | tf_op jit(solution)/shard_map/all_to_all | solution.py:244
  266.0 4.0 %all-to-all-start.6 = ((bf16[32,128,128]{2,1,0:T(8,128)(2,1)}), bf16[32,128,128]{2,1,0:T(8,128)(2,1)S(1)}, u32[]{:S(2)}, u32[]{:S(2)}) async-start(bf16[32,128,128]{2,1,0:T(8,128)(2,1)} %bitcast.75), calls=%async_computation.6 | async-start | bytes 2097152 | tf_op jit(solution)/shard_map/all_to_all | solution.py:241
  270.0 17.2 %all-to-all-done.6 = bf16[32,128,128]{2,1,0:T(8,128)(2,1)S(1)} async-done(((bf16[32,128,128]{2,1,0:T(8,128)(2,1)}), bf16[32,128,128]{2,1,0:T(8,128)(2,1)S(1)}, u32[]{:S(2)}, u32[]{:S(2)}) %all-to-all-start.6) | async-done | bytes 1048608 | tf_op jit(solution)/shard_map/all_to_all | solution.py:241
  288.0 6.4 %all-to-all-start.5 = ((bf16[16,64,128]{2,1,0:T(8,128)(2,1)}), bf16[16,64,128]{2,1,0:T(8,128)(2,1)S(1)}, u32[]{:S(2)}, u32[]{:S(2)}) async-start(bf16[16,64,128]{2,1,0:T(8,128)(2,1)} %broadcast_in_dim.21), calls=%async_computation.5 | async-start | bytes 524288 | tf_op jit(solution)/shard_map/all_to_all | solution.py:146
  294.4 1.4 bitcast_reduce_fusion
  298.5 9.7 %all-to-all-done.5 = bf16[16,64,128]{2,1,0:T(8,128)(2,1)S(1)} async-done(((bf16[16,64,128]{2,1,0:T(8,128)(2,1)}), bf16[16,64,128]{2,1,0:T(8,128)(2,1)S(1)}, u32[]{:S(2)}, u32[]{:S(2)}) %all-to-all-start.5) | async-done | bytes 262176 | tf_op jit(solution)/shard_map/all_to_all | solution.py:146
  (112 shorter events, 35.5 us)
Async XLA Ops:
  0.6 1.0 copy-start
  1.8 11.8 %copy-start.8 = (bf16[128,2048]{1,0:T(8,128)(2,1)S(1)}, bf16[128,2048]{1,0:T(8,128)(2,1)}, u32[]{:S(2)}) copy-start(bf16[128,2048]{1,0:T(8,128)(2,1)} %param.12) | copy-start | bytes 1572868
  3.1 27.8 %all-to-all-start = ((bf16[128,32,128]{2,0,1:T(8,128)(2,1)}), bf16[128,32,128]{2,0,1:T(8,128)(2,1)S(1)}, u32[]{:S(2)}, u32[]{:S(2)}) async-start(bf16[128,32,128]{2,0,1:T(8,128)(2,1)} %bitcast.7), calls=%async_computation | async-start | bytes 2097152 | tf_op jit(solution)/shard_map/all_to_all | solution.py:170
  13.7 40.7 %copy-start.1 = (bf16[1,1024,128]{2,1,0:T(8,128)(2,1)S(1)}, bf16[1,1024,128]{2,1,0:T(8,128)(2,1)}, u32[]{:S(2)}) copy-start(bf16[1,1024,128]{2,1,0:T(8,128)(2,1)} %param.10) | copy-start | bytes 786436
  13.7 40.7 %copy-start.9 = (s32[1,1,9,2]{2,3,1,0:T(2,128)S(1)}, s32[1,1,9,2]{2,3,1,0:T(2,128)}, u32[]{:S(2)}) copy-start(s32[1,1,9,2]{2,3,1,0:T(2,128)} %param.14) | copy-start | bytes 220
  32.1 21.3 %all-to-all-start.1 = ((bf16[128,32,128]{2,0,1:T(8,128)(2,1)}), bf16[128,32,128]{2,0,1:T(8,128)(2,1)S(1)}, u32[]{:S(2)}, u32[]{:S(2)}) async-start(bf16[128,32,128]{2,0,1:T(8,128)(2,1)} %bitcast.76), calls=%async_computation.1 | async-start | bytes 2097152 | tf_op jit(solution)/shard_map/all_to_all | solution.py:171
  53.4 1.0 copy-start.6
  69.7 51.0 %copy-start.5 = (bf16[4096,128]{1,0:T(8,128)(2,1)}, bf16[4096,128]{1,0:T(8,128)(2,1)S(1)}, u32[]{:S(2)}) copy-start(bf16[4096,128]{1,0:T(8,128)(2,1)S(1)} %get-tuple-element.442) | copy-start | bytes 3145732
  70.1 73.3 %copy-start.3 = (bf16[1,1024,128]{2,1,0:T(8,128)(2,1)S(1)}, bf16[1,1024,128]{2,1,0:T(8,128)(2,1)}, u32[]{:S(2)}) copy-start(bf16[1,1024,128]{2,1,0:T(8,128)(2,1)} %param.13) | copy-start | bytes 786436
  120.7 22.5 %all-to-all-start.3 = ((bf16[16,66,128]{2,1,0:T(8,128)(2,1)}), bf16[16,66,128]{2,1,0:T(8,128)(2,1)S(1)}, u32[]{:S(2)}, u32[]{:S(2)}) async-start(bf16[16,66,128]{2,1,0:T(8,128)(2,1)} %broadcast_in_dim.18), calls=%async_computation.3 | async-start | bytes 589824 | tf_op jit(solution)/shard_map/all_to_all | solution.py:146
  143.4 0.7 copy-start.7
  148.4 3.8 %copy-start.4 = (bf16[1024,128]{1,0:T(8,128)(2,1)S(1)}, bf16[1024,128]{1,0:T(8,128)(2,1)}, u32[]{:S(2)}) copy-start(bf16[1024,128]{1,0:T(8,128)(2,1)} %get-tuple-element.423) | copy-start | bytes 786436 | tf_op jit(solution)/shard_map/while
  157.3 3.8 %copy-start.4 = (bf16[1024,128]{1,0:T(8,128)(2,1)S(1)}, bf16[1024,128]{1,0:T(8,128)(2,1)}, u32[]{:S(2)}) copy-start(bf16[1024,128]{1,0:T(8,128)(2,1)} %get-tuple-element.423) | copy-start | bytes 786436 | tf_op jit(solution)/shard_map/while
  166.2 3.8 %copy-start.4 = (bf16[1024,128]{1,0:T(8,128)(2,1)S(1)}, bf16[1024,128]{1,0:T(8,128)(2,1)}, u32[]{:S(2)}) copy-start(bf16[1024,128]{1,0:T(8,128)(2,1)} %get-tuple-element.423) | copy-start | bytes 786436 | tf_op jit(solution)/shard_map/while
  173.7 61.0 %all-to-all-start.4 = ((bf16[16,64,128]{2,1,0:T(8,128)(2,1)}), bf16[16,64,128]{2,1,0:T(8,128)(2,1)S(1)}, u32[]{:S(2)}, u32[]{:S(2)}) async-start(bf16[16,64,128]{2,1,0:T(8,128)(2,1)} %bitcast.24), calls=%async_computation.4 | async-start | bytes 524288 | tf_op jit(solution)/shard_map/all_to_all | solution.py:135
  223.1 25.7 %copy-start.2 = (f32[4096,128]{1,0:T(8,128)S(1)}, f32[4096,128]{1,0:T(8,128)}, u32[]{:S(2)}) copy-start(f32[4096,128]{1,0:T(8,128)} %get-tuple-element.123) | copy-start | bytes 6291460
  234.7 31.3 %all-to-all-start.7 = ((bf16[32,128,128]{2,1,0:T(8,128)(2,1)}), bf16[32,128,128]{2,1,0:T(8,128)(2,1)}, u32[]{:S(2)}, u32[]{:S(2)}) async-start(bf16[32,128,128]{2,1,0:T(8,128)(2,1)} %bitcast.74), calls=%async_computation.7 | async-start | bytes 2097152 | tf_op jit(solution)/shard_map/all_to_all | solution.py:244
  266.0 21.3 %all-to-all-start.6 = ((bf16[32,128,128]{2,1,0:T(8,128)(2,1)}), bf16[32,128,128]{2,1,0:T(8,128)(2,1)S(1)}, u32[]{:S(2)}, u32[]{:S(2)}) async-start(bf16[32,128,128]{2,1,0:T(8,128)(2,1)} %bitcast.75), calls=%async_computation.6 | async-start | bytes 2097152 | tf_op jit(solution)/shard_map/all_to_all | solution.py:241
  288.0 20.2 %all-to-all-start.5 = ((bf16[16,64,128]{2,1,0:T(8,128)(2,1)}), bf16[16,64,128]{2,1,0:T(8,128)(2,1)S(1)}, u32[]{:S(2)}, u32[]{:S(2)}) async-start(bf16[16,64,128]{2,1,0:T(8,128)(2,1)} %broadcast_in_dim.21), calls=%async_computation.5 | async-start | bytes 524288 | tf_op jit(solution)/shard_map/all_to_all | solution.py:146

commit v3 on v2

v3 whole, which is shorter than its diff:
```python
import jax
import jax.numpy as jnp
from jax import lax
from jax.experimental import pallas as pl
from jax.experimental.pallas import tpu as pltpu
from jax.sharding import PartitionSpec as P

QPARTS = 2
QBLK = 512
KBLK = 512


NEG_START = -1e30


LIST_SLOTS = 9


def tile_starts(list_ref, position):
    query_block = jnp.clip(list_ref[position, 0], 0, QPARTS - 1)
    key_block = jnp.clip(list_ref[position, 1], 0, 7)
    return (
        pl.multiple_of(query_block * QBLK, QBLK),
        pl.multiple_of(key_block * KBLK, KBLK),
    )


def forward_kernel(softmax_scale, list_ref, count_ref, q_ref, k_ref, v_ref, max_ref, total_ref, accum_ref):
    max_ref[...] = jnp.full(max_ref.shape, NEG_START, jnp.float32)
    total_ref[...] = jnp.zeros(total_ref.shape, jnp.float32)
    accum_ref[...] = jnp.zeros(accum_ref.shape, jnp.float32)
    live_tiles = jnp.clip(count_ref[0], 0, LIST_SLOTS)

    def visit(position, carry):
        query_start, key_start = tile_starts(list_ref, position)
        rows = pl.ds(query_start, QBLK)
        keys = pl.ds(key_start, KBLK)
        scores = (
            lax.dot_general(
                q_ref[rows, :], k_ref[keys, :], (((1,), (1,)), ((), ())),
                preferred_element_type=jnp.float32,
            )
            * softmax_scale
        )
        old_max = max_ref[rows, :]
        new_max = jnp.maximum(old_max, jnp.max(scores, axis=1, keepdims=True))
        new_max = new_max.astype(jnp.bfloat16).astype(jnp.float32)
        weights = jnp.exp(scores - new_max[:, :1])
        shrink = jnp.exp(old_max - new_max)
        total_ref[rows, :] = total_ref[rows, :] * shrink + jnp.sum(weights, axis=1, keepdims=True)
        accum_ref[rows, :] = accum_ref[rows, :] * shrink[:, :1] + jnp.dot(
            weights.astype(jnp.bfloat16), v_ref[keys, :], preferred_element_type=jnp.float32
        )
        max_ref[rows, :] = new_max
        return carry

    lax.fori_loop(0, live_tiles, visit, 0)


def forward_item(query_item, key_head, value_head, listing, live_tiles, softmax_scale):
    query_rows, head_width = query_item.shape
    smem = pl.BlockSpec(memory_space=pltpu.SMEM)
    vmem = pl.BlockSpec(memory_space=pltpu.VMEM)
    row_shape = jax.ShapeDtypeStruct((query_rows, head_width), jnp.float32)
    run_max, run_total, run_accum = pl.pallas_call(
        lambda *refs: forward_kernel(softmax_scale, *refs),
        out_shape=(row_shape, row_shape, row_shape),
        in_specs=[smem, smem, vmem, vmem, vmem],
        out_specs=(vmem, vmem, vmem),
    )(listing, live_tiles.reshape(1), query_item, key_head, value_head)
    return run_max[:, 0], run_total[:, 0], run_accum


def backward_kernel(
    softmax_scale, list_ref, count_ref, q_ref, k_ref, v_ref, do_ref, log_ref, delta_ref,
    dq_ref, dk_ref, dv_ref, dq_acc, dk_acc, dv_acc,
):
    dq_acc[...] = jnp.zeros(dq_acc.shape, jnp.float32)
    dk_acc[...] = jnp.zeros(dk_acc.shape, jnp.float32)
    dv_acc[...] = jnp.zeros(dv_acc.shape, jnp.float32)
    live_tiles = jnp.clip(count_ref[0], 0, LIST_SLOTS)

    def visit(position, carry):
        query_start, key_start = tile_starts(list_ref, position)
        rows = pl.ds(query_start, QBLK)
        keys = pl.ds(key_start, KBLK)
        query_block = q_ref[rows, :]
        grad_block = do_ref[rows, :]
        key_block = k_ref[keys, :]
        value_block = v_ref[keys, :]
        scores = (
            lax.dot_general(
                query_block, key_block, (((1,), (1,)), ((), ())),
                preferred_element_type=jnp.float32,
            )
            * softmax_scale
        )
        probs = jnp.exp(scores - log_ref[rows, :])
        probs_half = probs.astype(jnp.bfloat16)
        dv_acc[keys, :] += lax.dot_general(
            probs_half, grad_block, (((0,), (0,)), ((), ())), preferred_element_type=jnp.float32
        )
        prob_grad = lax.dot_general(
            grad_block, value_block, (((1,), (1,)), ((), ())), preferred_element_type=jnp.float32
        )
        score_grad = (probs * (prob_grad - delta_ref[rows, :])).astype(jnp.bfloat16)
        dq_acc[rows, :] += (
            jnp.dot(score_grad, key_block, preferred_element_type=jnp.float32) * softmax_scale
        )
        dk_acc[keys, :] += (
            lax.dot_general(
                score_grad, query_block, (((0,), (0,)), ((), ())),
                preferred_element_type=jnp.float32,
            )
            * softmax_scale
        )
        return carry

    lax.fori_loop(0, live_tiles, visit, 0)
    dq_ref[...] = dq_acc[...].astype(dq_ref.dtype)
    dk_ref[...] = dk_acc[...].astype(dk_ref.dtype)
    dv_ref[...] = dv_acc[...].astype(dv_ref.dtype)


def backward_item(
    query_item, key_head, value_head, grad_item, log_total, deltas, listing, live_tiles, softmax_scale,
):
    query_rows, head_width = query_item.shape
    key_rows = key_head.shape[0]
    smem = pl.BlockSpec(memory_space=pltpu.SMEM)
    vmem = pl.BlockSpec(memory_space=pltpu.VMEM)
    return pl.pallas_call(
        lambda *refs: backward_kernel(softmax_scale, *refs),
        out_shape=(
            jax.ShapeDtypeStruct((query_rows, head_width), jnp.bfloat16),
            jax.ShapeDtypeStruct((key_rows, head_width), jnp.bfloat16),
            jax.ShapeDtypeStruct((key_rows, head_width), jnp.bfloat16),
        ),
        in_specs=[smem, smem] + [vmem] * 6,
        out_specs=(vmem, vmem, vmem),
        scratch_shapes=[
            pltpu.VMEM((query_rows, head_width), jnp.float32),
            pltpu.VMEM((key_rows, head_width), jnp.float32),
            pltpu.VMEM((key_rows, head_width), jnp.float32),
        ],
    )(
        listing,
        live_tiles.reshape(1),
        query_item,
        key_head,
        value_head,
        grad_item,
        log_total.reshape(query_rows, 1),
        deltas.reshape(query_rows, 1),
    )


def scatter_rows(rows, parts):
    return lax.all_to_all(
        rows.reshape(parts, rows.shape[0] // parts, rows.shape[1]),
        "grp",
        split_axis=0,
        concat_axis=0,
        tiled=True,
    )


def broadcast_rows(chunk, parts):
    spread = jnp.broadcast_to(chunk[None], (parts,) + chunk.shape)
    gathered = lax.all_to_all(spread, "grp", split_axis=0, concat_axis=0, tiled=True)
    return gathered.reshape(parts * chunk.shape[0], chunk.shape[1])


def per_device(queries, scene_keys, scene_values, grad_output, tile_list, tile_counts):
    items_here = queries.shape[0]
    head_width = queries.shape[2]
    query_rows = queries.shape[1]
    scene_here = scene_keys.shape[0]
    heads_total = scene_keys.shape[1] // head_width
    seq_devices = lax.axis_size("seq")
    groups = lax.axis_size("grp")
    chunk_rows = query_rows // groups
    group_keys = scene_here * seq_devices
    copies = max(1, QPARTS // items_here)
    heads_here = max(1, items_here // QPARTS)
    softmax_scale = head_width ** (-0.5)
    key_wide = jnp.repeat(
        scene_keys.reshape(scene_here, heads_total, head_width), copies, axis=1
    ).reshape(scene_here, -1)
    value_wide = jnp.repeat(
        scene_values.reshape(scene_here, heads_total, head_width), copies, axis=1
    ).reshape(scene_here, -1)
    key_group, value_group = (
        lax.all_to_all(key_wide, "seq", split_axis=1, concat_axis=0, tiled=True),
        lax.all_to_all(value_wide, "seq", split_axis=1, concat_axis=0, tiled=True),
    )
    key_group = key_group.reshape(group_keys, heads_here, head_width)
    value_group = value_group.reshape(group_keys, heads_here, head_width)
    part_max, part_total, part_accum = forward_item(
        queries[0],
        key_group[:, 0, :],
        value_group[:, 0, :],
        tile_list[0, 0],
        tile_counts[0, 0],
        softmax_scale,
    )
    total_hi = part_total.astype(jnp.bfloat16)
    total_lo = (part_total - total_hi.astype(jnp.float32)).astype(jnp.bfloat16)
    stats = jnp.stack(
        [
            jnp.concatenate(
                [part_max.astype(jnp.bfloat16).reshape(groups, chunk_rows), total_hi.reshape(groups, chunk_rows)],
                axis=1,
            ),
            jnp.concatenate(
                [total_lo.reshape(groups, chunk_rows), jnp.zeros((groups, chunk_rows), jnp.bfloat16)],
                axis=1,
            ),
        ],
        axis=1,
    )
    packed = jnp.concatenate(
        [part_accum.astype(jnp.bfloat16).reshape(groups, chunk_rows, head_width), stats], axis=1
    )
    arrived = scatter_rows(packed.reshape(groups * (chunk_rows + 2), head_width), groups)
    arrived = arrived.reshape(groups, chunk_rows + 2, head_width).astype(jnp.float32)
    got_accum = arrived[:, :chunk_rows, :]
    got_max = arrived[:, chunk_rows, :chunk_rows]
    got_total = arrived[:, chunk_rows, chunk_rows:] + arrived[:, chunk_rows + 1, :chunk_rows]
    top = jnp.max(got_max, axis=0)
    shrink = jnp.exp(got_max - top[None, :])
    chunk_total = jnp.sum(got_total * shrink, axis=0)
    chunk_accum = jnp.sum(got_accum * shrink[:, :, None], axis=0)
    chunk_out = (chunk_accum / chunk_total[:, None]).astype(jnp.bfloat16)
    chunk_hi = chunk_total.astype(jnp.bfloat16)
    chunk_lo = (chunk_total - chunk_hi.astype(jnp.float32)).astype(jnp.bfloat16)
    chunk_stats = jnp.stack(
        [
            jnp.concatenate([top.astype(jnp.bfloat16), chunk_hi]),
            jnp.concatenate([chunk_lo, jnp.zeros((chunk_rows,), jnp.bfloat16)]),
        ]
    )
    back = broadcast_rows(jnp.concatenate([chunk_out, chunk_stats], axis=0), groups)
    back = back.reshape(groups, chunk_rows + 2, head_width)
    attended = back[:, :chunk_rows, :].reshape(1, query_rows, head_width)
    back_stats = back[:, chunk_rows:, :].astype(jnp.float32)
    row_top = back_stats[:, 0, :chunk_rows].reshape(1, query_rows)
    row_total = (back_stats[:, 0, chunk_rows:] + back_stats[:, 1, :chunk_rows]).reshape(1, query_rows)
    log_total = row_top + jnp.log(row_total)
    deltas = jnp.sum(attended.astype(jnp.float32) * grad_output.astype(jnp.float32), axis=2)
    query_grad, key_grad, value_grad = backward_item(
        queries[0],
        key_group[:, 0, :],
        value_group[:, 0, :],
        grad_output[0],
        log_total[0],
        deltas[0],
        tile_list[0, 0],
        tile_counts[0, 0],
        softmax_scale,
    )
    key_stack = key_grad[:, None, :]
    value_stack = value_grad[:, None, :]
    key_back, value_back = (
        lax.all_to_all(
            key_stack.reshape(group_keys, -1), "seq", split_axis=0, concat_axis=1, tiled=True
        ),
        lax.all_to_all(
            value_stack.reshape(group_keys, -1), "seq", split_axis=0, concat_axis=1, tiled=True
        ),
    )
    grad_keys = (
        jnp.sum(
            key_back.reshape(scene_here, heads_total, copies, head_width).astype(jnp.float32),
            axis=2,
        )
        .astype(jnp.bfloat16)
        .reshape(scene_here, -1)
    )
    grad_values = (
        jnp.sum(
            value_back.reshape(scene_here, heads_total, copies, head_width).astype(jnp.float32),
            axis=2,
        )
        .astype(jnp.bfloat16)
        .reshape(scene_here, -1)
    )
    query_parts = scatter_rows(query_grad, groups)
    query_chunk = jnp.sum(query_parts.astype(jnp.float32), axis=0).astype(jnp.bfloat16)
    grad_queries = broadcast_rows(query_chunk, groups).reshape(1, query_rows, head_width)
    return (attended, grad_queries, grad_keys, grad_values)


def solution(mesh):
    in_specs = (
        P("seq", None, None),
        P(("grp", "seq"), None),
        P(("grp", "seq"), None),
        P("seq", None, None),
        P("grp", "seq", None, None),
        P("grp", "seq"),
    )
    out_specs = (
        P("seq", None, None),
        P("seq", None, None),
        P(("grp", "seq"), None),
        P(("grp", "seq"), None),
    )
    return jax.shard_map(
        per_device, mesh=mesh, in_specs=in_specs, out_specs=out_specs, check_vma=False
    )
```

time: 315 us -> 230 us (0.73)
  starting transfers between devices: 91.7 us -> 23.7 us
  blocking collectives: 49.1 us -> 106 us
  waiting for transfers between devices: 107 us -> 60.6 us
  matrix products: 23.1 us -> 0 us
  Pallas kernels: 0 us -> 17.6 us
  loops' own time: 13.3 us -> 0 us
  other arithmetic: 6.88 us -> 2.53 us
    all_to_all x2 -> x0, starting transfers between devices: 52.2 us -> none  [the longest x1 48.3 us: scatter_rows(): lax.all_to_all(rows.reshape(parts, rows.shape[0] // parts, rows.shape[1])...]
    all_to_all x0 -> x2, blocking collectives: none -> 47.5 us  [the longest x1 27.8 us: per_device(): lax.all_to_all(key_stack.reshape(group_keys, -1), 'seq', split_axis=0, co...]
    all_to_all x2 -> x0, waiting for transfers between devices: 28.9 us -> none  [the longest x1 17.2 us: per_device(): lax.all_to_all(key_stack.reshape(group_keys, -1), 'seq', split_axis=0, co...]
    dot_general x21 -> x0, matrix products: 23.1 us -> none  [the longest x3 6 us: backward_visit_tile(): lax.dot_general(score_grad, query_block, (((0,), (0,)), ((), ())), prefer...]
    pallas_call x0 -> x2, Pallas kernels: none -> 17.6 us  [the longest x1 9.34 us: backward_item(): pl.pallas_call(lambda *refs: backward_kernel(softmax_scale, *refs), out_s...]
    all_to_all x2 -> x1, waiting for transfers between devices: 27.6 us -> 11 us  [broadcast_rows(): lax.all_to_all(spread, 'grp', split_axis=0, concat_axis=0, tiled=True)]
    another operation x2 -> x0, loops' own time: 13.3 us -> none  [the longest x1 6.68 us: backward_item(): return lax.fori_loop(0, live_tiles, backward_visit_tile, initial)]
    all_to_all x1, starting transfers between devices: 14 us -> 3.98 us  [per_device(): lax.all_to_all(value_stack.reshape(group_keys, -1), 'seq', split_axis=0,...]
  transfers between devices with their start and end apart: 7 -> 4, of which waited for: 7 -> 4; matrix products, arithmetic and copies ran while one was open for 2% -> 2% of each run, Pallas kernels for 0% -> 0%
where the time goes in v3:
time: 230 us; the launch traced here: 226 us
  blocking collectives  106 us (46%)
  waiting for transfers between devices  60.6 us (26%)
  starting transfers between devices  23.7 us (10%)
  Pallas kernels  17.6 us (8%)
  local copies, waits for them, and re-layouts  14.3 us (6%)
  other arithmetic  2.53 us (1%)
    all_to_all x2, blocking collectives, scatter_rows(): lax.all_to_all(rows.reshape(parts, rows.shape[0] // parts, rows.shape[1])...  58.1 us
    all_to_all x1, blocking collectives, per_device(): lax.all_to_all(key_stack.reshape(group_keys, -1), 'seq', split_axis=0, co...  27.8 us
    all_to_all x1, blocking collectives, broadcast_rows(): lax.all_to_all(spread, 'grp', split_axis=0, concat_axis=0, tiled=True)  19.7 us
    all_to_all x1, waiting for transfers between devices, per_device(): lax.all_to_all(value_stack.reshape(group_keys, -1), 'seq', split_axis=0,...  17.2 us
    all_to_all x1, waiting for transfers between devices, per_device(): lax.all_to_all(key_wide, 'seq', split_axis=1, concat_axis=0, tiled=True)  17.1 us
    all_to_all x1, waiting for transfers between devices, per_device(): lax.all_to_all(value_wide, 'seq', split_axis=1, concat_axis=0, tiled=True)  15.3 us
    all_to_all x1, waiting for transfers between devices, broadcast_rows(): lax.all_to_all(spread, 'grp', split_axis=0, concat_axis=0, tiled=True)  11 us
    all_to_all x1, starting transfers between devices, per_device(): lax.all_to_all(key_wide, 'seq', split_axis=1, concat_axis=0, tiled=True)  10.6 us
  transfers between devices with their start and end apart: 4, of which 4 were waited for; matrix products, arithmetic and copies ran while one was open for 2% of the time, Pallas kernels for 0%

profile of v3, /device:TPU:1, one launch (start us, length us, event | category | flops | bytes accessed | tf_op | source)
XLA Modules:
  0.0 225.8 jit_solution(799426812211406744)
XLA Ops:
  0.6 1.0 copy-done
  1.8 1.2 broadcast_in_dim.8
  3.0 10.6 %all-to-all-start = ((bf16[128,32,128]{2,0,1:T(8,128)(2,1)}), bf16[128,32,128]{2,0,1:T(8,128)(2,1)S(1)}, u32[]{:S(2)}, u32[]{:S(2)}) async-start(bf16[128,32,128]{2,0,1:T(8,128)(2,1)} %bitcast.3), calls=%async_computation | async-start | bytes 2097152 | tf_op jit(solution)/shard_map/all_to_all | solution.py:194
  13.8 17.1 %all-to-all-done = bf16[128,32,128]{2,0,1:T(8,128)(2,1)S(1)} async-done(((bf16[128,32,128]{2,0,1:T(8,128)(2,1)}), bf16[128,32,128]{2,0,1:T(8,128)(2,1)S(1)}, u32[]{:S(2)}, u32[]{:S(2)}) %all-to-all-start) | async-done | bytes 1048608 | tf_op jit(solution)/shard_map/all_to_all | solution.py:194
  30.9 1.3 broadcast_in_dim.9
  32.3 4.0 %all-to-all-start.1 = ((bf16[128,32,128]{2,0,1:T(8,128)(2,1)}), bf16[128,32,128]{2,0,1:T(8,128)(2,1)S(1)}, u32[]{:S(2)}, u32[]{:S(2)}) async-start(bf16[128,32,128]{2,0,1:T(8,128)(2,1)} %bitcast.59), calls=%async_computation.1 | async-start | bytes 2097152 | tf_op jit(solution)/shard_map/all_to_all | solution.py:195
  38.3 15.3 %all-to-all-done.1 = bf16[128,32,128]{2,0,1:T(8,128)(2,1)S(1)} async-done(((bf16[128,32,128]{2,0,1:T(8,128)(2,1)}), bf16[128,32,128]{2,0,1:T(8,128)(2,1)S(1)}, u32[]{:S(2)}, u32[]{:S(2)}) %all-to-all-start.1) | async-done | bytes 1048608 | tf_op jit(solution)/shard_map/all_to_all | solution.py:195
  53.6 1.0 copy-done.2
  54.6 8.3 %shard_map.93 = (f32[1024,128]{1,0:T(8,128)}, f32[1024,128]{1,0:T(8,128)}, f32[1024,128]{1,0:T(8,128)}) custom-call(s32[9,2]{1,0:T(8,128)} %copy.38.refs_0_, s32[1]{0:T(128)} %bitcast.53.refs_1_, bf16[1024,128]{1,0:T(8,128)(2,1)} %bitcast.69, bf16[4096,128]{1,0:T(8,128)(2,1)} %bitcast.55, bf16[4096,128]{1,0:T(8,128)(2,1)} %bitcast.57), custom_call_target="tpu_custom_call" | custom-call | tf_op jit(solution)/shard_map/pallas_call | solution.py:65
  62.9 1.2 convert_element_type.62
  64.8 33.8 %all_to_all.90 = bf16[16,66,128]{2,1,0:T(8,128)(2,1)S(1)} all-to-all(bf16[16,66,128]{2,1,0:T(8,128)(2,1)S(1)} %pad_maximum_fusion), channel_id=1, replica_groups=mesh['grp'=16,'seq'=32] {'grp'}, dimensions={0} | all-to-all | bytes 540672 | tf_op jit(solution)/shard_map/all_to_all | solution.py:159
  99.3 19.7 %all_to_all.91 = bf16[16,66,128]{2,1,0:T(8,128)(2,1)S(1)} all-to-all(bf16[16,66,128]{2,1,0:T(8,128)(2,1)S(1)} %broadcast_in_dim.10), channel_id=1, replica_groups=mesh['grp'=16,'seq'=32] {'grp'}, dimensions={0} | all-to-all | bytes 540672 | tf_op jit(solution)/shard_map/all_to_all | solution.py:170
  119.1 1.3 add.43.refs_6_
  120.4 1.0 copy-done.4
  121.6 1.0 copy.44.refs_7_
  122.7 9.3 %shard_map.94 = (bf16[1024,128]{1,0:T(8,128)(2,1)}, bf16[4096,128]{1,0:T(8,128)(2,1)}, bf16[4096,128]{1,0:T(8,128)(2,1)}) custom-call(s32[9,2]{1,0:T(8,128)} %copy.38.refs_0_, s32[1]{0:T(128)} %bitcast.54.refs_1_, bf16[1024,128]{1,0:T(8,128)(2,1)} %bitcast.70, bf16[4096,128]{1,0:T(8,128)(2,1)} %bitcast.56, bf16[4096,128]{1,0:T(8,128)(2,1)} %bitcast.58, ...), custom_call_target="tpu_custom_call" | custom-call | tf_op jit(solution)/shard_map/pallas_call | solution.py:132
  132.0 24.3 %all_to_all.92 = bf16[16,64,128]{2,1,0:T(8,128)(2,1)S(1)} all-to-all(bf16[16,64,128]{2,1,0:T(8,128)(2,1)} %bitcast.71), channel_id=1, replica_groups=mesh['grp'=16,'seq'=32] {'grp'}, dimensions={0} | all-to-all | bytes 524288 | tf_op jit(solution)/shard_map/all_to_all | solution.py:159
  156.3 27.8 %all_to_all.93 = bf16[32,128,128]{2,1,0:T(8,128)(2,1)S(1)} all-to-all(bf16[32,128,128]{2,1,0:T(8,128)(2,1)} %bitcast.64), channel_id=1, replica_groups=mesh['grp'=16,'seq'=32] {'seq'}, dimensions={0} | all-to-all | bytes 2097152 | tf_op jit(solution)/shard_map/all_to_all | solution.py:265
  184.1 4.0 %all-to-all-start.7 = ((bf16[32,128,128]{2,1,0:T(8,128)(2,1)}), bf16[32,128,128]{2,1,0:T(8,128)(2,1)S(1)}, u32[]{:S(2)}, u32[]{:S(2)}) async-start(bf16[32,128,128]{2,1,0:T(8,128)(2,1)} %bitcast.63), calls=%async_computation.7 | async-start | bytes 2097152 | tf_op jit(solution)/shard_map/all_to_all | solution.py:268
  188.1 17.2 %all-to-all-done.7 = bf16[32,128,128]{2,1,0:T(8,128)(2,1)S(1)} async-done(((bf16[32,128,128]{2,1,0:T(8,128)(2,1)}), bf16[32,128,128]{2,1,0:T(8,128)(2,1)S(1)}, u32[]{:S(2)}, u32[]{:S(2)}) %all-to-all-start.7) | async-done | bytes 1048608 | tf_op jit(solution)/shard_map/all_to_all | solution.py:268
  206.1 5.1 %all-to-all-start.5 = ((bf16[16,64,128]{2,1,0:T(8,128)(2,1)}), bf16[16,64,128]{2,1,0:T(8,128)(2,1)S(1)}, u32[]{:S(2)}, u32[]{:S(2)}) async-start(bf16[16,64,128]{2,1,0:T(8,128)(2,1)} %broadcast_in_dim.11), calls=%async_computation.5 | async-start | bytes 524288 | tf_op jit(solution)/shard_map/all_to_all | solution.py:170
  211.7 1.0 copy.47
  213.2 1.0 copy.48
  214.2 11.0 %all-to-all-done.5 = bf16[16,64,128]{2,1,0:T(8,128)(2,1)S(1)} async-done(((bf16[16,64,128]{2,1,0:T(8,128)(2,1)}), bf16[16,64,128]{2,1,0:T(8,128)(2,1)S(1)}, u32[]{:S(2)}, u32[]{:S(2)}) %all-to-all-start.5) | async-done | bytes 262176 | tf_op jit(solution)/shard_map/all_to_all | solution.py:170
  (51 shorter events, 5.7 us)
Async XLA Ops:
  0.6 1.0 copy-start
  3.0 10.6 %copy-start.5 = (bf16[128,2048]{1,0:T(8,128)(2,1)S(1)}, bf16[128,2048]{1,0:T(8,128)(2,1)}, u32[]{:S(2)}) copy-start(bf16[128,2048]{1,0:T(8,128)(2,1)} %param.8) | copy-start | bytes 1572868
  3.0 27.9 %all-to-all-start = ((bf16[128,32,128]{2,0,1:T(8,128)(2,1)}), bf16[128,32,128]{2,0,1:T(8,128)(2,1)S(1)}, u32[]{:S(2)}, u32[]{:S(2)}) async-start(bf16[128,32,128]{2,0,1:T(8,128)(2,1)} %bitcast.3), calls=%async_computation | async-start | bytes 2097152 | tf_op jit(solution)/shard_map/all_to_all | solution.py:194
  30.9 1.4 copy-start.1
  32.3 21.3 %all-to-all-start.1 = ((bf16[128,32,128]{2,0,1:T(8,128)(2,1)}), bf16[128,32,128]{2,0,1:T(8,128)(2,1)S(1)}, u32[]{:S(2)}, u32[]{:S(2)}) async-start(bf16[128,32,128]{2,0,1:T(8,128)(2,1)} %bitcast.59), calls=%async_computation.1 | async-start | bytes 2097152 | tf_op jit(solution)/shard_map/all_to_all | solution.py:195
  36.9 0.7 copy-start.8
  53.6 1.0 copy-start.2
  62.9 1.2 copy-start.7
  62.9 1.5 copy-start.6
  120.4 1.0 copy-start.4
  120.4 1.2 copy-start.3
  184.1 21.3 %all-to-all-start.7 = ((bf16[32,128,128]{2,1,0:T(8,128)(2,1)}), bf16[32,128,128]{2,1,0:T(8,128)(2,1)S(1)}, u32[]{:S(2)}, u32[]{:S(2)}) async-start(bf16[32,128,128]{2,1,0:T(8,128)(2,1)} %bitcast.63), calls=%async_computation.7 | async-start | bytes 2097152 | tf_op jit(solution)/shard_map/all_to_all | solution.py:268
  206.1 19.0 %all-to-all-start.5 = ((bf16[16,64,128]{2,1,0:T(8,128)(2,1)}), bf16[16,64,128]{2,1,0:T(8,128)(2,1)S(1)}, u32[]{:S(2)}, u32[]{:S(2)}) async-start(bf16[16,64,128]{2,1,0:T(8,128)(2,1)} %broadcast_in_dim.11), calls=%async_computation.5 | async-start | bytes 524288 | tf_op jit(solution)/shard_map/all_to_all | solution.py:170

commit v4 on v3

--- a/solution.py
+++ b/solution.py
@@ -184,18 +184,20 @@
     copies = max(1, QPARTS // items_here)
     heads_here = max(1, items_here // QPARTS)
     softmax_scale = head_width ** (-0.5)
-    key_wide = jnp.repeat(
-        scene_keys.reshape(scene_here, heads_total, head_width), copies, axis=1
+    both_wide = jnp.repeat(
+        jnp.stack(
+            [
+                scene_keys.reshape(scene_here, heads_total, head_width),
+                scene_values.reshape(scene_here, heads_total, head_width),
+            ],
+            axis=2,
+        ),
+        copies,
+        axis=1,
     ).reshape(scene_here, -1)
-    value_wide = jnp.repeat(
-        scene_values.reshape(scene_here, heads_total, head_width), copies, axis=1
-    ).reshape(scene_here, -1)
-    key_group, value_group = (
-        lax.all_to_all(key_wide, "seq", split_axis=1, concat_axis=0, tiled=True),
-        lax.all_to_all(value_wide, "seq", split_axis=1, concat_axis=0, tiled=True),
-    )
-    key_group = key_group.reshape(group_keys, heads_here, head_width)
-    value_group = value_group.reshape(group_keys, heads_here, head_width)
+    both_group = lax.all_to_all(both_wide, "seq", split_axis=1, concat_axis=0, tiled=True)
+    key_group = both_group[:, None, :head_width]
+    value_group = both_group[:, None, head_width:]
     part_max, part_total, part_accum = forward_item(
         queries[0],
         key_group[:, 0, :],
@@ -259,32 +261,12 @@
         tile_counts[0, 0],
         softmax_scale,
     )
-    key_stack = key_grad[:, None, :]
-    value_stack = value_grad[:, None, :]
-    key_back, value_back = (
-        lax.all_to_all(
-            key_stack.reshape(group_keys, -1), "seq", split_axis=0, concat_axis=1, tiled=True
-        ),
-        lax.all_to_all(
-            value_stack.reshape(group_keys, -1), "seq", split_axis=0, concat_axis=1, tiled=True
-        ),
-    )
-    grad_keys = (
-        jnp.sum(
-            key_back.reshape(scene_here, heads_total, copies, head_width).astype(jnp.float32),
-            axis=2,
-        )
-        .astype(jnp.bfloat16)
-        .reshape(scene_here, -1)
-    )
-    grad_values = (
-        jnp.sum(
-            value_back.reshape(scene_here, heads_total, copies, head_width).astype(jnp.float32),
-            axis=2,
-        )
-        .astype(jnp.bfloat16)
-        .reshape(scene_here, -1)
-    )
+    both_back = lax.all_to_all(
+        jnp.concatenate([key_grad, value_grad], axis=1), "seq", split_axis=0, concat_axis=1, tiled=True
+    ).reshape(scene_here, heads_total, copies, 2, head_width)
+    both_sum = jnp.sum(both_back.astype(jnp.float32), axis=2).astype(jnp.bfloat16)
+    grad_keys = both_sum[:, :, 0, :].reshape(scene_here, -1)
+    grad_values = both_sum[:, :, 1, :].reshape(scene_here, -1)
     query_parts = scatter_rows(query_grad, groups)
     query_chunk = jnp.sum(query_parts.astype(jnp.float32), axis=0).astype(jnp.bfloat16)
     grad_queries = broadcast_rows(query_chunk, groups).reshape(1, query_rows, head_width)

time: 230 us -> 231 us (level); the launches traced: 226 us -> 230 us
  blocking collectives: 106 us -> 85.6 us
  local copies, waits for them, and re-layouts: 14.3 us -> 24.1 us
  starting transfers between devices: 23.7 us -> 32.4 us
  other arithmetic: 2.53 us -> 10.3 us
  Pallas kernels: 17.6 us -> 11.1 us
  waiting for transfers between devices: 60.6 us -> 64.6 us
    all_to_all x1 -> x0, blocking collectives: 27.8 us -> none  [per_device(): lax.all_to_all(key_stack.reshape(group_keys, -1), 'seq', split_axis=0, co...]
    all_to_all x1, starting transfers between devices: 5.13 us -> 11 us  [broadcast_rows(): lax.all_to_all(spread, 'grp', split_axis=0, concat_axis=0, tiled=True)]
    all_to_all x1, blocking collectives: 19.7 us -> 25.2 us  [broadcast_rows(): lax.all_to_all(spread, 'grp', split_axis=0, concat_axis=0, tiled=True)]
    reduce_sum x2 -> x1, other arithmetic: 0.32 us -> 5.31 us  [per_device(): jnp.sum(both_back.astype(jnp.float32), axis=2).astype(jnp.bfloat16)]
    slice x0 -> x4, local copies, waits for them, and re-layouts: none -> 4.87 us  [the longest x2 2.66 us: per_device(): grad_values = both_sum[:, :, 1, :].reshape(scene_here, -1)]
    all_to_all x3 -> x2, waiting for transfers between devices: 49.7 us -> 54.4 us  [the longest x1 27.8 us: per_device(): lax.all_to_all(jnp.concatenate([key_grad, value_grad], axis=1), 'seq', sp...]
    pallas_call x1, Pallas kernels: 9.34 us -> 6.02 us  [backward_item(): pl.pallas_call(lambda *refs: backward_kernel(softmax_scale, *refs), out_s...]
    pallas_call x1, Pallas kernels: 8.31 us -> 5.05 us  [forward_item(): pl.pallas_call(lambda *refs: forward_kernel(softmax_scale, *refs), out_sh...]
  transfers between devices with their start and end apart: 4 -> 3, of which waited for: 4 -> 3; matrix products, arithmetic and copies ran while one was open for 2% -> 2% of each run, Pallas kernels for 0% -> 0%
where the time goes in v4:
time: 231 us; the launch traced here: 230 us
  blocking collectives  85.6 us (37%)
  waiting for transfers between devices  64.6 us (28%)
  starting transfers between devices  32.4 us (14%)
  local copies, waits for them, and re-layouts  24.1 us (10%)
  Pallas kernels  11.1 us (5%)
  other arithmetic  10.3 us (4%)
    all_to_all x2, blocking collectives, scatter_rows(): lax.all_to_all(rows.reshape(parts, rows.shape[0] // parts, rows.shape[1])...  60.3 us
    all_to_all x1, waiting for transfers between devices, per_device(): lax.all_to_all(jnp.concatenate([key_grad, value_grad], axis=1), 'seq', sp...  27.8 us
    all_to_all x1, waiting for transfers between devices, per_device(): lax.all_to_all(both_wide, 'seq', split_axis=1, concat_axis=0, tiled=True)  26.6 us
    all_to_all x1, blocking collectives, broadcast_rows(): lax.all_to_all(spread, 'grp', split_axis=0, concat_axis=0, tiled=True)  25.2 us
    all_to_all x1, starting transfers between devices, broadcast_rows(): lax.all_to_all(spread, 'grp', split_axis=0, concat_axis=0, tiled=True)  11 us
    all_to_all x1, starting transfers between devices, per_device(): lax.all_to_all(jnp.concatenate([key_grad, value_grad], axis=1), 'seq', sp...  10.7 us
    all_to_all x1, starting transfers between devices, per_device(): lax.all_to_all(both_wide, 'seq', split_axis=1, concat_axis=0, tiled=True)  10.7 us
    all_to_all x1, waiting for transfers between devices, broadcast_rows(): lax.all_to_all(spread, 'grp', split_axis=0, concat_axis=0, tiled=True)  10.2 us
  transfers between devices with their start and end apart: 3, of which 3 were waited for; matrix products, arithmetic and copies ran while one was open for 2% of the time, Pallas kernels for 0%

profile of v4, /device:TPU:1, one launch (start us, length us, event | category | flops | bytes accessed | tf_op | source)
XLA Modules:
  0.0 229.5 jit_solution(6069208145416169929)
XLA Ops:
  0.6 1.1 copy.46
  1.8 1.1 copy.47
  3.0 1.1 copy.33
  4.1 1.9 broadcast_in_dim.6
  6.0 2.6 %all_to_all.38 = bf16[128,32,256]{2,0,1:T(8,128)(2,1)} reshape(bf16[128,16,2,2,128]{4,3,0,2,1:T(2,128)(2,1)S(1)} %broadcast_in_dim.6) | data formatting | bytes 4194304 | tf_op jit(solution)/shard_map/all_to_all | solution.py:198
  8.7 10.7 %all-to-all-start = ((bf16[128,32,256]{2,0,1:T(8,128)(2,1)}), bf16[128,32,256]{2,0,1:T(8,128)(2,1)S(1)}, u32[]{:S(2)}, u32[]{:S(2)}) async-start(bf16[128,32,256]{2,0,1:T(8,128)(2,1)} %all_to_all.38), calls=%async_computation | async-start | bytes 4194304 | tf_op jit(solution)/shard_map/all_to_all | solution.py:198
  20.7 26.6 %all-to-all-done = bf16[128,32,256]{2,0,1:T(8,128)(2,1)S(1)} async-done(((bf16[128,32,256]{2,0,1:T(8,128)(2,1)}), bf16[128,32,256]{2,0,1:T(8,128)(2,1)S(1)}, u32[]{:S(2)}, u32[]{:S(2)}) %all-to-all-start) | async-done | bytes 2097184 | tf_op jit(solution)/shard_map/all_to_all | solution.py:198
  47.3 1.5 fusion.5
  48.8 5.0 %shard_map.93 = (f32[1024,128]{1,0:T(8,128)}, f32[1024,128]{1,0:T(8,128)}, f32[1024,128]{1,0:T(8,128)}) custom-call(s32[9,2]{1,0:T(8,128)} %copy.34.refs_0_, s32[1]{0:T(128)} %bitcast.42.refs_1_, bf16[1024,128]{1,0:T(8,128)(2,1)} %bitcast.55, bf16[4096,128]{1,0:T(8,128)(2,1)} %get-tuple-element.25.refs_3_, bf16[4096,128]{1,0:T(8,128)(2,1)} %get-tuple-element.24.refs_4_), custom_call_target="tpu_custom_call" | custom-call | tf_op jit(solution)/shard_map/pallas_call | solution.py:65
  54.9 1.3 fusion.1
  56.3 1.3 slice_reduce_fusion
  57.8 31.6 %all_to_all.55 = bf16[16,66,128]{2,1,0:T(8,128)(2,1)S(1)} all-to-all(bf16[16,66,128]{2,1,0:T(8,128)(2,1)S(1)} %pad_maximum_fusion.2), channel_id=1, replica_groups=mesh['grp'=16,'seq'=32] {'grp'}, dimensions={0} | all-to-all | bytes 540672 | tf_op jit(solution)/shard_map/all_to_all | solution.py:159
  90.0 25.2 %all_to_all.56 = bf16[16,66,128]{2,1,0:T(8,128)(2,1)S(1)} all-to-all(bf16[16,66,128]{2,1,0:T(8,128)(2,1)S(1)} %broadcast_in_dim.7), channel_id=1, replica_groups=mesh['grp'=16,'seq'=32] {'grp'}, dimensions={0} | all-to-all | bytes 540672 | tf_op jit(solution)/shard_map/all_to_all | solution.py:170
  115.3 1.3 add.43.refs_6_
  117.9 6.0 %shard_map.94 = (bf16[1024,128]{1,0:T(8,128)(2,1)}, bf16[4096,128]{1,0:T(8,128)(2,1)}, bf16[4096,128]{1,0:T(8,128)(2,1)}) custom-call(s32[9,2]{1,0:T(8,128)} %copy.34.refs_0_, s32[1]{0:T(128)} %bitcast.43.refs_1_, bf16[1024,128]{1,0:T(8,128)(2,1)} %bitcast.56, bf16[4096,128]{1,0:T(8,128)(2,1)} %get-tuple-element.25.refs_3_, ...), custom_call_target="tpu_custom_call" | custom-call | tf_op jit(solution)/shard_map/pallas_call | solution.py:132
  123.9 28.8 %all_to_all.57 = bf16[16,64,128]{2,1,0:T(8,128)(2,1)S(1)} all-to-all(bf16[16,64,128]{2,1,0:T(8,128)(2,1)} %bitcast.59), channel_id=1, replica_groups=mesh['grp'=16,'seq'=32] {'grp'}, dimensions={0} | all-to-all | bytes 524288 | tf_op jit(solution)/shard_map/all_to_all | solution.py:159
  153.5 11.0 %all-to-all-start.4 = ((bf16[16,64,128]{2,1,0:T(8,128)(2,1)}), bf16[16,64,128]{2,1,0:T(8,128)(2,1)S(1)}, u32[]{:S(2)}, u32[]{:S(2)}) async-start(bf16[16,64,128]{2,1,0:T(8,128)(2,1)} %broadcast_in_dim.8), calls=%async_computation.4 | async-start | bytes 524288 | tf_op jit(solution)/shard_map/all_to_all | solution.py:170
  164.5 2.8 %pad_maximum_fusion = bf16[4096,256]{1,0:T(8,128)(2,1)} fusion(bf16[4096,128]{1,0:T(8,128)(2,1)} %get-tuple-element.15, bf16[4096,128]{1,0:T(8,128)(2,1)S(1)} %copy-done.1), kind=kLoop, calls=%fused_computation | loop fusion | flops 4194304 | bytes 4194304 | tf_op jit(solution)/shard_map/concatenate | solution.py:265
  167.3 10.2 %all-to-all-done.4 = bf16[16,64,128]{2,1,0:T(8,128)(2,1)S(1)} async-done(((bf16[16,64,128]{2,1,0:T(8,128)(2,1)}), bf16[16,64,128]{2,1,0:T(8,128)(2,1)S(1)}, u32[]{:S(2)}, u32[]{:S(2)}) %all-to-all-start.4) | async-done | bytes 262176 | tf_op jit(solution)/shard_map/all_to_all | solution.py:170
  177.5 10.7 %all-to-all-start.5 = ((bf16[32,128,256]{2,1,0:T(8,128)(2,1)}), bf16[32,128,256]{2,1,0:T(8,128)(2,1)S(1)}, u32[]{:S(2)}, u32[]{:S(2)}) async-start(bf16[32,128,256]{2,1,0:T(8,128)(2,1)} %bitcast.18), calls=%async_computation.5 | async-start | bytes 4194304 | tf_op jit(solution)/shard_map/all_to_all | solution.py:264
  188.3 27.8 %all-to-all-done.5 = bf16[32,128,256]{2,1,0:T(8,128)(2,1)S(1)} async-done(((bf16[32,128,256]{2,1,0:T(8,128)(2,1)}), bf16[32,128,256]{2,1,0:T(8,128)(2,1)S(1)}, u32[]{:S(2)}, u32[]{:S(2)}) %all-to-all-start.5) | async-done | bytes 2097184 | tf_op jit(solution)/shard_map/all_to_all | solution.py:264
  216.0 2.1 reshape.116
  218.1 5.3 %reduce_sum.55 = bf16[128,16,2,128]{3,2,0,1:T(2,128)(2,1)S(1)} reduce(bf16[128,16,2,2,128]{4,3,0,2,1:T(2,128)(2,1)} %reshape.116, bf16[]{:T(256)} %constant.3.clone.1), dimensions={2}, to_apply=%region_5.0 | reduce | flops 524288 | bytes 3145730 | tf_op jit(solution)/shard_map/reduce_sum | solution.py:267
  223.4 1.9 fusion.6
  (43 shorter events, 9.1 us)
Async XLA Ops:
  8.7 11.3 %copy-start.3 = (s32[1,1,9,2]{2,3,1,0:T(2,128)S(1)}, s32[1,1,9,2]{2,3,1,0:T(2,128)}, u32[]{:S(2)}) copy-start(s32[1,1,9,2]{2,3,1,0:T(2,128)} %param.10) | copy-start | bytes 220
  8.7 38.6 %all-to-all-start = ((bf16[128,32,256]{2,0,1:T(8,128)(2,1)}), bf16[128,32,256]{2,0,1:T(8,128)(2,1)S(1)}, u32[]{:S(2)}, u32[]{:S(2)}) async-start(bf16[128,32,256]{2,0,1:T(8,128)(2,1)} %all_to_all.38), calls=%async_computation | async-start | bytes 4194304 | tf_op jit(solution)/shard_map/all_to_all | solution.py:198
  57.7 58.9 %copy-start.2 = (bf16[1,1024,128]{2,1,0:T(8,128)(2,1)S(1)}, bf16[1,1024,128]{2,1,0:T(8,128)(2,1)}, u32[]{:S(2)}) copy-start(bf16[1,1024,128]{2,1,0:T(8,128)(2,1)} %param.9) | copy-start | bytes 786436
  116.6 7.3 %copy-start = (bf16[16,64,128]{2,1,0:T(8,128)(2,1)}, bf16[16,64,128]{2,1,0:T(8,128)(2,1)S(1)}, u32[]{:S(2)}) copy-start(bf16[16,64,128]{2,1,0:T(8,128)(2,1)S(1)} %slice.68) | copy-start | bytes 786436
  123.9 40.6 %copy-start.1 = (bf16[4096,128]{1,0:T(8,128)(2,1)S(1)}, bf16[4096,128]{1,0:T(8,128)(2,1)}, u32[]{:S(2)}) copy-start(bf16[4096,128]{1,0:T(8,128)(2,1)} %get-tuple-element.14) | copy-start | bytes 3145732
  153.5 24.1 %all-to-all-start.4 = ((bf16[16,64,128]{2,1,0:T(8,128)(2,1)}), bf16[16,64,128]{2,1,0:T(8,128)(2,1)S(1)}, u32[]{:S(2)}, u32[]{:S(2)}) async-start(bf16[16,64,128]{2,1,0:T(8,128)(2,1)} %broadcast_in_dim.8), calls=%async_computation.4 | async-start | bytes 524288 | tf_op jit(solution)/shard_map/all_to_all | solution.py:170
  177.5 38.5 %all-to-all-start.5 = ((bf16[32,128,256]{2,1,0:T(8,128)(2,1)}), bf16[32,128,256]{2,1,0:T(8,128)(2,1)S(1)}, u32[]{:S(2)}, u32[]{:S(2)}) async-start(bf16[32,128,256]{2,1,0:T(8,128)(2,1)} %bitcast.18), calls=%async_computation.5 | async-start | bytes 4194304 | tf_op jit(solution)/shard_map/all_to_all | solution.py:264

commit v5 on v4

--- a/solution.py
+++ b/solution.py
@@ -155,19 +155,56 @@
     )
 
 
-def scatter_rows(rows, parts):
-    return lax.all_to_all(
-        rows.reshape(parts, rows.shape[0] // parts, rows.shape[1]),
-        "grp",
-        split_axis=0,
-        concat_axis=0,
-        tiled=True,
-    )
-
-
-def broadcast_rows(chunk, parts):
-    spread = jnp.broadcast_to(chunk[None], (parts,) + chunk.shape)
-    gathered = lax.all_to_all(spread, "grp", split_axis=0, concat_axis=0, tiled=True)
+def exchange_kernel(broadcast, x_ref, y_ref, send_sem, recv_sem):
+    groups = y_ref.shape[0]
+    me = lax.axis_index("grp")
+    lane = lax.axis_index("seq")
+    mesh_ids = pl.DeviceIdType.MESH
+    barrier = pltpu.get_barrier_semaphore()
+    for step in range(1, groups):
+        pl.semaphore_signal(
+            barrier, inc=1, device_id=(lax.rem(me + step, groups), lane), device_id_type=mesh_ids
+        )
+    pl.semaphore_wait(barrier, groups - 1)
+    copies = []
+    for step in range(1, groups):
+        target = lax.rem(me + step, groups)
+        copy = pltpu.make_async_remote_copy(
+            src_ref=x_ref if broadcast else x_ref.at[target],
+            dst_ref=y_ref.at[me],
+            send_sem=send_sem.at[step],
+            recv_sem=recv_sem.at[step],
+            device_id=(target, lane),
+            device_id_type=mesh_ids,
+        )
+        copy.start()
+        copies.append(copy)
+    y_ref[me] = x_ref[...] if broadcast else x_ref[me]
+    for copy in copies:
+        copy.wait()
+
+
+def grp_exchange(x, groups, broadcast, collective):
+    out_shape = (groups,) + (x.shape if broadcast else x.shape[1:])
+    vmem = pl.BlockSpec(memory_space=pltpu.VMEM)
+    return pl.pallas_call(
+        lambda *refs: exchange_kernel(broadcast, *refs),
+        out_shape=jax.ShapeDtypeStruct(out_shape, x.dtype),
+        in_specs=[vmem],
+        out_specs=vmem,
+        scratch_shapes=[pltpu.SemaphoreType.DMA((groups,)), pltpu.SemaphoreType.DMA((groups,))],
+        compiler_params=pltpu.CompilerParams(collective_id=collective, has_side_effects=True),
+    )(x)
+
+
+def scatter_rows(rows, parts, collective):
+    return grp_exchange(
+        rows.reshape(parts, rows.shape[0] // parts, rows.shape[1]), parts, False, collective
+    )
+
+
+def broadcast_rows(chunk, parts, collective):
+    gathered = grp_exchange(chunk, parts, True, collective)
     return gathered.reshape(parts * chunk.shape[0], chunk.shape[1])
 
 
@@ -224,7 +261,7 @@
     packed = jnp.concatenate(
         [part_accum.astype(jnp.bfloat16).reshape(groups, chunk_rows, head_width), stats], axis=1
     )
-    arrived = scatter_rows(packed.reshape(groups * (chunk_rows + 2), head_width), groups)
+    arrived = scatter_rows(packed.reshape(groups * (chunk_rows + 2), head_width), groups, 0)
     arrived = arrived.reshape(groups, chunk_rows + 2, head_width).astype(jnp.float32)
     got_accum = arrived[:, :chunk_rows, :]
     got_max = arrived[:, chunk_rows, :chunk_rows]
@@ -242,7 +279,7 @@
             jnp.concatenate([chunk_lo, jnp.zeros((chunk_rows,), jnp.bfloat16)]),
         ]
     )
-    back = broadcast_rows(jnp.concatenate([chunk_out, chunk_stats], axis=0), groups)
+    back = broadcast_rows(jnp.concatenate([chunk_out, chunk_stats], axis=0), groups, 1)
     back = back.reshape(groups, chunk_rows + 2, head_width)
     attended = back[:, :chunk_rows, :].reshape(1, query_rows, head_width)
     back_stats = back[:, chunk_rows:, :].astype(jnp.float32)
@@ -267,9 +304,9 @@
     both_sum = jnp.sum(both_back.astype(jnp.float32), axis=2).astype(jnp.bfloat16)
     grad_keys = both_sum[:, :, 0, :].reshape(scene_here, -1)
     grad_values = both_sum[:, :, 1, :].reshape(scene_here, -1)
-    query_parts = scatter_rows(query_grad, groups)
+    query_parts = scatter_rows(query_grad, groups, 2)
     query_chunk = jnp.sum(query_parts.astype(jnp.float32), axis=0).astype(jnp.bfloat16)
-    grad_queries = broadcast_rows(query_chunk, groups).reshape(1, query_rows, head_width)
+    grad_queries = broadcast_rows(query_chunk, groups, 3).reshape(1, query_rows, head_width)
     return (attended, grad_queries, grad_keys, grad_values)
 
 

time: 231 us -> 206 us (0.89)
  Pallas kernels: 11.1 us -> 108 us
  blocking collectives: 85.6 us -> 0 us
  waiting for transfers between devices: 64.6 us -> 26.6 us
  starting transfers between devices: 32.4 us -> 26.9 us
  other arithmetic: 10.3 us -> 15.2 us
    pallas_call x0 -> x4, Pallas kernels: none -> 96.8 us  [grp_exchange(): pl.pallas_call(lambda *refs: exchange_kernel(broadcast, *refs), out_shape...]
    all_to_all x3 -> x0, blocking collectives: 85.6 us -> none  [the longest x2 60.3 us: scatter_rows(): lax.all_to_all(rows.reshape(parts, rows.shape[0] // parts, rows.shape[1])...]
    all_to_all x1, waiting for transfers between devices: 27.8 us -> 0.01 us  [per_device(): lax.all_to_all(jnp.concatenate([key_grad, value_grad], axis=1), 'seq', sp...]
    all_to_all x1 -> x0, starting transfers between devices: 11 us -> none  [broadcast_rows(): lax.all_to_all(spread, 'grp', split_axis=0, concat_axis=0, tiled=True)]
    all_to_all x1 -> x0, waiting for transfers between devices: 10.2 us -> none  [broadcast_rows(): lax.all_to_all(spread, 'grp', split_axis=0, concat_axis=0, tiled=True)]
    all_to_all x1, starting transfers between devices: 10.7 us -> 16.2 us  [per_device(): lax.all_to_all(jnp.concatenate([key_grad, value_grad], axis=1), 'seq', sp...]
  transfers between devices with their start and end apart: 3 -> 2, of which waited for: 3 -> 1; matrix products, arithmetic and copies ran while one was open for 2% -> 1% of each run, Pallas kernels for 0% -> 22%
where the time goes in v5:
time: 206 us; the launch traced here: 203 us
  Pallas kernels  108 us (52%)
  starting transfers between devices  26.9 us (13%)
  waiting for transfers between devices  26.6 us (13%)
  local copies, waits for them, and re-layouts  25 us (12%)
  other arithmetic  15.2 us (7%)
    pallas_call x4, Pallas kernels, grp_exchange(): pl.pallas_call(lambda *refs: exchange_kernel(broadcast, *refs), out_shape...  96.8 us
    all_to_all x1, waiting for transfers between devices, per_device(): lax.all_to_all(both_wide, 'seq', split_axis=1, concat_axis=0, tiled=True)  26.6 us
    all_to_all x1, starting transfers between devices, per_device(): lax.all_to_all(jnp.concatenate([key_grad, value_grad], axis=1), 'seq', sp...  16.2 us
    all_to_all x1, starting transfers between devices, per_device(): lax.all_to_all(both_wide, 'seq', split_axis=1, concat_axis=0, tiled=True)  10.7 us
    pallas_call x1, Pallas kernels, backward_item(): pl.pallas_call(lambda *refs: backward_kernel(softmax_scale, *refs), out_s...  6.02 us
    reduce_sum x1, other arithmetic, per_device(): jnp.sum(both_back.astype(jnp.float32), axis=2).astype(jnp.bfloat16)  5.31 us
    pallas_call x1, Pallas kernels, forward_item(): pl.pallas_call(lambda *refs: forward_kernel(softmax_scale, *refs), out_sh...  5.05 us
    unnamed x13, local copies, waits for them, and re-layouts  5.03 us
  transfers between devices with their start and end apart: 2, of which 1 were waited for; matrix products, arithmetic and copies ran while one was open for 1% of the time, Pallas kernels for 22%

profile of v5, /device:TPU:1, one launch (start us, length us, event | category | flops | bytes accessed | tf_op | source)
XLA Modules:
  0.0 203.1 jit_solution(18120415714952505856)
XLA Ops:
  0.6 1.1 copy.51
  1.8 1.1 copy.52
  3.0 1.1 copy.38
  4.1 1.9 broadcast_in_dim.2
  6.0 2.6 %all_to_all.26 = bf16[128,32,256]{2,0,1:T(8,128)(2,1)} reshape(bf16[128,16,2,2,128]{4,3,0,2,1:T(2,128)(2,1)S(1)} %broadcast_in_dim.2) | data formatting | bytes 4194304 | tf_op jit(solution)/shard_map/all_to_all | solution.py:235
  8.7 10.7 %all-to-all-start = ((bf16[128,32,256]{2,0,1:T(8,128)(2,1)}), bf16[128,32,256]{2,0,1:T(8,128)(2,1)S(1)}, u32[]{:S(2)}, u32[]{:S(2)}) async-start(bf16[128,32,256]{2,0,1:T(8,128)(2,1)} %all_to_all.26), calls=%async_computation | async-start | bytes 4194304 | tf_op jit(solution)/shard_map/all_to_all | solution.py:235
  20.7 26.6 %all-to-all-done = bf16[128,32,256]{2,0,1:T(8,128)(2,1)S(1)} async-done(((bf16[128,32,256]{2,0,1:T(8,128)(2,1)}), bf16[128,32,256]{2,0,1:T(8,128)(2,1)S(1)}, u32[]{:S(2)}, u32[]{:S(2)}) %all-to-all-start) | async-done | bytes 2097184 | tf_op jit(solution)/shard_map/all_to_all | solution.py:235
  47.3 1.5 fusion.5
  48.8 5.0 %shard_map.93 = (f32[1024,128]{1,0:T(8,128)}, f32[1024,128]{1,0:T(8,128)}, f32[1024,128]{1,0:T(8,128)}) custom-call(s32[9,2]{1,0:T(8,128)} %copy.39.refs_0_, s32[1]{0:T(128)} %bitcast.42.refs_1_, bf16[1024,128]{1,0:T(8,128)(2,1)} %bitcast.56, bf16[4096,128]{1,0:T(8,128)(2,1)} %get-tuple-element.25.refs_3_, bf16[4096,128]{1,0:T(8,128)(2,1)} %get-tuple-element.24.refs_4_), custom_call_target="tpu_custom_call" | custom-call | tf_op jit(solution)/shard_map/pallas_call | solution.py:65
  53.8 1.1 convert_element_type.60
  54.9 1.3 fusion.1
  56.3 1.3 slice_reduce_fusion
  58.5 28.5 %shard_map.94 = bf16[16,66,128]{2,1,0:T(8,128)(2,1)} custom-call(bf16[16,66,128]{2,1,0:T(8,128)(2,1)} %pad_maximum_fusion.2.refs_0_), custom_call_target="tpu_custom_call" | custom-call | tf_op jit(solution)/shard_map/pallas_call | solution.py:190
  89.9 24.1 %shard_map.95 = bf16[16,66,128]{2,1,0:T(8,128)(2,1)} custom-call(bf16[66,128]{1,0:T(8,128)(2,1)} %pad_maximum_fusion.3.refs_0_), custom_call_target="tpu_custom_call" | custom-call | tf_op jit(solution)/shard_map/pallas_call | solution.py:190
  115.9 1.3 add.43.refs_6_
  118.4 6.0 %shard_map.96 = (bf16[1024,128]{1,0:T(8,128)(2,1)}, bf16[4096,128]{1,0:T(8,128)(2,1)}, bf16[4096,128]{1,0:T(8,128)(2,1)}) custom-call(s32[9,2]{1,0:T(8,128)} %copy.39.refs_0_, s32[1]{0:T(128)} %bitcast.43.refs_1_, bf16[1024,128]{1,0:T(8,128)(2,1)} %bitcast.57, bf16[4096,128]{1,0:T(8,128)(2,1)} %get-tuple-element.25.refs_3_, ...), custom_call_target="tpu_custom_call" | custom-call | tf_op jit(solution)/shard_map/pallas_call | solution.py:132
  124.4 3.1 %pad_maximum_fusion = bf16[4096,256]{1,0:T(8,128)(2,1)} fusion(bf16[4096,128]{1,0:T(8,128)(2,1)} %get-tuple-element.15, bf16[4096,128]{1,0:T(8,128)(2,1)} %get-tuple-element.14), kind=kLoop, calls=%fused_computation | loop fusion | flops 4194304 | bytes 4194304 | tf_op jit(solution)/shard_map/concatenate | solution.py:302
  127.5 16.2 %all-to-all-start.1 = ((bf16[32,128,256]{2,1,0:T(8,128)(2,1)}), bf16[32,128,256]{2,1,0:T(8,128)(2,1)S(1)}, u32[]{:S(2)}, u32[]{:S(2)}) async-start(bf16[32,128,256]{2,1,0:T(8,128)(2,1)} %bitcast.46), calls=%async_computation.1 | async-start | bytes 4194304 | tf_op jit(solution)/shard_map/all_to_all | solution.py:301
  143.7 23.3 %shard_map.97 = bf16[16,64,128]{2,1,0:T(8,128)(2,1)} custom-call(bf16[16,64,128]{2,1,0:T(8,128)(2,1)} %bitcast.60), custom_call_target="tpu_custom_call" | custom-call | tf_op jit(solution)/shard_map/pallas_call | solution.py:190
  167.1 1.6 reduce_sum.54.refs_0_
  168.7 20.9 %shard_map.98 = bf16[16,64,128]{2,1,0:T(8,128)(2,1)} custom-call(bf16[64,128]{1,0:T(8,128)(2,1)} %reduce_sum.54.refs_0_), custom_call_target="tpu_custom_call" | custom-call | tf_op jit(solution)/shard_map/pallas_call | solution.py:190
  189.6 2.1 %reshape.114 = bf16[128,16,2,2,128]{4,3,0,2,1:T(2,128)(2,1)} reshape(bf16[128,32,256]{2,0,1:T(8,128)(2,1)S(1)} %bitcast.44) | data formatting | bytes 4194304 | tf_op jit(solution)/shard_map/reshape | solution.py:303
  191.7 5.3 %reduce_sum.55 = bf16[128,16,2,128]{3,2,0,1:T(2,128)(2,1)S(1)} reduce(bf16[128,16,2,2,128]{4,3,0,2,1:T(2,128)(2,1)} %reshape.114, bf16[]{:T(256)} %constant.3.clone.1), dimensions={2}, to_apply=%region_5.0 | reduce | flops 524288 | bytes 3145730 | tf_op jit(solution)/shard_map/reduce_sum | solution.py:304
  197.0 1.9 fusion.6
  (40 shorter events, 11.9 us)
Async XLA Ops:
  8.7 11.3 %copy-start.3 = (s32[1,1,9,2]{2,3,1,0:T(2,128)S(1)}, s32[1,1,9,2]{2,3,1,0:T(2,128)}, u32[]{:S(2)}) copy-start(s32[1,1,9,2]{2,3,1,0:T(2,128)} %param.10) | copy-start | bytes 220
  8.7 38.6 %all-to-all-start = ((bf16[128,32,256]{2,0,1:T(8,128)(2,1)}), bf16[128,32,256]{2,0,1:T(8,128)(2,1)S(1)}, u32[]{:S(2)}, u32[]{:S(2)}) async-start(bf16[128,32,256]{2,0,1:T(8,128)(2,1)} %all_to_all.26), calls=%async_computation | async-start | bytes 4194304 | tf_op jit(solution)/shard_map/all_to_all | solution.py:235
  57.7 59.4 %copy-start.2 = (bf16[1,1024,128]{2,1,0:T(8,128)(2,1)S(1)}, bf16[1,1024,128]{2,1,0:T(8,128)(2,1)}, u32[]{:S(2)}) copy-start(bf16[1,1024,128]{2,1,0:T(8,128)(2,1)} %param.9) | copy-start | bytes 786436
  115.7 8.7 %copy-start = (bf16[16,64,128]{2,1,0:T(8,128)(2,1)}, bf16[16,64,128]{2,1,0:T(8,128)(2,1)S(1)}, u32[]{:S(2)}) copy-start(bf16[16,64,128]{2,1,0:T(8,128)(2,1)S(1)} %slice.54) | copy-start | bytes 786436
  127.5 62.0 %all-to-all-start.1 = ((bf16[32,128,256]{2,1,0:T(8,128)(2,1)}), bf16[32,128,256]{2,1,0:T(8,128)(2,1)S(1)}, u32[]{:S(2)}, u32[]{:S(2)}) async-start(bf16[32,128,256]{2,1,0:T(8,128)(2,1)} %bitcast.46), calls=%async_computation.1 | async-start | bytes 4194304 | tf_op jit(solution)/shard_map/all_to_all | solution.py:301
  199.6 2.8 %copy-start.1 = (bf16[16,64,128]{2,1,0:T(8,128)(2,1)S(1)}, bf16[16,64,128]{2,1,0:T(8,128)(2,1)}, u32[]{:S(2)}) copy-start(bf16[16,64,128]{2,1,0:T(8,128)(2,1)} %shard_map.98) | copy-start | bytes 786436

commit v6 on v5

--- a/solution.py
+++ b/solution.py
@@ -221,18 +221,23 @@
     copies = max(1, QPARTS // items_here)
     heads_here = max(1, items_here // QPARTS)
     softmax_scale = head_width ** (-0.5)
-    both_wide = jnp.repeat(
-        jnp.stack(
-            [
-                scene_keys.reshape(scene_here, heads_total, head_width),
-                scene_values.reshape(scene_here, heads_total, head_width),
-            ],
-            axis=2,
-        ),
-        copies,
-        axis=1,
-    ).reshape(scene_here, -1)
-    both_group = lax.all_to_all(both_wide, "seq", split_axis=1, concat_axis=0, tiled=True)
+    half_keys = scene_here // QPARTS
+    both_here = jnp.stack(
+        [
+            scene_keys.reshape(QPARTS, half_keys, heads_total, head_width),
+            scene_values.reshape(QPARTS, half_keys, heads_total, head_width),
+        ],
+        axis=3,
+    ).transpose(2, 0, 1, 3, 4)
+    mine = lax.all_to_all(
+        both_here.reshape(seq_devices, half_keys, 2 * head_width), "seq", 0, 0, tiled=True
+    )
+    pairs = [(2 * h + c, 2 * h + 1 - c) for h in range(seq_devices // 2) for c in range(2)]
+    other = lax.ppermute(mine, "seq", pairs)
+    core = lax.rem(lax.axis_index("seq"), 2)
+    both_group = jnp.where(
+        core == 0, jnp.stack([mine, other], axis=1), jnp.stack([other, mine], axis=1)
+    ).reshape(group_keys, 2 * head_width)
     key_group = both_group[:, None, :head_width]
     value_group = both_group[:, None, head_width:]
     part_max, part_total, part_accum = forward_item(
@@ -298,12 +303,19 @@
         tile_counts[0, 0],
         softmax_scale,
     )
-    both_back = lax.all_to_all(
-        jnp.concatenate([key_grad, value_grad], axis=1), "seq", split_axis=0, concat_axis=1, tiled=True
-    ).reshape(scene_here, heads_total, copies, 2, head_width)
-    both_sum = jnp.sum(both_back.astype(jnp.float32), axis=2).astype(jnp.bfloat16)
-    grad_keys = both_sum[:, :, 0, :].reshape(scene_here, -1)
-    grad_values = both_sum[:, :, 1, :].reshape(scene_here, -1)
+    both_parts = jnp.concatenate([key_grad, value_grad], axis=1).reshape(
+        seq_devices, QPARTS, half_keys, 2 * head_width
+    )
+    kept = lax.dynamic_index_in_dim(both_parts, core, axis=1, keepdims=False)
+    given = lax.dynamic_index_in_dim(both_parts, 1 - core, axis=1, keepdims=False)
+    summed = (kept.astype(jnp.float32) + lax.ppermute(given, "seq", pairs).astype(jnp.float32)).astype(
+        jnp.bfloat16
+    )
+    both_back = lax.all_to_all(summed, "seq", 0, 0, tiled=True)
+    both_back = both_back.reshape(heads_total, QPARTS, half_keys, 2, head_width).transpose(1, 2, 0, 3, 4)
+    both_back = both_back.reshape(scene_here, heads_total, 2, head_width)
+    grad_keys = both_back[:, :, 0, :].reshape(scene_here, -1)
+    grad_values = both_back[:, :, 1, :].reshape(scene_here, -1)
     query_parts = scatter_rows(query_grad, groups, 2)
     query_chunk = jnp.sum(query_parts.astype(jnp.float32), axis=0).astype(jnp.bfloat16)
     grad_queries = broadcast_rows(query_chunk, groups, 3).reshape(1, query_rows, head_width)

time: 206 us -> 192 us (0.932)
  blocking collectives: 0 us -> 26.8 us
  waiting for transfers between devices: 26.6 us -> 3.3 us
  local copies, waits for them, and re-layouts: 25 us -> 16.8 us
  starting transfers between devices: 26.9 us -> 19 us
  other arithmetic: 15.2 us -> 11.4 us
    all_to_all x0 -> x1, blocking collectives: none -> 26.8 us  [per_device(): lax.all_to_all(both_here.reshape(seq_devices, half_keys, 2 * head_width),...]
    all_to_all x2 -> x1, waiting for transfers between devices: 26.6 us -> 0.01 us  [per_device(): both_back = lax.all_to_all(summed, 'seq', 0, 0, tiled=True)]
    all_to_all x2 -> x1, starting transfers between devices: 26.9 us -> 7.43 us  [per_device(): both_back = lax.all_to_all(summed, 'seq', 0, 0, tiled=True)]
    ppermute x0 -> x2, starting transfers between devices: none -> 11.6 us  [the longest x1 9.28 us: per_device(): lax.ppermute(given, 'seq', pairs).astype(jnp.float32)]
    reduce_sum x1 -> x0, other arithmetic: 5.31 us -> none  [per_device(): jnp.sum(both_back.astype(jnp.float32), axis=2).astype(jnp.bfloat16)]
    ppermute x0 -> x2, waiting for transfers between devices: none -> 3.3 us  [the longest x1 2.39 us: per_device(): lax.ppermute(given, 'seq', pairs).astype(jnp.float32)]
    slice x3 -> x1, local copies, waits for them, and re-layouts: 3.38 us -> 0.18 us  [per_device(): grad_values = both_back[:, :, 1, :].reshape(scene_here, -1)]
    all_to_all x1 -> x0, local copies, waits for them, and re-layouts: 2.65 us -> none  [per_device(): lax.all_to_all(both_wide, 'seq', split_axis=1, concat_axis=0, tiled=True)]
  transfers between devices with their start and end apart: 2 -> 3, of which waited for: 1 -> 2; matrix products, arithmetic and copies ran while one was open for 1% -> 1% of each run, Pallas kernels for 22% -> 24%
where the time goes in v6:
time: 192 us; the launch traced here: 189 us
  Pallas kernels  110 us (57%)
  blocking collectives  26.8 us (14%)
  starting transfers between devices  19 us (10%)
  local copies, waits for them, and re-layouts  16.8 us (9%)
  other arithmetic  11.4 us (6%)
  waiting for transfers between devices  3.3 us (2%)
    pallas_call x4, Pallas kernels, grp_exchange(): pl.pallas_call(lambda *refs: exchange_kernel(broadcast, *refs), out_shape...  98.9 us
    all_to_all x1, blocking collectives, per_device(): lax.all_to_all(both_here.reshape(seq_devices, half_keys, 2 * head_width),...  26.8 us
    ppermute x1, starting transfers between devices, per_device(): lax.ppermute(given, 'seq', pairs).astype(jnp.float32)  9.28 us
    all_to_all x1, starting transfers between devices, per_device(): both_back = lax.all_to_all(summed, 'seq', 0, 0, tiled=True)  7.43 us
    pallas_call x1, Pallas kernels, backward_item(): pl.pallas_call(lambda *refs: backward_kernel(softmax_scale, *refs), out_s...  6.02 us
    pallas_call x1, Pallas kernels, forward_item(): pl.pallas_call(lambda *refs: forward_kernel(softmax_scale, *refs), out_sh...  5.05 us
    unnamed x13, local copies, waits for them, and re-layouts  4.88 us
  transfers between devices with their start and end apart: 3, of which 2 were waited for; matrix products, arithmetic and copies ran while one was open for 1% of the time, Pallas kernels for 24%

profile of v6, /device:TPU:1, one launch (start us, length us, event | category | flops | bytes accessed | tf_op | source)
XLA Modules:
  0.0 188.9 jit_solution(5377218603185054464)
XLA Ops:
  0.6 1.1 copy.34
  1.8 1.1 copy.35
  3.0 1.1 copy.24
  4.9 26.8 %all_to_all.10 = bf16[32,64,256]{2,1,0:T(8,128)(2,1)S(1)} all-to-all(bf16[32,64,256]{2,1,0:T(8,128)(2,1)S(1)} %reshape.119), channel_id=1, replica_groups=mesh['grp'=16,'seq'=32] {'seq'}, dimensions={0} | all-to-all | bytes 2097152 | tf_op jit(solution)/shard_map/all_to_all | solution.py:232
  31.7 2.3 %collective-permute-start = (bf16[32,64,256]{2,1,0:T(8,128)(2,1)S(1)}, bf16[32,64,256]{2,1,0:T(8,128)(2,1)S(1)}, u32[]{:S(2)}, u32[]{:S(2)}) collective-permute-start(bf16[32,64,256]{2,1,0:T(8,128)(2,1)S(1)} %all_to_all.10), channel_id=1, source_target_pairs={{0,1},{1,0},{2,3},{3,2},{4,5},{5,4},{6,7},{7,6},{8,9},{9,8},{10,11... | collective-permute-start | bytes 3145736 | tf_op jit(solution)/shard_map/ppermute | solution.py:236
  36.5 1.5 fusion.6
  37.9 5.1 %shard_map.93 = (f32[1024,128]{1,0:T(8,128)}, f32[1024,128]{1,0:T(8,128)}, f32[1024,128]{1,0:T(8,128)}) custom-call(s32[9,2]{1,0:T(8,128)} %copy.25.refs_0_, s32[1]{0:T(128)} %bitcast.56.refs_1_, bf16[1024,128]{1,0:T(8,128)(2,1)} %bitcast.74, bf16[4096,128]{1,0:T(8,128)(2,1)} %get-tuple-element.21.refs_3_, bf16[4096,128]{1,0:T(8,128)(2,1)} %get-tuple-element.20.refs_4_), custom_call_target="tpu_custom_call" | custom-call | tf_op jit(solution)/shard_map/pallas_call | solution.py:65
  43.0 1.2 slice_reduce_fusion
  44.3 1.3 fusion.2
  45.8 1.1 convert_element_type.70
  47.6 31.2 %shard_map.94 = bf16[16,66,128]{2,1,0:T(8,128)(2,1)} custom-call(bf16[16,66,128]{2,1,0:T(8,128)(2,1)} %pad_maximum_fusion.1.refs_0_), custom_call_target="tpu_custom_call" | custom-call | tf_op jit(solution)/shard_map/pallas_call | solution.py:190
  78.8 1.0 convert_element_type.75
  81.8 23.0 %shard_map.95 = bf16[16,66,128]{2,1,0:T(8,128)(2,1)} custom-call(bf16[66,128]{1,0:T(8,128)(2,1)} %pad_maximum_fusion.2.refs_0_), custom_call_target="tpu_custom_call" | custom-call | tf_op jit(solution)/shard_map/pallas_call | solution.py:190
  106.7 1.0 copy.31.refs_7_
  107.9 1.3 add.57.refs_6_
  109.1 6.0 %shard_map.96 = (bf16[1024,128]{1,0:T(8,128)(2,1)}, bf16[4096,128]{1,0:T(8,128)(2,1)}, bf16[4096,128]{1,0:T(8,128)(2,1)}) custom-call(s32[9,2]{1,0:T(8,128)} %copy.25.refs_0_, s32[1]{0:T(128)} %bitcast.57.refs_1_, bf16[1024,128]{1,0:T(8,128)(2,1)} %bitcast.75, bf16[4096,128]{1,0:T(8,128)(2,1)} %get-tuple-element.21.refs_3_, ...), custom_call_target="tpu_custom_call" | custom-call | tf_op jit(solution)/shard_map/pallas_call | solution.py:132
  115.2 1.8 pad_maximum_fusion
  117.1 9.3 %collective-permute-start.1 = (bf16[32,64,256]{2,1,0:T(8,128)(2,1)S(1)}, bf16[32,64,256]{2,1,0:T(8,128)(2,1)}, u32[]{:S(2)}, u32[]{:S(2)}) collective-permute-start(bf16[32,64,256]{2,1,0:T(8,128)(2,1)S(1)} %dynamic-slice_bitcast_fusion), channel_id=1, source_target_pairs={{0,1},{1,0},{2,3},{3,2},{4,5},{5,4},{6,7},{7,6},{8,9},{9,8},{10,11... | collective-permute-start | bytes 3145736 | tf_op jit(solution)/shard_map/ppermute | solution.py:311
  126.3 2.4 %collective-permute-done.1 = bf16[32,64,256]{2,1,0:T(8,128)(2,1)} collective-permute-done((bf16[32,64,256]{2,1,0:T(8,128)(2,1)S(1)}, bf16[32,64,256]{2,1,0:T(8,128)(2,1)}, u32[]{:S(2)}, u32[]{:S(2)}) %collective-permute-start.1) | collective-permute-done | bytes 1048608 | tf_op jit(solution)/shard_map/ppermute | solution.py:311
  128.7 2.6 %fusion = bf16[32,64,256]{2,1,0:T(8,128)(2,1)} fusion(bf16[32,64,256]{2,1,0:T(8,128)(2,1)} %collective-permute-done.1, bf16[32,2,64,256]{3,2,1,0:T(8,128)(2,1)S(1)} %bitcast.59, s32[]{:T(128)S(6)} %select_n.22), kind=kLoop, calls=%fused_computation.3 | loop fusion | flops 2097152 | bytes 3145732 | tf_op jit(solution)/shard_map/convert_element_type | solution.py:311
  131.3 7.4 %all-to-all-start.1 = ((bf16[32,64,256]{2,1,0:T(8,128)(2,1)}), bf16[32,64,256]{2,1,0:T(8,128)(2,1)S(1)}, u32[]{:S(2)}, u32[]{:S(2)}) async-start(bf16[32,64,256]{2,1,0:T(8,128)(2,1)} %fusion), calls=%async_computation.1 | async-start | bytes 2097152 | tf_op jit(solution)/shard_map/all_to_all | solution.py:314
  138.8 21.7 %shard_map.97 = bf16[16,64,128]{2,1,0:T(8,128)(2,1)} custom-call(bf16[16,64,128]{2,1,0:T(8,128)(2,1)} %bitcast.80), custom_call_target="tpu_custom_call" | custom-call | tf_op jit(solution)/shard_map/pallas_call | solution.py:190
  160.5 1.6 reduce_sum.42.refs_0_
  162.1 23.0 %shard_map.98 = bf16[16,64,128]{2,1,0:T(8,128)(2,1)} custom-call(bf16[64,128]{1,0:T(8,128)(2,1)} %reduce_sum.42.refs_0_), custom_call_target="tpu_custom_call" | custom-call | tf_op jit(solution)/shard_map/pallas_call | solution.py:190
  (43 shorter events, 11.4 us)
Async XLA Ops:
  4.1 29.9 %copy-start.3 = (s32[1,1,9,2]{2,3,1,0:T(2,128)S(1)}, s32[1,1,9,2]{2,3,1,0:T(2,128)}, u32[]{:S(2)}) copy-start(s32[1,1,9,2]{2,3,1,0:T(2,128)} %param.10) | copy-start | bytes 220
  31.7 4.6 %collective-permute-start = (bf16[32,64,256]{2,1,0:T(8,128)(2,1)S(1)}, bf16[32,64,256]{2,1,0:T(8,128)(2,1)S(1)}, u32[]{:S(2)}, u32[]{:S(2)}) collective-permute-start(bf16[32,64,256]{2,1,0:T(8,128)(2,1)S(1)} %all_to_all.10), channel_id=1, source_target_pairs={{0,1},{1,0},{2,3},{3,2},{4,5},{5,4},{6,7},{7,6},{8,9},{9,8},{10,11... | collective-permute-start | bytes 3145736 | tf_op jit(solution)/shard_map/ppermute | solution.py:236
  45.8 60.7 %copy-start.2 = (bf16[1,1024,128]{2,1,0:T(8,128)(2,1)S(1)}, bf16[1,1024,128]{2,1,0:T(8,128)(2,1)}, u32[]{:S(2)}) copy-start(bf16[1,1024,128]{2,1,0:T(8,128)(2,1)} %param.9) | copy-start | bytes 786436
  105.7 9.5 %copy-start = (bf16[16,64,128]{2,1,0:T(8,128)(2,1)}, bf16[16,64,128]{2,1,0:T(8,128)(2,1)S(1)}, u32[]{:S(2)}) copy-start(bf16[16,64,128]{2,1,0:T(8,128)(2,1)S(1)} %slice.54) | copy-start | bytes 786436
  117.1 11.7 %collective-permute-start.1 = (bf16[32,64,256]{2,1,0:T(8,128)(2,1)S(1)}, bf16[32,64,256]{2,1,0:T(8,128)(2,1)}, u32[]{:S(2)}, u32[]{:S(2)}) collective-permute-start(bf16[32,64,256]{2,1,0:T(8,128)(2,1)S(1)} %dynamic-slice_bitcast_fusion), channel_id=1, source_target_pairs={{0,1},{1,0},{2,3},{3,2},{4,5},{5,4},{6,7},{7,6},{8,9},{9,8},{10,11... | collective-permute-start | bytes 3145736 | tf_op jit(solution)/shard_map/ppermute | solution.py:311
  131.3 53.9 %all-to-all-start.1 = ((bf16[32,64,256]{2,1,0:T(8,128)(2,1)}), bf16[32,64,256]{2,1,0:T(8,128)(2,1)S(1)}, u32[]{:S(2)}, u32[]{:S(2)}) async-start(bf16[32,64,256]{2,1,0:T(8,128)(2,1)} %fusion), calls=%async_computation.1 | async-start | bytes 2097152 | tf_op jit(solution)/shard_map/all_to_all | solution.py:314
  186.2 2.1 %copy-start.1 = (bf16[16,64,128]{2,1,0:T(8,128)(2,1)S(1)}, bf16[16,64,128]{2,1,0:T(8,128)(2,1)}, u32[]{:S(2)}) copy-start(bf16[16,64,128]{2,1,0:T(8,128)(2,1)} %shard_map.98) | copy-start | bytes 786436

commit v7 on v6

--- a/solution.py
+++ b/solution.py
@@ -197,6 +197,64 @@
     )(x)
 
 
+def reduce_kernel(x_ref, y_ref, part_ref, send_sem, recv_sem, back_send, back_recv):
+    groups = y_ref.shape[0]
+    me = lax.axis_index("grp")
+    lane = lax.axis_index("seq")
+    mesh_ids = pl.DeviceIdType.MESH
+    barrier = pltpu.get_barrier_semaphore()
+    for step in range(1, groups):
+        pl.semaphore_signal(
+            barrier, inc=1, device_id=(lax.rem(me + step, groups), lane), device_id_type=mesh_ids
+        )
+    pl.semaphore_wait(barrier, groups - 1)
+    copies = []
+    for step in range(1, groups):
+        target = lax.rem(me + step, groups)
+        copy = pltpu.make_async_remote_copy(
+            src_ref=x_ref.at[target],
+            dst_ref=part_ref.at[me],
+            send_sem=send_sem.at[step],
+            recv_sem=recv_sem.at[step],
+            device_id=(target, lane),
+            device_id_type=mesh_ids,
+        )
+        copy.start()
+        copies.append(copy)
+    part_ref[me] = x_ref[me]
+    for copy in copies:
+        copy.wait()
+    y_ref[me] = jnp.sum(part_ref[...].astype(jnp.float32), axis=0).astype(y_ref.dtype)
+    copies = []
+    for step in range(1, groups):
+        target = lax.rem(me + step, groups)
+        copy = pltpu.make_async_remote_copy(
+            src_ref=y_ref.at[me],
+            dst_ref=y_ref.at[me],
+            send_sem=back_send.at[step],
+            recv_sem=back_recv.at[step],
+            device_id=(target, lane),
+            device_id_type=mesh_ids,
+        )
+        copy.start()
+        copies.append(copy)
+    for copy in copies:
+        copy.wait()
+
+
+def grp_reduce(x, groups, collective):
+    vmem = pl.BlockSpec(memory_space=pltpu.VMEM)
+    sems = pltpu.SemaphoreType.DMA((groups,))
+    return pl.pallas_call(
+        reduce_kernel,
+        out_shape=jax.ShapeDtypeStruct(x.shape, x.dtype),
+        in_specs=[vmem],
+        out_specs=vmem,
+        scratch_shapes=[pltpu.VMEM(x.shape, x.dtype), sems, sems, sems, sems],
+        compiler_params=pltpu.CompilerParams(collective_id=collective, has_side_effects=True),
+    )(x)
+
+
 def scatter_rows(rows, parts, collective):
     return grp_exchange(
         rows.reshape(parts, rows.shape[0] // parts, rows.shape[1]), parts, False, collective
@@ -316,9 +374,9 @@
     both_back = both_back.reshape(scene_here, heads_total, 2, head_width)
     grad_keys = both_back[:, :, 0, :].reshape(scene_here, -1)
     grad_values = both_back[:, :, 1, :].reshape(scene_here, -1)
-    query_parts = scatter_rows(query_grad, groups, 2)
-    query_chunk = jnp.sum(query_parts.astype(jnp.float32), axis=0).astype(jnp.bfloat16)
-    grad_queries = broadcast_rows(query_chunk, groups, 3).reshape(1, query_rows, head_width)
+    grad_queries = grp_reduce(
+        query_grad.reshape(groups, chunk_rows, head_width), groups, 2
+    ).reshape(1, query_rows, head_width)
     return (attended, grad_queries, grad_keys, grad_values)
 
 

time: 192 us -> 183 us (0.953)
  Pallas kernels: 110 us -> 106 us
  starting transfers between devices: 19 us -> 16.8 us
    pallas_call x4 -> x2, Pallas kernels: 98.9 us -> 51.3 us  [grp_exchange(): pl.pallas_call(lambda *refs: exchange_kernel(broadcast, *refs), out_shape...]
    pallas_call x0 -> x1, Pallas kernels: none -> 43.9 us  [grp_reduce(): pl.pallas_call(reduce_kernel, out_shape=jax.ShapeDtypeStruct(x.shape, x.d...]
    ppermute x1, starting transfers between devices: 9.28 us -> 7.24 us  [per_device(): lax.ppermute(given, 'seq', pairs).astype(jnp.float32)]
  transfers between devices with their start and end apart: 3 -> 3, of which waited for: 2 -> 2; matrix products, arithmetic and copies ran while one was open for 1% -> 0% of each run, Pallas kernels for 24% -> 24%
where the time goes in v7:
time: 183 us; the launch traced here: 181 us
  Pallas kernels  106 us (58%)
  blocking collectives  26.8 us (15%)
  local copies, waits for them, and re-layouts  16.8 us (9%)
  starting transfers between devices  16.8 us (9%)
  other arithmetic  9.81 us (5%)
  waiting for transfers between devices  3.3 us (2%)
    pallas_call x2, Pallas kernels, grp_exchange(): pl.pallas_call(lambda *refs: exchange_kernel(broadcast, *refs), out_shape...  51.3 us
    pallas_call x1, Pallas kernels, grp_reduce(): pl.pallas_call(reduce_kernel, out_shape=jax.ShapeDtypeStruct(x.shape, x.d...  43.9 us
    all_to_all x1, blocking collectives, per_device(): lax.all_to_all(both_here.reshape(seq_devices, half_keys, 2 * head_width),...  26.8 us
    all_to_all x1, starting transfers between devices, per_device(): both_back = lax.all_to_all(summed, 'seq', 0, 0, tiled=True)  7.26 us
    ppermute x1, starting transfers between devices, per_device(): lax.ppermute(given, 'seq', pairs).astype(jnp.float32)  7.24 us
    pallas_call x1, Pallas kernels, backward_item(): pl.pallas_call(lambda *refs: backward_kernel(softmax_scale, *refs), out_s...  6.03 us
    pallas_call x1, Pallas kernels, forward_item(): pl.pallas_call(lambda *refs: forward_kernel(softmax_scale, *refs), out_sh...  5.05 us
    unnamed x13, local copies, waits for them, and re-layouts  4.88 us
  transfers between devices with their start and end apart: 3, of which 2 were waited for; matrix products, arithmetic and copies ran while one was open for 0% of the time, Pallas kernels for 24%

profile of v7, /device:TPU:1, one launch (start us, length us, event | category | flops | bytes accessed | tf_op | source)
XLA Modules:
  0.0 181.3 jit_solution(9585689801781084125)
XLA Ops:
  0.6 1.1 copy.34
  1.8 1.1 copy.35
  3.0 1.1 copy.24
  4.9 26.8 %all_to_all.10 = bf16[32,64,256]{2,1,0:T(8,128)(2,1)S(1)} all-to-all(bf16[32,64,256]{2,1,0:T(8,128)(2,1)S(1)} %reshape.122), channel_id=1, replica_groups=mesh['grp'=16,'seq'=32] {'seq'}, dimensions={0} | all-to-all | bytes 2097152 | tf_op jit(solution)/shard_map/all_to_all | solution.py:290
  31.7 2.3 %collective-permute-start = (bf16[32,64,256]{2,1,0:T(8,128)(2,1)S(1)}, bf16[32,64,256]{2,1,0:T(8,128)(2,1)S(1)}, u32[]{:S(2)}, u32[]{:S(2)}) collective-permute-start(bf16[32,64,256]{2,1,0:T(8,128)(2,1)S(1)} %all_to_all.10), channel_id=1, source_target_pairs={{0,1},{1,0},{2,3},{3,2},{4,5},{5,4},{6,7},{7,6},{8,9},{9,8},{10,11... | collective-permute-start | bytes 3145736 | tf_op jit(solution)/shard_map/ppermute | solution.py:294
  36.5 1.5 fusion.6
  37.9 5.1 %shard_map.93 = (f32[1024,128]{1,0:T(8,128)}, f32[1024,128]{1,0:T(8,128)}, f32[1024,128]{1,0:T(8,128)}) custom-call(s32[9,2]{1,0:T(8,128)} %copy.25.refs_0_, s32[1]{0:T(128)} %bitcast.56.refs_1_, bf16[1024,128]{1,0:T(8,128)(2,1)} %bitcast.74, bf16[4096,128]{1,0:T(8,128)(2,1)} %get-tuple-element.21.refs_3_, bf16[4096,128]{1,0:T(8,128)(2,1)} %get-tuple-element.20.refs_4_), custom_call_target="tpu_custom_call" | custom-call | tf_op jit(solution)/shard_map/pallas_call | solution.py:65
  43.0 1.2 slice_reduce_fusion
  44.3 1.3 fusion.2
  45.8 1.1 convert_element_type.68
  47.6 32.3 %shard_map.94 = bf16[16,66,128]{2,1,0:T(8,128)(2,1)} custom-call(bf16[16,66,128]{2,1,0:T(8,128)(2,1)} %pad_maximum_fusion.1.refs_0_), custom_call_target="tpu_custom_call" | custom-call | tf_op jit(solution)/shard_map/pallas_call | solution.py:190
  79.9 1.0 convert_element_type.73
  82.8 19.0 %shard_map.95 = bf16[16,66,128]{2,1,0:T(8,128)(2,1)} custom-call(bf16[66,128]{1,0:T(8,128)(2,1)} %pad_maximum_fusion.2.refs_0_), custom_call_target="tpu_custom_call" | custom-call | tf_op jit(solution)/shard_map/pallas_call | solution.py:190
  101.9 1.0 slice.54
  103.9 1.0 copy.31.refs_7_
  105.0 1.3 add.57.refs_6_
  106.3 6.0 %shard_map.96 = (bf16[1024,128]{1,0:T(8,128)(2,1)}, bf16[4096,128]{1,0:T(8,128)(2,1)}, bf16[4096,128]{1,0:T(8,128)(2,1)}) custom-call(s32[9,2]{1,0:T(8,128)} %copy.25.refs_0_, s32[1]{0:T(128)} %bitcast.57.refs_1_, bf16[1024,128]{1,0:T(8,128)(2,1)} %bitcast.75, bf16[4096,128]{1,0:T(8,128)(2,1)} %get-tuple-element.21.refs_3_, ...), custom_call_target="tpu_custom_call" | custom-call | tf_op jit(solution)/shard_map/pallas_call | solution.py:132
  112.3 1.8 pad_maximum_fusion
  114.2 7.2 %collective-permute-start.1 = (bf16[32,64,256]{2,1,0:T(8,128)(2,1)S(1)}, bf16[32,64,256]{2,1,0:T(8,128)(2,1)}, u32[]{:S(2)}, u32[]{:S(2)}) collective-permute-start(bf16[32,64,256]{2,1,0:T(8,128)(2,1)S(1)} %dynamic-slice_bitcast_fusion), channel_id=1, source_target_pairs={{0,1},{1,0},{2,3},{3,2},{4,5},{5,4},{6,7},{7,6},{8,9},{9,8},{10,11... | collective-permute-start | bytes 3145736 | tf_op jit(solution)/shard_map/ppermute | solution.py:369
  121.4 2.4 %collective-permute-done.1 = bf16[32,64,256]{2,1,0:T(8,128)(2,1)} collective-permute-done((bf16[32,64,256]{2,1,0:T(8,128)(2,1)S(1)}, bf16[32,64,256]{2,1,0:T(8,128)(2,1)}, u32[]{:S(2)}, u32[]{:S(2)}) %collective-permute-start.1) | collective-permute-done | bytes 1048608 | tf_op jit(solution)/shard_map/ppermute | solution.py:369
  123.8 2.6 %fusion = bf16[32,64,256]{2,1,0:T(8,128)(2,1)} fusion(bf16[32,64,256]{2,1,0:T(8,128)(2,1)} %collective-permute-done.1, bf16[32,2,64,256]{3,2,1,0:T(8,128)(2,1)S(1)} %bitcast.59, s32[]{:T(128)S(6)} %select_n.22), kind=kLoop, calls=%fused_computation.3 | loop fusion | flops 2097152 | bytes 3145732 | tf_op jit(solution)/shard_map/convert_element_type | solution.py:369
  126.4 7.3 %all-to-all-start.1 = ((bf16[32,64,256]{2,1,0:T(8,128)(2,1)}), bf16[32,64,256]{2,1,0:T(8,128)(2,1)S(1)}, u32[]{:S(2)}, u32[]{:S(2)}) async-start(bf16[32,64,256]{2,1,0:T(8,128)(2,1)} %fusion), calls=%async_computation.1 | async-start | bytes 2097152 | tf_op jit(solution)/shard_map/all_to_all | solution.py:372
  133.7 43.9 %shard_map.97 = bf16[16,64,128]{2,1,0:T(8,128)(2,1)} custom-call(bf16[16,64,128]{2,1,0:T(8,128)(2,1)} %bitcast.80), custom_call_target="tpu_custom_call" | custom-call | tf_op jit(solution)/shard_map/pallas_call | solution.py:248
  178.7 0.9 copy.40
  (41 shorter events, 9.5 us)
Async XLA Ops:
  4.1 29.9 %copy-start.3 = (s32[1,1,9,2]{2,3,1,0:T(2,128)S(1)}, s32[1,1,9,2]{2,3,1,0:T(2,128)}, u32[]{:S(2)}) copy-start(s32[1,1,9,2]{2,3,1,0:T(2,128)} %param.10) | copy-start | bytes 220
  31.7 4.6 %collective-permute-start = (bf16[32,64,256]{2,1,0:T(8,128)(2,1)S(1)}, bf16[32,64,256]{2,1,0:T(8,128)(2,1)S(1)}, u32[]{:S(2)}, u32[]{:S(2)}) collective-permute-start(bf16[32,64,256]{2,1,0:T(8,128)(2,1)S(1)} %all_to_all.10), channel_id=1, source_target_pairs={{0,1},{1,0},{2,3},{3,2},{4,5},{5,4},{6,7},{7,6},{8,9},{9,8},{10,11... | collective-permute-start | bytes 3145736 | tf_op jit(solution)/shard_map/ppermute | solution.py:294
  45.8 57.9 %copy-start.2 = (bf16[1,1024,128]{2,1,0:T(8,128)(2,1)S(1)}, bf16[1,1024,128]{2,1,0:T(8,128)(2,1)}, u32[]{:S(2)}) copy-start(bf16[1,1024,128]{2,1,0:T(8,128)(2,1)} %param.9) | copy-start | bytes 786436
  102.8 9.5 %copy-start = (bf16[16,64,128]{2,1,0:T(8,128)(2,1)}, bf16[16,64,128]{2,1,0:T(8,128)(2,1)S(1)}, u32[]{:S(2)}) copy-start(bf16[16,64,128]{2,1,0:T(8,128)(2,1)S(1)} %slice.54) | copy-start | bytes 786436
  114.2 9.6 %collective-permute-start.1 = (bf16[32,64,256]{2,1,0:T(8,128)(2,1)S(1)}, bf16[32,64,256]{2,1,0:T(8,128)(2,1)}, u32[]{:S(2)}, u32[]{:S(2)}) collective-permute-start(bf16[32,64,256]{2,1,0:T(8,128)(2,1)S(1)} %dynamic-slice_bitcast_fusion), channel_id=1, source_target_pairs={{0,1},{1,0},{2,3},{3,2},{4,5},{5,4},{6,7},{7,6},{8,9},{9,8},{10,11... | collective-permute-start | bytes 3145736 | tf_op jit(solution)/shard_map/ppermute | solution.py:369
  126.4 51.1 %all-to-all-start.1 = ((bf16[32,64,256]{2,1,0:T(8,128)(2,1)}), bf16[32,64,256]{2,1,0:T(8,128)(2,1)S(1)}, u32[]{:S(2)}, u32[]{:S(2)}) async-start(bf16[32,64,256]{2,1,0:T(8,128)(2,1)} %fusion), calls=%async_computation.1 | async-start | bytes 2097152 | tf_op jit(solution)/shard_map/all_to_all | solution.py:372
  178.5 2.1 %copy-start.1 = (bf16[16,64,128]{2,1,0:T(8,128)(2,1)S(1)}, bf16[16,64,128]{2,1,0:T(8,128)(2,1)}, u32[]{:S(2)}) copy-start(bf16[16,64,128]{2,1,0:T(8,128)(2,1)} %shard_map.97) | copy-start | bytes 786436

commit v8 on v7

--- a/solution.py
+++ b/solution.py
@@ -255,6 +255,94 @@
     )(x)
 
 
+def combine_kernel(
+    acc_in, stats_in, out_ref, stats_out, acc_part, stats_part,
+    send_acc, recv_acc, send_stats, recv_stats, back_send, back_recv, stat_send, stat_recv,
+):
+    groups, chunk_rows, head_width = out_ref.shape
+    me = lax.axis_index("grp")
+    lane = lax.axis_index("seq")
+    mesh_ids = pl.DeviceIdType.MESH
+    barrier = pltpu.get_barrier_semaphore()
+    for step in range(1, groups):
+        pl.semaphore_signal(
+            barrier, inc=1, device_id=(lax.rem(me + step, groups), lane), device_id_type=mesh_ids
+        )
+    pl.semaphore_wait(barrier, groups - 1)
+    copies = []
+    for step in range(1, groups):
+        target = lax.rem(me + step, groups)
+        for source, landing, sent, got in (
+            (acc_in, acc_part, send_acc, recv_acc),
+            (stats_in, stats_part, send_stats, recv_stats),
+        ):
+            copy = pltpu.make_async_remote_copy(
+                src_ref=source.at[target],
+                dst_ref=landing.at[me],
+                send_sem=sent.at[step],
+                recv_sem=got.at[step],
+                device_id=(target, lane),
+                device_id_type=mesh_ids,
+            )
+            copy.start()
+            copies.append(copy)
+    acc_part[me] = acc_in[me]
+    stats_part[me] = stats_in[me]
+    for copy in copies:
+        copy.wait()
+    columns = jnp.transpose(stats_part[...].reshape(groups * 8, 128))
+    maxima = [columns[:chunk_rows, 8 * g : 8 * g + 1] for g in range(groups)]
+    totals = [columns[chunk_rows:, 8 * g : 8 * g + 1] for g in range(groups)]
+    top = maxima[0]
+    for g in range(1, groups):
+        top = jnp.maximum(top, maxima[g])
+    row_total = jnp.zeros_like(top)
+    row_accum = jnp.zeros((chunk_rows, head_width), jnp.float32)
+    for g in range(groups):
+        shrink = jnp.exp(maxima[g] - top)
+        row_total = row_total + totals[g] * shrink
+        row_accum = row_accum + acc_part[g].astype(jnp.float32) * shrink
+    out_ref[me] = (row_accum / row_total).astype(out_ref.dtype)
+    spread = jnp.concatenate(
+        [jnp.broadcast_to(top, (chunk_rows, 128)), jnp.broadcast_to(row_total, (chunk_rows, 128))], axis=0
+    )
+    stats_out[me] = jnp.transpose(spread)[:8, :]
+    copies = []
+    for step in range(1, groups):
+        target = lax.rem(me + step, groups)
+        for source, sent, got in ((out_ref, back_send, back_recv), (stats_out, stat_send, stat_recv)):
+            copy = pltpu.make_async_remote_copy(
+                src_ref=source.at[me],
+                dst_ref=source.at[me],
+                send_sem=sent.at[step],
+                recv_sem=got.at[step],
+                device_id=(target, lane),
+                device_id_type=mesh_ids,
+            )
+            copy.start()
+            copies.append(copy)
+    for copy in copies:
+        copy.wait()
+
+
+def grp_combine(accum, stats, collective):
+    groups = accum.shape[0]
+    vmem = pl.BlockSpec(memory_space=pltpu.VMEM)
+    sems = pltpu.SemaphoreType.DMA((groups,))
+    return pl.pallas_call(
+        combine_kernel,
+        out_shape=(
+            jax.ShapeDtypeStruct(accum.shape, accum.dtype),
+            jax.ShapeDtypeStruct(stats.shape, stats.dtype),
+        ),
+        in_specs=[vmem, vmem],
+        out_specs=(vmem, vmem),
+        scratch_shapes=[pltpu.VMEM(accum.shape, accum.dtype), pltpu.VMEM(stats.shape, stats.dtype)]
+        + [sems] * 8,
+        compiler_params=pltpu.CompilerParams(collective_id=collective, has_side_effects=True),
+    )(accum, stats)
+
+
 def scatter_rows(rows, parts, collective):
     return grp_exchange(
         rows.reshape(parts, rows.shape[0] // parts, rows.shape[1]), parts, False, collective
@@ -306,48 +394,16 @@
         tile_counts[0, 0],
         softmax_scale,
     )
-    total_hi = part_total.astype(jnp.bfloat16)
-    total_lo = (part_total - total_hi.astype(jnp.float32)).astype(jnp.bfloat16)
-    stats = jnp.stack(
-        [
-            jnp.concatenate(
-                [part_max.astype(jnp.bfloat16).reshape(groups, chunk_rows), total_hi.reshape(groups, chunk_rows)],
-                axis=1,
-            ),
-            jnp.concatenate(
-                [total_lo.reshape(groups, chunk_rows), jnp.zeros((groups, chunk_rows), jnp.bfloat16)],
-                axis=1,
-            ),
-        ],
-        axis=1,
-    )
-    packed = jnp.concatenate(
-        [part_accum.astype(jnp.bfloat16).reshape(groups, chunk_rows, head_width), stats], axis=1
-    )
-    arrived = scatter_rows(packed.reshape(groups * (chunk_rows + 2), head_width), groups, 0)
-    arrived = arrived.reshape(groups, chunk_rows + 2, head_width).astype(jnp.float32)
-    got_accum = arrived[:, :chunk_rows, :]
-    got_max = arrived[:, chunk_rows, :chunk_rows]
-    got_total = arrived[:, chunk_rows, chunk_rows:] + arrived[:, chunk_rows + 1, :chunk_rows]
-    top = jnp.max(got_max, axis=0)
-    shrink = jnp.exp(got_max - top[None, :])
-    chunk_total = jnp.sum(got_total * shrink, axis=0)
-    chunk_accum = jnp.sum(got_accum * shrink[:, :, None], axis=0)
-    chunk_out = (chunk_accum / chunk_total[:, None]).astype(jnp.bfloat16)
-    chunk_hi = chunk_total.astype(jnp.bfloat16)
-    chunk_lo = (chunk_total - chunk_hi.astype(jnp.float32)).astype(jnp.bfloat16)
-    chunk_stats = jnp.stack(
-        [
-            jnp.concatenate([top.astype(jnp.bfloat16), chunk_hi]),
-            jnp.concatenate([chunk_lo, jnp.zeros((chunk_rows,), jnp.bfloat16)]),
-        ]
-    )
-    back = broadcast_rows(jnp.concatenate([chunk_out, chunk_stats], axis=0), groups, 1)
-    back = back.reshape(groups, chunk_rows + 2, head_width)
-    attended = back[:, :chunk_rows, :].reshape(1, query_rows, head_width)
-    back_stats = back[:, chunk_rows:, :].astype(jnp.float32)
-    row_top = back_stats[:, 0, :chunk_rows].reshape(1, query_rows)
-    row_total = (back_stats[:, 0, chunk_rows:] + back_stats[:, 1, :chunk_rows]).reshape(1, query_rows)
+    stats = jnp.concatenate(
+        [part_max.reshape(groups, 1, chunk_rows), part_total.reshape(groups, 1, chunk_rows)], axis=2
+    )
+    stats = jnp.concatenate([stats, jnp.zeros((groups, 7, 2 * chunk_rows), jnp.float32)], axis=1)
+    out_rows, out_stats = grp_combine(
+        part_accum.astype(jnp.bfloat16).reshape(groups, chunk_rows, head_width), stats, 0
+    )
+    attended = out_rows.reshape(1, query_rows, head_width)
+    row_top = out_stats[:, 0, :chunk_rows].reshape(1, query_rows)
+    row_total = out_stats[:, 0, chunk_rows:].reshape(1, query_rows)
     log_total = row_top + jnp.log(row_total)
     deltas = jnp.sum(attended.astype(jnp.float32) * grad_output.astype(jnp.float32), axis=2)
     query_grad, key_grad, value_grad = backward_item(

time: 183 us -> 176 us (0.962)
  starting transfers between devices: 16.8 us -> 12.1 us
  local copies, waits for them, and re-layouts: 16.8 us -> 14.8 us
    pallas_call x1, Pallas kernels: 43.9 us -> 37.9 us  [grp_reduce(): pl.pallas_call(reduce_kernel, out_shape=jax.ShapeDtypeStruct(x.shape, x.d...]
    ppermute x1, starting transfers between devices: 7.24 us -> 1.92 us  [per_device(): lax.ppermute(given, 'seq', pairs).astype(jnp.float32)]
    pallas_call x1, Pallas kernels: 5.05 us -> 8.34 us  [forward_item(): pl.pallas_call(lambda *refs: forward_kernel(softmax_scale, *refs), out_sh...]
    pallas_call x1, Pallas kernels: 6.03 us -> 9.31 us  [backward_item(): pl.pallas_call(lambda *refs: backward_kernel(softmax_scale, *refs), out_s...]
    convert_element_type x6 -> x0, other arithmetic: 1.89 us -> none  [the longest x1 1 us: per_device(): arrived.reshape(groups, chunk_rows + 2, head_width).astype(jnp.float32)]
    unnamed x13 -> x14, local copies, waits for them, and re-layouts: 4.88 us -> 5.57 us
    pallas_call x2 -> x1, Pallas kernels: 51.3 us -> 51.8 us  [grp_combine(): pl.pallas_call(combine_kernel, out_shape=(jax.ShapeDtypeStruct(accum.shap...]
  transfers between devices with their start and end apart: 3 -> 3, of which waited for: 2 -> 2; matrix products, arithmetic and copies ran while one was open for 0% -> 0% of each run, Pallas kernels for 24% -> 22%
where the time goes in v8:
time: 176 us
  Pallas kernels  107 us (61%)
  blocking collectives  26.8 us (15%)
  local copies, waits for them, and re-layouts  14.8 us (8%)
  starting transfers between devices  12.1 us (7%)
  other arithmetic  9.29 us (5%)
  waiting for transfers between devices  3.66 us (2%)
    pallas_call x1, Pallas kernels, grp_combine(): pl.pallas_call(combine_kernel, out_shape=(jax.ShapeDtypeStruct(accum.shap...  51.8 us
    pallas_call x1, Pallas kernels, grp_reduce(): pl.pallas_call(reduce_kernel, out_shape=jax.ShapeDtypeStruct(x.shape, x.d...  37.9 us
    all_to_all x1, blocking collectives, per_device(): lax.all_to_all(both_here.reshape(seq_devices, half_keys, 2 * head_width),...  26.8 us
    pallas_call x1, Pallas kernels, backward_item(): pl.pallas_call(lambda *refs: backward_kernel(softmax_scale, *refs), out_s...  9.31 us
    pallas_call x1, Pallas kernels, forward_item(): pl.pallas_call(lambda *refs: forward_kernel(softmax_scale, *refs), out_sh...  8.34 us
    all_to_all x1, starting transfers between devices, per_device(): both_back = lax.all_to_all(summed, 'seq', 0, 0, tiled=True)  7.92 us
    unnamed x14, local copies, waits for them, and re-layouts  5.57 us
  transfers between devices with their start and end apart: 3, of which 2 were waited for; matrix products, arithmetic and copies ran while one was open for 0% of the time, Pallas kernels for 22%

profile of v8, /device:TPU:1, one launch (start us, length us, event | category | flops | bytes accessed | tf_op | source)
XLA Modules:
  0.0 175.6 jit_solution(8318989098461050812)
XLA Ops:
  0.6 1.1 copy.22
  1.8 1.1 copy.23
  3.0 1.1 copy.14
  4.9 26.8 %all_to_all.10 = bf16[32,64,256]{2,1,0:T(8,128)(2,1)S(1)} all-to-all(bf16[32,64,256]{2,1,0:T(8,128)(2,1)S(1)} %reshape.81), channel_id=1, replica_groups=mesh['grp'=16,'seq'=32] {'seq'}, dimensions={0} | all-to-all | bytes 2097152 | tf_op jit(solution)/shard_map/all_to_all | solution.py:378
  31.7 2.3 %collective-permute-start = (bf16[32,64,256]{2,1,0:T(8,128)(2,1)S(1)}, bf16[32,64,256]{2,1,0:T(8,128)(2,1)S(1)}, u32[]{:S(2)}, u32[]{:S(2)}) collective-permute-start(bf16[32,64,256]{2,1,0:T(8,128)(2,1)S(1)} %all_to_all.10), channel_id=1, source_target_pairs={{0,1},{1,0},{2,3},{3,2},{4,5},{5,4},{6,7},{7,6},{8,9},{9,8},{10,11... | collective-permute-start | bytes 3145736 | tf_op jit(solution)/shard_map/ppermute | solution.py:382
  35.3 0.9 collective-permute-done
  36.4 1.5 fusion.1
  37.9 8.3 %shard_map.93 = (f32[1024,128]{1,0:T(8,128)}, f32[1024,128]{1,0:T(8,128)}, f32[1024,128]{1,0:T(8,128)}) custom-call(s32[9,2]{1,0:T(8,128)} %copy.15.refs_0_, s32[1]{0:T(128)} %bitcast.46.refs_1_, bf16[1024,128]{1,0:T(8,128)(2,1)} %bitcast.64, bf16[4096,128]{1,0:T(8,128)(2,1)} %get-tuple-element.21.refs_3_, bf16[4096,128]{1,0:T(8,128)(2,1)} %get-tuple-element.20.refs_4_), custom_call_target="tpu_custom_call" | custom-call | tf_op jit(solution)/shard_map/pallas_call | solution.py:65
  46.3 1.5 slice_reduce_fusion
  48.0 1.8 %convert_element_type.29 = bf16[1024,128]{1,0:T(8,128)(2,1)} convert(f32[1024,128]{1,0:T(8,128)} %get-tuple-element.12) | non-fusion elementwise | flops 131072 | bytes 786432 | tf_op jit(solution)/shard_map/convert_element_type | solution.py:402
  50.4 51.8 %shard_map.94 = (bf16[16,64,128]{2,1,0:T(8,128)(2,1)}, f32[16,8,128]{2,1,0:T(8,128)}) custom-call(bf16[16,64,128]{2,1,0:T(8,128)(2,1)} %bitcast.59, f32[16,8,128]{2,1,0:T(8,128)} %select_maximum_fusion.stats_in), custom_call_target="tpu_custom_call" | custom-call | tf_op jit(solution)/shard_map/pallas_call | solution.py:332
  102.3 1.0 add_reduce_fusion
  103.3 1.3 add.33.refs_6_
  104.6 1.2 multiply_reduce_fusion
  105.8 1.0 copy.20.refs_7_
  106.8 9.3 %shard_map.95 = (bf16[1024,128]{1,0:T(8,128)(2,1)}, bf16[4096,128]{1,0:T(8,128)(2,1)}, bf16[4096,128]{1,0:T(8,128)(2,1)}) custom-call(s32[9,2]{1,0:T(8,128)} %copy.15.refs_0_, s32[1]{0:T(128)} %bitcast.47.refs_1_, bf16[1024,128]{1,0:T(8,128)(2,1)} %bitcast.65, bf16[4096,128]{1,0:T(8,128)(2,1)} %get-tuple-element.21.refs_3_, ...), custom_call_target="tpu_custom_call" | custom-call | tf_op jit(solution)/shard_map/pallas_call | solution.py:132
  116.1 1.8 %pad_maximum_fusion = bf16[4096,256]{1,0:T(8,128)(2,1)S(1)} fusion(bf16[4096,128]{1,0:T(8,128)(2,1)} %get-tuple-element.19, bf16[4096,128]{1,0:T(8,128)(2,1)} %get-tuple-element.18), kind=kLoop, calls=%fused_computation.1 | loop fusion | flops 4194304 | bytes 4194304 | tf_op jit(solution)/shard_map/concatenate | solution.py:420
  118.0 1.9 %collective-permute-start.1 = (bf16[32,64,256]{2,1,0:T(8,128)(2,1)S(1)}, bf16[32,64,256]{2,1,0:T(8,128)(2,1)}, u32[]{:S(2)}, u32[]{:S(2)}) collective-permute-start(bf16[32,64,256]{2,1,0:T(8,128)(2,1)S(1)} %dynamic-slice_bitcast_fusion), channel_id=1, source_target_pairs={{0,1},{1,0},{2,3},{3,2},{4,5},{5,4},{6,7},{7,6},{8,9},{9,8},{10,11... | collective-permute-start | bytes 3145736 | tf_op jit(solution)/shard_map/ppermute | solution.py:425
  119.9 2.8 %collective-permute-done.1 = bf16[32,64,256]{2,1,0:T(8,128)(2,1)} collective-permute-done((bf16[32,64,256]{2,1,0:T(8,128)(2,1)S(1)}, bf16[32,64,256]{2,1,0:T(8,128)(2,1)}, u32[]{:S(2)}, u32[]{:S(2)}) %collective-permute-start.1) | collective-permute-done | bytes 1048608 | tf_op jit(solution)/shard_map/ppermute | solution.py:425
  122.7 2.6 %fusion = bf16[32,64,256]{2,1,0:T(8,128)(2,1)} fusion(bf16[32,64,256]{2,1,0:T(8,128)(2,1)} %collective-permute-done.1, bf16[32,2,64,256]{3,2,1,0:T(8,128)(2,1)S(1)} %bitcast.49, s32[]{:T(128)S(6)} %select_n.22), kind=kLoop, calls=%fused_computation.3 | loop fusion | flops 2097152 | bytes 3145732 | tf_op jit(solution)/shard_map/convert_element_type | solution.py:425
  125.2 7.9 %all-to-all-start.1 = ((bf16[32,64,256]{2,1,0:T(8,128)(2,1)}), bf16[32,64,256]{2,1,0:T(8,128)(2,1)S(1)}, u32[]{:S(2)}, u32[]{:S(2)}) async-start(bf16[32,64,256]{2,1,0:T(8,128)(2,1)} %fusion), calls=%async_computation.1 | async-start | bytes 2097152 | tf_op jit(solution)/shard_map/all_to_all | solution.py:428
  133.2 37.9 %shard_map.96 = bf16[16,64,128]{2,1,0:T(8,128)(2,1)} custom-call(bf16[16,64,128]{2,1,0:T(8,128)(2,1)} %bitcast.70), custom_call_target="tpu_custom_call" | custom-call | tf_op jit(solution)/shard_map/pallas_call | solution.py:248
  172.3 0.9 copy.28
  173.2 0.9 copy.29
  (22 shorter events, 5.2 us)
Async XLA Ops:
  4.1 29.9 %copy-start.3 = (s32[1,1,9,2]{2,3,1,0:T(2,128)S(1)}, s32[1,1,9,2]{2,3,1,0:T(2,128)}, u32[]{:S(2)}) copy-start(s32[1,1,9,2]{2,3,1,0:T(2,128)} %param.10) | copy-start | bytes 220
  31.7 4.6 %collective-permute-start = (bf16[32,64,256]{2,1,0:T(8,128)(2,1)S(1)}, bf16[32,64,256]{2,1,0:T(8,128)(2,1)S(1)}, u32[]{:S(2)}, u32[]{:S(2)}) collective-permute-start(bf16[32,64,256]{2,1,0:T(8,128)(2,1)S(1)} %all_to_all.10), channel_id=1, source_target_pairs={{0,1},{1,0},{2,3},{3,2},{4,5},{5,4},{6,7},{7,6},{8,9},{9,8},{10,11... | collective-permute-start | bytes 3145736 | tf_op jit(solution)/shard_map/ppermute | solution.py:382
  37.9 66.7 %copy-start.2 = (bf16[1,1024,128]{2,1,0:T(8,128)(2,1)S(1)}, bf16[1,1024,128]{2,1,0:T(8,128)(2,1)}, u32[]{:S(2)}) copy-start(bf16[1,1024,128]{2,1,0:T(8,128)(2,1)} %param.9) | copy-start | bytes 786436
  118.0 4.7 %collective-permute-start.1 = (bf16[32,64,256]{2,1,0:T(8,128)(2,1)S(1)}, bf16[32,64,256]{2,1,0:T(8,128)(2,1)}, u32[]{:S(2)}, u32[]{:S(2)}) collective-permute-start(bf16[32,64,256]{2,1,0:T(8,128)(2,1)S(1)} %dynamic-slice_bitcast_fusion), channel_id=1, source_target_pairs={{0,1},{1,0},{2,3},{3,2},{4,5},{5,4},{6,7},{7,6},{8,9},{9,8},{10,11... | collective-permute-start | bytes 3145736 | tf_op jit(solution)/shard_map/ppermute | solution.py:425
  125.2 45.8 %all-to-all-start.1 = ((bf16[32,64,256]{2,1,0:T(8,128)(2,1)}), bf16[32,64,256]{2,1,0:T(8,128)(2,1)S(1)}, u32[]{:S(2)}, u32[]{:S(2)}) async-start(bf16[32,64,256]{2,1,0:T(8,128)(2,1)} %fusion), calls=%async_computation.1 | async-start | bytes 2097152 | tf_op jit(solution)/shard_map/all_to_all | solution.py:428
  172.1 2.1 %copy-start = (bf16[16,64,128]{2,1,0:T(8,128)(2,1)S(1)}, bf16[16,64,128]{2,1,0:T(8,128)(2,1)}, u32[]{:S(2)}) copy-start(bf16[16,64,128]{2,1,0:T(8,128)(2,1)} %get-tuple-element.15) | copy-start | bytes 786436
  172.1 2.8 %copy-start.1 = (bf16[16,64,128]{2,1,0:T(8,128)(2,1)S(1)}, bf16[16,64,128]{2,1,0:T(8,128)(2,1)}, u32[]{:S(2)}) copy-start(bf16[16,64,128]{2,1,0:T(8,128)(2,1)} %shard_map.96) | copy-start | bytes 786436

commit v9 on v8

--- a/solution.py
+++ b/solution.py
@@ -25,7 +25,9 @@
     )
 
 
-def forward_kernel(softmax_scale, list_ref, count_ref, q_ref, k_ref, v_ref, max_ref, total_ref, accum_ref):
+def forward_kernel(
+    softmax_scale, list_ref, count_ref, q_ref, k_ref, v_ref, acc_out, stats_out, max_ref, total_ref, accum_ref
+):
     max_ref[...] = jnp.full(max_ref.shape, NEG_START, jnp.float32)
     total_ref[...] = jnp.zeros(total_ref.shape, jnp.float32)
     accum_ref[...] = jnp.zeros(accum_ref.shape, jnp.float32)
@@ -55,26 +57,47 @@
         return carry
 
     lax.fori_loop(0, live_tiles, visit, 0)
-
-
-def forward_item(query_item, key_head, value_head, listing, live_tiles, softmax_scale):
+    groups, chunk_rows = acc_out.shape[0], acc_out.shape[1]
+    for g in range(groups):
+        rows = pl.ds(g * chunk_rows, chunk_rows)
+        acc_out[g] = accum_ref[rows, :].astype(acc_out.dtype)
+        stacked = jnp.concatenate([max_ref[rows, :], total_ref[rows, :]], axis=0)
+        stats_out[g] = jnp.transpose(stacked)[:8, :]
+
+
+def forward_item(query_item, key_head, value_head, listing, live_tiles, softmax_scale, groups):
     query_rows, head_width = query_item.shape
+    chunk_rows = query_rows // groups
     smem = pl.BlockSpec(memory_space=pltpu.SMEM)
     vmem = pl.BlockSpec(memory_space=pltpu.VMEM)
-    row_shape = jax.ShapeDtypeStruct((query_rows, head_width), jnp.float32)
-    run_max, run_total, run_accum = pl.pallas_call(
+    rows_f32 = pltpu.VMEM((query_rows, head_width), jnp.float32)
+    return pl.pallas_call(
         lambda *refs: forward_kernel(softmax_scale, *refs),
-        out_shape=(row_shape, row_shape, row_shape),
+        out_shape=(
+            jax.ShapeDtypeStruct((groups, chunk_rows, head_width), jnp.bfloat16),
+            jax.ShapeDtypeStruct((groups, 8, 2 * chunk_rows), jnp.float32),
+        ),
         in_specs=[smem, smem, vmem, vmem, vmem],
-        out_specs=(vmem, vmem, vmem),
+        out_specs=(vmem, vmem),
+        scratch_shapes=[rows_f32, rows_f32, rows_f32],
     )(listing, live_tiles.reshape(1), query_item, key_head, value_head)
-    return run_max[:, 0], run_total[:, 0], run_accum
 
 
 def backward_kernel(
-    softmax_scale, list_ref, count_ref, q_ref, k_ref, v_ref, do_ref, log_ref, delta_ref,
-    dq_ref, dk_ref, dv_ref, dq_acc, dk_acc, dv_acc,
+    softmax_scale, list_ref, count_ref, q_ref, k_ref, v_ref, do_ref, att_ref, stats_ref,
+    dq_ref, dk_ref, dv_ref, dq_acc, dk_acc, dv_acc, log_ref, delta_ref,
 ):
+    groups = stats_ref.shape[0]
+    chunk_rows = stats_ref.shape[2] // 2
+    for g in range(groups):
+        rows = pl.ds(g * chunk_rows, chunk_rows)
+        columns = jnp.transpose(jnp.broadcast_to(stats_ref[g][0:1, :], (2 * chunk_rows, 2 * chunk_rows)))
+        log_ref[rows, :] = columns[:chunk_rows, 0:1] + jnp.log(columns[chunk_rows:, 0:1])
+        delta_ref[rows, :] = jnp.sum(
+            att_ref[rows, :].astype(jnp.float32) * do_ref[rows, :].astype(jnp.float32),
+            axis=1,
+            keepdims=True,
+        )
     dq_acc[...] = jnp.zeros(dq_acc.shape, jnp.float32)
     dk_acc[...] = jnp.zeros(dk_acc.shape, jnp.float32)
     dv_acc[...] = jnp.zeros(dv_acc.shape, jnp.float32)
@@ -123,7 +146,7 @@
 
 
 def backward_item(
-    query_item, key_head, value_head, grad_item, log_total, deltas, listing, live_tiles, softmax_scale,
+    query_item, key_head, value_head, grad_item, attended, stats, listing, live_tiles, softmax_scale,
 ):
     query_rows, head_width = query_item.shape
     key_rows = key_head.shape[0]
@@ -142,6 +165,8 @@
             pltpu.VMEM((query_rows, head_width), jnp.float32),
             pltpu.VMEM((key_rows, head_width), jnp.float32),
             pltpu.VMEM((key_rows, head_width), jnp.float32),
+            pltpu.VMEM((query_rows, 1), jnp.float32),
+            pltpu.VMEM((query_rows, 1), jnp.float32),
         ],
     )(
         listing,
@@ -150,8 +175,8 @@
         key_head,
         value_head,
         grad_item,
-        log_total.reshape(query_rows, 1),
-        deltas.reshape(query_rows, 1),
+        attended,
+        stats,
     )
 
 
@@ -386,33 +411,24 @@
     ).reshape(group_keys, 2 * head_width)
     key_group = both_group[:, None, :head_width]
     value_group = both_group[:, None, head_width:]
-    part_max, part_total, part_accum = forward_item(
+    part_accum, stats = forward_item(
         queries[0],
         key_group[:, 0, :],
         value_group[:, 0, :],
         tile_list[0, 0],
         tile_counts[0, 0],
         softmax_scale,
-    )
-    stats = jnp.concatenate(
-        [part_max.reshape(groups, 1, chunk_rows), part_total.reshape(groups, 1, chunk_rows)], axis=2
-    )
-    stats = jnp.concatenate([stats, jnp.zeros((groups, 7, 2 * chunk_rows), jnp.float32)], axis=1)
-    out_rows, out_stats = grp_combine(
-        part_accum.astype(jnp.bfloat16).reshape(groups, chunk_rows, head_width), stats, 0
-    )
+        groups,
+    )
+    out_rows, out_stats = grp_combine(part_accum, stats, 0)
     attended = out_rows.reshape(1, query_rows, head_width)
-    row_top = out_stats[:, 0, :chunk_rows].reshape(1, query_rows)
-    row_total = out_stats[:, 0, chunk_rows:].reshape(1, query_rows)
-    log_total = row_top + jnp.log(row_total)
-    deltas = jnp.sum(attended.astype(jnp.float32) * grad_output.astype(jnp.float32), axis=2)
     query_grad, key_grad, value_grad = backward_item(
         queries[0],
         key_group[:, 0, :],
         value_group[:, 0, :],
         grad_output[0],
-        log_total[0],
-        deltas[0],
+        attended[0],
+        out_stats,
         tile_list[0, 0],
         tile_counts[0, 0],
         softmax_scale,

time: 176 us -> 169 us (0.960)
  local copies, waits for them, and re-layouts: 14.8 us -> 10.1 us
  other arithmetic: 9.29 us -> 4.62 us
  Pallas kernels: 107 us -> 111 us
    pallas_call x1, Pallas kernels: 37.9 us -> 42.7 us  [grp_reduce(): pl.pallas_call(reduce_kernel, out_shape=jax.ShapeDtypeStruct(x.shape, x.d...]
    pallas_call x1, Pallas kernels: 51.8 us -> 55.3 us  [grp_combine(): pl.pallas_call(combine_kernel, out_shape=(jax.ShapeDtypeStruct(accum.shap...]
    pallas_call x1, Pallas kernels: 8.34 us -> 5.96 us  [forward_item(): pl.pallas_call(lambda *refs: forward_kernel(softmax_scale, *refs), out_sh...]
    all_to_all x1, starting transfers between devices: 7.92 us -> 5.61 us  [per_device(): both_back = lax.all_to_all(summed, 'seq', 0, 0, tiled=True)]
    pallas_call x1, Pallas kernels: 9.31 us -> 7.34 us  [backward_item(): pl.pallas_call(lambda *refs: backward_kernel(softmax_scale, *refs), out_s...]
    unnamed x14 -> x10, local copies, waits for them, and re-layouts: 5.57 us -> 3.71 us
    convert_element_type x1 -> x0, other arithmetic: 1.78 us -> none  [per_device(): part_accum.astype(jnp.bfloat16).reshape(groups, chunk_rows, head_width)]
  transfers between devices with their start and end apart: 3 -> 3, of which waited for: 2 -> 2; matrix products, arithmetic and copies ran while one was open for 0% -> 0% of each run, Pallas kernels for 22% -> 25%
where the time goes in v9:
time: 169 us; the launch traced here: 168 us
  Pallas kernels  111 us (66%)
  blocking collectives  26.8 us (16%)
  starting transfers between devices  10.4 us (6%)
  local copies, waits for them, and re-layouts  10.1 us (6%)
  other arithmetic  4.62 us (3%)
  waiting for transfers between devices  3.3 us (2%)
    pallas_call x1, Pallas kernels, grp_combine(): pl.pallas_call(combine_kernel, out_shape=(jax.ShapeDtypeStruct(accum.shap...  55.3 us
    pallas_call x1, Pallas kernels, grp_reduce(): pl.pallas_call(reduce_kernel, out_shape=jax.ShapeDtypeStruct(x.shape, x.d...  42.7 us
    all_to_all x1, blocking collectives, per_device(): lax.all_to_all(both_here.reshape(seq_devices, half_keys, 2 * head_width),...  26.8 us
    pallas_call x1, Pallas kernels, backward_item(): pl.pallas_call(lambda *refs: backward_kernel(softmax_scale, *refs), out_s...  7.34 us
    pallas_call x1, Pallas kernels, forward_item(): pl.pallas_call(lambda *refs: forward_kernel(softmax_scale, *refs), out_sh...  5.96 us
    all_to_all x1, starting transfers between devices, per_device(): both_back = lax.all_to_all(summed, 'seq', 0, 0, tiled=True)  5.61 us
    unnamed x10, local copies, waits for them, and re-layouts  3.71 us
  transfers between devices with their start and end apart: 3, of which 2 were waited for; matrix products, arithmetic and copies ran while one was open for 0% of the time, Pallas kernels for 25%

profile of v9, /device:TPU:1, one launch (start us, length us, event | category | flops | bytes accessed | tf_op | source)
XLA Modules:
  0.0 168.1 jit_solution(116192101296428125)
XLA Ops:
  0.6 1.1 copy.14
  1.8 1.1 copy.15
  3.0 1.1 copy.10
  4.1 0.7 reshape.36
  4.9 26.8 %all_to_all.10 = bf16[32,64,256]{2,1,0:T(8,128)(2,1)S(1)} all-to-all(bf16[32,64,256]{2,1,0:T(8,128)(2,1)S(1)} %reshape.36), channel_id=1, replica_groups=mesh['grp'=16,'seq'=32] {'seq'}, dimensions={0} | all-to-all | bytes 2097152 | tf_op jit(solution)/shard_map/all_to_all | solution.py:403
  31.7 2.3 %collective-permute-start = (bf16[32,64,256]{2,1,0:T(8,128)(2,1)S(1)}, bf16[32,64,256]{2,1,0:T(8,128)(2,1)S(1)}, u32[]{:S(2)}, u32[]{:S(2)}) collective-permute-start(bf16[32,64,256]{2,1,0:T(8,128)(2,1)S(1)} %all_to_all.10), channel_id=1, source_target_pairs={{0,1},{1,0},{2,3},{3,2},{4,5},{5,4},{6,7},{7,6},{8,9},{9,8},{10,11... | collective-permute-start | bytes 3145736 | tf_op jit(solution)/shard_map/ppermute | solution.py:407
  34.0 0.7 copy.11.refs_0_
  35.3 0.9 collective-permute-done
  36.3 0.2 maximum_select_fusion
  36.4 1.5 fusion.1
  37.9 6.0 %shard_map.93 = (bf16[16,64,128]{2,1,0:T(8,128)(2,1)}, f32[16,8,128]{2,1,0:T(8,128)}) custom-call(s32[9,2]{1,0:T(8,128)} %copy.11.refs_0_, s32[1]{0:T(128)} %bitcast.39.refs_1_, bf16[1024,128]{1,0:T(8,128)(2,1)} %bitcast.55, bf16[4096,128]{1,0:T(8,128)(2,1)} %get-tuple-element.19.refs_3_, bf16[4096,128]{1,0:T(8,128)(2,1)} %get-tuple-element.18.refs_4_), custom_call_target="tpu_custom_call" | custom-call | tf_op jit(solution)/shard_map/pallas_call | solution.py:74
  43.9 55.3 %shard_map.94 = (bf16[16,64,128]{2,1,0:T(8,128)(2,1)}, f32[16,8,128]{2,1,0:T(8,128)}) custom-call(bf16[16,64,128]{2,1,0:T(8,128)(2,1)} %get-tuple-element.11.acc_in, f32[16,8,128]{2,1,0:T(8,128)} %get-tuple-element.12.stats_in), custom_call_target="tpu_custom_call" | custom-call | tf_op jit(solution)/shard_map/pallas_call | solution.py:357
  99.2 7.3 %shard_map.95 = (bf16[1024,128]{1,0:T(8,128)(2,1)}, bf16[4096,128]{1,0:T(8,128)(2,1)}, bf16[4096,128]{1,0:T(8,128)(2,1)}) custom-call(s32[9,2]{1,0:T(8,128)} %copy.11.refs_0_, s32[1]{0:T(128)} %bitcast.40.refs_1_, bf16[1024,128]{1,0:T(8,128)(2,1)} %bitcast.56, bf16[4096,128]{1,0:T(8,128)(2,1)} %get-tuple-element.19.refs_3_, ...), custom_call_target="tpu_custom_call" | custom-call | tf_op jit(solution)/shard_map/pallas_call | solution.py:155
  106.6 1.8 %pad_maximum_fusion = bf16[4096,256]{1,0:T(8,128)(2,1)S(1)} fusion(bf16[4096,128]{1,0:T(8,128)(2,1)} %get-tuple-element.17, bf16[4096,128]{1,0:T(8,128)(2,1)} %get-tuple-element.16), kind=kLoop, calls=%fused_computation.1 | loop fusion | flops 4194304 | bytes 4194304 | tf_op jit(solution)/shard_map/concatenate | solution.py:436
  108.5 2.5 %collective-permute-start.1 = (bf16[32,64,256]{2,1,0:T(8,128)(2,1)S(1)}, bf16[32,64,256]{2,1,0:T(8,128)(2,1)}, u32[]{:S(2)}, u32[]{:S(2)}) collective-permute-start(bf16[32,64,256]{2,1,0:T(8,128)(2,1)S(1)} %dynamic-slice_bitcast_fusion), channel_id=1, source_target_pairs={{0,1},{1,0},{2,3},{3,2},{4,5},{5,4},{6,7},{7,6},{8,9},{9,8},{10,11... | collective-permute-start | bytes 3145736 | tf_op jit(solution)/shard_map/ppermute | solution.py:441
  111.0 2.4 %collective-permute-done.1 = bf16[32,64,256]{2,1,0:T(8,128)(2,1)} collective-permute-done((bf16[32,64,256]{2,1,0:T(8,128)(2,1)S(1)}, bf16[32,64,256]{2,1,0:T(8,128)(2,1)}, u32[]{:S(2)}, u32[]{:S(2)}) %collective-permute-start.1) | collective-permute-done | bytes 1048608 | tf_op jit(solution)/shard_map/ppermute | solution.py:441
  113.4 2.6 %fusion = bf16[32,64,256]{2,1,0:T(8,128)(2,1)} fusion(bf16[32,64,256]{2,1,0:T(8,128)(2,1)} %collective-permute-done.1, bf16[32,2,64,256]{3,2,1,0:T(8,128)(2,1)S(1)} %bitcast.42, s32[]{:T(128)S(6)} %select_n.22), kind=kLoop, calls=%fused_computation.3 | loop fusion | flops 2097152 | bytes 3145732 | tf_op jit(solution)/shard_map/convert_element_type | solution.py:441
  115.9 5.6 %all-to-all-start.1 = ((bf16[32,64,256]{2,1,0:T(8,128)(2,1)}), bf16[32,64,256]{2,1,0:T(8,128)(2,1)S(1)}, u32[]{:S(2)}, u32[]{:S(2)}) async-start(bf16[32,64,256]{2,1,0:T(8,128)(2,1)} %fusion), calls=%async_computation.1 | async-start | bytes 2097152 | tf_op jit(solution)/shard_map/all_to_all | solution.py:444
  121.6 42.7 %shard_map.96 = bf16[16,64,128]{2,1,0:T(8,128)(2,1)} custom-call(bf16[16,64,128]{2,1,0:T(8,128)(2,1)} %bitcast.60), custom_call_target="tpu_custom_call" | custom-call | tf_op jit(solution)/shard_map/pallas_call | solution.py:273
  164.3 0.3 reshape.41
  164.6 0.7 copy.13
  165.5 1.2 copy_bitcast_fusion
  166.7 0.7 copy.23
  167.4 0.7 copy.24
  (10 shorter events, 0.4 us)
Async XLA Ops:
  4.1 29.9 %copy-start.2 = (s32[1,1,9,2]{2,3,1,0:T(2,128)S(1)}, s32[1,1,9,2]{2,3,1,0:T(2,128)}, u32[]{:S(2)}) copy-start(s32[1,1,9,2]{2,3,1,0:T(2,128)} %param.10) | copy-start | bytes 220
  31.7 4.6 %collective-permute-start = (bf16[32,64,256]{2,1,0:T(8,128)(2,1)S(1)}, bf16[32,64,256]{2,1,0:T(8,128)(2,1)S(1)}, u32[]{:S(2)}, u32[]{:S(2)}) collective-permute-start(bf16[32,64,256]{2,1,0:T(8,128)(2,1)S(1)} %all_to_all.10), channel_id=1, source_target_pairs={{0,1},{1,0},{2,3},{3,2},{4,5},{5,4},{6,7},{7,6},{8,9},{9,8},{10,11... | collective-permute-start | bytes 3145736 | tf_op jit(solution)/shard_map/ppermute | solution.py:407
  108.5 4.9 %collective-permute-start.1 = (bf16[32,64,256]{2,1,0:T(8,128)(2,1)S(1)}, bf16[32,64,256]{2,1,0:T(8,128)(2,1)}, u32[]{:S(2)}, u32[]{:S(2)}) collective-permute-start(bf16[32,64,256]{2,1,0:T(8,128)(2,1)S(1)} %dynamic-slice_bitcast_fusion), channel_id=1, source_target_pairs={{0,1},{1,0},{2,3},{3,2},{4,5},{5,4},{6,7},{7,6},{8,9},{9,8},{10,11... | collective-permute-start | bytes 3145736 | tf_op jit(solution)/shard_map/ppermute | solution.py:441
  115.9 48.3 %all-to-all-start.1 = ((bf16[32,64,256]{2,1,0:T(8,128)(2,1)}), bf16[32,64,256]{2,1,0:T(8,128)(2,1)S(1)}, u32[]{:S(2)}, u32[]{:S(2)}) async-start(bf16[32,64,256]{2,1,0:T(8,128)(2,1)} %fusion), calls=%async_computation.1 | async-start | bytes 2097152 | tf_op jit(solution)/shard_map/all_to_all | solution.py:444
  165.3 1.4 copy-start
  165.3 2.1 %copy-start.1 = (bf16[16,64,128]{2,1,0:T(8,128)(2,1)S(1)}, bf16[16,64,128]{2,1,0:T(8,128)(2,1)}, u32[]{:S(2)}) copy-start(bf16[16,64,128]{2,1,0:T(8,128)(2,1)} %shard_map.96) | copy-start | bytes 786436

commit v10 on v9

--- a/solution.py
+++ b/solution.py
@@ -85,7 +85,7 @@
 
 def backward_kernel(
     softmax_scale, list_ref, count_ref, q_ref, k_ref, v_ref, do_ref, att_ref, stats_ref,
-    dq_ref, dk_ref, dv_ref, dq_acc, dk_acc, dv_acc, log_ref, delta_ref,
+    dq_ref, kept_ref, given_ref, dq_acc, dk_acc, dv_acc, log_ref, delta_ref,
 ):
     groups = stats_ref.shape[0]
     chunk_rows = stats_ref.shape[2] // 2
@@ -141,8 +141,14 @@
 
     lax.fori_loop(0, live_tiles, visit, 0)
     dq_ref[...] = dq_acc[...].astype(dq_ref.dtype)
-    dk_ref[...] = dk_acc[...].astype(dk_ref.dtype)
-    dv_ref[...] = dv_acc[...].astype(dv_ref.dtype)
+    sources, half, width = kept_ref.shape
+    head_width = width // 2
+    core = lax.rem(lax.axis_index("seq"), 2)
+    for source in range(sources):
+        for out_ref, which in ((kept_ref, core), (given_ref, 1 - core)):
+            rows = pl.ds(pl.multiple_of(source * 2 * half + which * half, half), half)
+            out_ref[source, :, :head_width] = dk_acc[rows, :].astype(out_ref.dtype)
+            out_ref[source, :, head_width:] = dv_acc[rows, :].astype(out_ref.dtype)
 
 
 def backward_item(
@@ -150,14 +156,16 @@
 ):
     query_rows, head_width = query_item.shape
     key_rows = key_head.shape[0]
+    sources = lax.axis_size("seq")
+    halves = (sources, key_rows // sources // QPARTS, 2 * head_width)
     smem = pl.BlockSpec(memory_space=pltpu.SMEM)
     vmem = pl.BlockSpec(memory_space=pltpu.VMEM)
     return pl.pallas_call(
         lambda *refs: backward_kernel(softmax_scale, *refs),
         out_shape=(
             jax.ShapeDtypeStruct((query_rows, head_width), jnp.bfloat16),
-            jax.ShapeDtypeStruct((key_rows, head_width), jnp.bfloat16),
-            jax.ShapeDtypeStruct((key_rows, head_width), jnp.bfloat16),
+            jax.ShapeDtypeStruct(halves, jnp.bfloat16),
+            jax.ShapeDtypeStruct(halves, jnp.bfloat16),
         ),
         in_specs=[smem, smem] + [vmem] * 6,
         out_specs=(vmem, vmem, vmem),
@@ -422,7 +430,7 @@
     )
     out_rows, out_stats = grp_combine(part_accum, stats, 0)
     attended = out_rows.reshape(1, query_rows, head_width)
-    query_grad, key_grad, value_grad = backward_item(
+    query_grad, kept, given = backward_item(
         queries[0],
         key_group[:, 0, :],
         value_group[:, 0, :],
@@ -433,11 +441,6 @@
         tile_counts[0, 0],
         softmax_scale,
     )
-    both_parts = jnp.concatenate([key_grad, value_grad], axis=1).reshape(
-        seq_devices, QPARTS, half_keys, 2 * head_width
-    )
-    kept = lax.dynamic_index_in_dim(both_parts, core, axis=1, keepdims=False)
-    given = lax.dynamic_index_in_dim(both_parts, 1 - core, axis=1, keepdims=False)
     summed = (kept.astype(jnp.float32) + lax.ppermute(given, "seq", pairs).astype(jnp.float32)).astype(
         jnp.bfloat16
     )

time: 169 us -> 170 us (level)
  starting transfers between devices: 10.4 us -> 16.8 us
  Pallas kernels: 111 us -> 106 us
  local copies, waits for them, and re-layouts: 10.1 us -> 12.3 us
  other arithmetic: 4.62 us -> 2.85 us
    pallas_call x1, Pallas kernels: 55.3 us -> 51 us  [grp_combine(): pl.pallas_call(combine_kernel, out_shape=(jax.ShapeDtypeStruct(accum.shap...]
    all_to_all x1, starting transfers between devices: 5.61 us -> 9.66 us  [per_device(): both_back = lax.all_to_all(summed, 'seq', 0, 0, tiled=True)]
    ppermute x1, starting transfers between devices: 2.51 us -> 4.88 us  [per_device(): lax.ppermute(given, 'seq', pairs).astype(jnp.float32)]
    concatenate x1 -> x0, other arithmetic: 1.77 us -> none  [per_device(): jnp.concatenate([key_grad, value_grad], axis=1)]
    slice x1, local copies, waits for them, and re-layouts: 0.18 us -> 1.93 us  [per_device(): grad_values = both_back[:, :, 1, :].reshape(scene_here, -1)]
    unnamed x10 -> x12, local copies, waits for them, and re-layouts: 3.71 us -> 4.94 us
  transfers between devices with their start and end apart: 3 -> 3, of which waited for: 2 -> 2; matrix products, arithmetic and copies ran while one was open for 0% -> 0% of each run, Pallas kernels for 25% -> 26%
where the time goes in v10:
time: 170 us; the launch traced here: 169 us
  Pallas kernels  106 us (62%)
  blocking collectives  26.8 us (16%)
  starting transfers between devices  16.8 us (10%)
  local copies, waits for them, and re-layouts  12.3 us (7%)
  waiting for transfers between devices  3.39 us (2%)
  other arithmetic  2.85 us (2%)
    pallas_call x1, Pallas kernels, grp_combine(): pl.pallas_call(combine_kernel, out_shape=(jax.ShapeDtypeStruct(accum.shap...  51 us
    pallas_call x1, Pallas kernels, grp_reduce(): pl.pallas_call(reduce_kernel, out_shape=jax.ShapeDtypeStruct(x.shape, x.d...  43.7 us
    all_to_all x1, blocking collectives, per_device(): lax.all_to_all(both_here.reshape(seq_devices, half_keys, 2 * head_width),...  26.8 us
    all_to_all x1, starting transfers between devices, per_device(): both_back = lax.all_to_all(summed, 'seq', 0, 0, tiled=True)  9.66 us
    pallas_call x1, Pallas kernels, backward_item(): pl.pallas_call(lambda *refs: backward_kernel(softmax_scale, *refs), out_s...  6.28 us
    unnamed x12, local copies, waits for them, and re-layouts  4.94 us
    ppermute x1, starting transfers between devices, per_device(): lax.ppermute(given, 'seq', pairs).astype(jnp.float32)  4.88 us
    pallas_call x1, Pallas kernels, forward_item(): pl.pallas_call(lambda *refs: forward_kernel(softmax_scale, *refs), out_sh...  4.88 us
  transfers between devices with their start and end apart: 3, of which 2 were waited for; matrix products, arithmetic and copies ran while one was open for 0% of the time, Pallas kernels for 26%

profile of v10, /device:TPU:1, one launch (start us, length us, event | category | flops | bytes accessed | tf_op | source)
XLA Modules:
  0.0 169.4 jit_solution(15308778256418530082)
XLA Ops:
  0.6 1.1 copy.17
  1.8 1.1 copy.18
  3.0 1.1 copy.10
  4.1 0.7 reshape.31
  4.9 26.8 %all_to_all.10 = bf16[32,64,256]{2,1,0:T(8,128)(2,1)S(1)} all-to-all(bf16[32,64,256]{2,1,0:T(8,128)(2,1)S(1)} %reshape.31), channel_id=1, replica_groups=mesh['grp'=16,'seq'=32] {'seq'}, dimensions={0} | all-to-all | bytes 2097152 | tf_op jit(solution)/shard_map/all_to_all | solution.py:411
  31.7 2.3 %collective-permute-start = (bf16[32,64,256]{2,1,0:T(8,128)(2,1)S(1)}, bf16[32,64,256]{2,1,0:T(8,128)(2,1)S(1)}, u32[]{:S(2)}, u32[]{:S(2)}) collective-permute-start(bf16[32,64,256]{2,1,0:T(8,128)(2,1)S(1)} %all_to_all.10), channel_id=1, source_target_pairs={{0,1},{1,0},{2,3},{3,2},{4,5},{5,4},{6,7},{7,6},{8,9},{9,8},{10,11... | collective-permute-start | bytes 3145736 | tf_op jit(solution)/shard_map/ppermute | solution.py:415
  34.7 0.7 copy.11.refs_0_
  35.3 0.9 collective-permute-done
  36.4 1.5 fusion
  37.9 4.9 %shard_map.93 = (bf16[16,64,128]{2,1,0:T(8,128)(2,1)}, f32[16,8,128]{2,1,0:T(8,128)}) custom-call(s32[9,2]{1,0:T(8,128)} %copy.11.refs_0_, s32[1]{0:T(128)} %bitcast.34.refs_1_, bf16[1024,128]{1,0:T(8,128)(2,1)} %bitcast.47, bf16[4096,128]{1,0:T(8,128)(2,1)} %get-tuple-element.19.refs_3_, bf16[4096,128]{1,0:T(8,128)(2,1)} %get-tuple-element.18.refs_4_), custom_call_target="tpu_custom_call" | custom-call | tf_op jit(solution)/shard_map/pallas_call | solution.py:74
  42.8 51.0 %shard_map.94 = (bf16[16,64,128]{2,1,0:T(8,128)(2,1)}, f32[16,8,128]{2,1,0:T(8,128)}) custom-call(bf16[16,64,128]{2,1,0:T(8,128)(2,1)} %get-tuple-element.11.acc_in, f32[16,8,128]{2,1,0:T(8,128)} %get-tuple-element.12.stats_in), custom_call_target="tpu_custom_call" | custom-call | tf_op jit(solution)/shard_map/pallas_call | solution.py:365
  93.8 6.3 %shard_map.95 = (bf16[1024,128]{1,0:T(8,128)(2,1)}, bf16[32,64,256]{2,1,0:T(8,128)(2,1)}, bf16[32,64,256]{2,1,0:T(8,128)(2,1)}) custom-call(s32[9,2]{1,0:T(8,128)} %copy.11.refs_0_, s32[1]{0:T(128)} %bitcast.35.refs_1_, bf16[1024,128]{1,0:T(8,128)(2,1)} %bitcast.48, bf16[4096,128]{1,0:T(8,128)(2,1)} %get-tuple-element.19.refs_3_, ...), custom_call_target="tpu_custom_call" | custom-call | tf_op jit(solution)/shard_map/pallas_call | solution.py:163
  100.1 4.9 %collective-permute-start.1 = (bf16[32,64,256]{2,1,0:T(8,128)(2,1)}, bf16[32,64,256]{2,1,0:T(8,128)(2,1)S(1)}, u32[]{:S(2)}, u32[]{:S(2)}) collective-permute-start(bf16[32,64,256]{2,1,0:T(8,128)(2,1)} %get-tuple-element.17), channel_id=1, source_target_pairs={{0,1},{1,0},{2,3},{3,2},{4,5},{5,4},{6,7},{7,6},{8,9},{9,8},{10,11... | collective-permute-start | bytes 3145736 | tf_op jit(solution)/shard_map/ppermute | solution.py:444
  104.9 2.5 %collective-permute-done.1 = bf16[32,64,256]{2,1,0:T(8,128)(2,1)S(1)} collective-permute-done((bf16[32,64,256]{2,1,0:T(8,128)(2,1)}, bf16[32,64,256]{2,1,0:T(8,128)(2,1)S(1)}, u32[]{:S(2)}, u32[]{:S(2)}) %collective-permute-start.1) | collective-permute-done | bytes 1048608 | tf_op jit(solution)/shard_map/ppermute | solution.py:444
  107.4 2.6 %add_convert_fusion = bf16[32,64,256]{2,1,0:T(8,128)(2,1)} fusion(bf16[32,64,256]{2,1,0:T(8,128)(2,1)S(1)} %collective-permute-done.1, bf16[32,64,256]{2,1,0:T(8,128)(2,1)} %get-tuple-element.16), kind=kLoop, calls=%fused_computation.1 | loop fusion | flops 2097152 | bytes 3145728 | tf_op jit(solution)/shard_map/convert_element_type | solution.py:444
  110.0 9.7 %all-to-all-start.1 = ((bf16[32,64,256]{2,1,0:T(8,128)(2,1)}), bf16[32,64,256]{2,1,0:T(8,128)(2,1)S(1)}, u32[]{:S(2)}, u32[]{:S(2)}) async-start(bf16[32,64,256]{2,1,0:T(8,128)(2,1)} %add_convert_fusion), calls=%async_computation.1 | async-start | bytes 2097152 | tf_op jit(solution)/shard_map/all_to_all | solution.py:447
  119.7 43.7 %shard_map.96 = bf16[16,64,128]{2,1,0:T(8,128)(2,1)} custom-call(bf16[16,64,128]{2,1,0:T(8,128)(2,1)} %bitcast.52), custom_call_target="tpu_custom_call" | custom-call | tf_op jit(solution)/shard_map/pallas_call | solution.py:281
  163.3 0.3 reshape.35
  163.6 1.9 %fusion.1 = (bf16[128,16,1,128]{3,2,0,1:T(2,128)(2,1)S(1)}, bf16[128,16,1,128]{3,2,0,1:T(2,128)(2,1)S(1)}) fusion(bf16[128,16,2,128]{3,2,0,1:T(2,128)(2,1)S(1)} %bitcast.36), kind=kLoop, calls=%fused_computation.6 | loop fusion | bytes 2097152 | tf_op jit(solution)/shard_map/slice | solution.py:451
  165.6 0.6 copy.16
  166.2 0.6 copy.15
  166.8 1.2 copy_bitcast_fusion
  168.0 0.7 copy.26
  168.7 0.7 copy.27
  (9 shorter events, 0.3 us)
Async XLA Ops:
  4.1 30.5 %copy-start.2 = (s32[1,1,9,2]{2,3,1,0:T(2,128)S(1)}, s32[1,1,9,2]{2,3,1,0:T(2,128)}, u32[]{:S(2)}) copy-start(s32[1,1,9,2]{2,3,1,0:T(2,128)} %param.10) | copy-start | bytes 220
  31.7 4.6 %collective-permute-start = (bf16[32,64,256]{2,1,0:T(8,128)(2,1)S(1)}, bf16[32,64,256]{2,1,0:T(8,128)(2,1)S(1)}, u32[]{:S(2)}, u32[]{:S(2)}) collective-permute-start(bf16[32,64,256]{2,1,0:T(8,128)(2,1)S(1)} %all_to_all.10), channel_id=1, source_target_pairs={{0,1},{1,0},{2,3},{3,2},{4,5},{5,4},{6,7},{7,6},{8,9},{9,8},{10,11... | collective-permute-start | bytes 3145736 | tf_op jit(solution)/shard_map/ppermute | solution.py:415
  100.1 7.4 %collective-permute-start.1 = (bf16[32,64,256]{2,1,0:T(8,128)(2,1)}, bf16[32,64,256]{2,1,0:T(8,128)(2,1)S(1)}, u32[]{:S(2)}, u32[]{:S(2)}) collective-permute-start(bf16[32,64,256]{2,1,0:T(8,128)(2,1)} %get-tuple-element.17), channel_id=1, source_target_pairs={{0,1},{1,0},{2,3},{3,2},{4,5},{5,4},{6,7},{7,6},{8,9},{9,8},{10,11... | collective-permute-start | bytes 3145736 | tf_op jit(solution)/shard_map/ppermute | solution.py:444
  110.0 53.3 %all-to-all-start.1 = ((bf16[32,64,256]{2,1,0:T(8,128)(2,1)}), bf16[32,64,256]{2,1,0:T(8,128)(2,1)S(1)}, u32[]{:S(2)}, u32[]{:S(2)}) async-start(bf16[32,64,256]{2,1,0:T(8,128)(2,1)} %add_convert_fusion), calls=%async_computation.1 | async-start | bytes 2097152 | tf_op jit(solution)/shard_map/all_to_all | solution.py:447
  166.2 1.8 %copy-start = (bf16[16,64,128]{2,1,0:T(8,128)(2,1)S(1)}, bf16[16,64,128]{2,1,0:T(8,128)(2,1)}, u32[]{:S(2)}) copy-start(bf16[16,64,128]{2,1,0:T(8,128)(2,1)} %get-tuple-element.13) | copy-start | bytes 786436
  166.2 2.5 %copy-start.1 = (bf16[16,64,128]{2,1,0:T(8,128)(2,1)S(1)}, bf16[16,64,128]{2,1,0:T(8,128)(2,1)}, u32[]{:S(2)}) copy-start(bf16[16,64,128]{2,1,0:T(8,128)(2,1)} %shard_map.96) | copy-start | bytes 786436

commit v11 on v9

--- a/solution.py
+++ b/solution.py
@@ -368,6 +368,77 @@
     )(accum, stats)
 
 
+def gather_kernel(k_ref, v_ref, k_out, v_out, send_sem, recv_sem, pair_send, pair_recv):
+    halves, sources, half, head_width = k_out.shape
+    me = lax.axis_index("seq")
+    grp_here = lax.axis_index("grp")
+    mine = lax.rem(me, 2)
+    partner = me + 1 - 2 * mine
+    head = me // 2
+    mesh_ids = pl.DeviceIdType.MESH
+    barrier = pltpu.get_barrier_semaphore()
+    for step in range(1, sources):
+        pl.semaphore_signal(
+            barrier, inc=1, device_id=(grp_here, lax.rem(me + step, sources)), device_id_type=mesh_ids
+        )
+    pl.semaphore_wait(barrier, sources - 1)
+    copies = []
+    for step in range(1, sources):
+        target = lax.rem(me + step, sources)
+        rows = pl.ds(pl.multiple_of(lax.rem(target, 2) * half, half), half)
+        cols = pl.ds(pl.multiple_of((target // 2) * head_width, head_width), head_width)
+        for index, (source, landing) in enumerate(((k_ref, k_out), (v_ref, v_out))):
+            copy = pltpu.make_async_remote_copy(
+                src_ref=source.at[rows, cols],
+                dst_ref=landing.at[lax.rem(target, 2), me],
+                send_sem=send_sem.at[index, step],
+                recv_sem=recv_sem.at[index, step],
+                device_id=(grp_here, target),
+                device_id_type=mesh_ids,
+            )
+            copy.start()
+            copies.append(copy)
+    own_rows = pl.ds(pl.multiple_of(mine * half, half), half)
+    own_cols = pl.ds(pl.multiple_of(head * head_width, head_width), head_width)
+    k_out[mine, me] = k_ref[own_rows, own_cols]
+    v_out[mine, me] = v_ref[own_rows, own_cols]
+    for copy in copies:
+        copy.wait()
+    copies = []
+    for index, landing in enumerate((k_out, v_out)):
+        copy = pltpu.make_async_remote_copy(
+            src_ref=landing.at[mine],
+            dst_ref=landing.at[mine],
+            send_sem=pair_send.at[index],
+            recv_sem=pair_recv.at[index],
+            device_id=(grp_here, partner),
+            device_id_type=mesh_ids,
+        )
+        copy.start()
+        copies.append(copy)
+    for copy in copies:
+        copy.wait()
+
+
+def seq_gather(scene_keys, scene_values, sources, head_width, collective):
+    half = scene_keys.shape[0] // QPARTS
+    vmem = pl.BlockSpec(memory_space=pltpu.VMEM)
+    out = jax.ShapeDtypeStruct((QPARTS, sources, half, head_width), scene_keys.dtype)
+    return pl.pallas_call(
+        gather_kernel,
+        out_shape=(out, out),
+        in_specs=[vmem, vmem],
+        out_specs=(vmem, vmem),
+        scratch_shapes=[
+            pltpu.SemaphoreType.DMA((2, sources)),
+            pltpu.SemaphoreType.DMA((2, sources)),
+            pltpu.SemaphoreType.DMA((2,)),
+            pltpu.SemaphoreType.DMA((2,)),
+        ],
+        compiler_params=pltpu.CompilerParams(collective_id=collective, has_side_effects=True),
+    )(scene_keys, scene_values)
+
+
 def scatter_rows(rows, parts, collective):
     return grp_exchange(
         rows.reshape(parts, rows.shape[0] // parts, rows.shape[1]), parts, False, collective
@@ -393,24 +464,11 @@
     heads_here = max(1, items_here // QPARTS)
     softmax_scale = head_width ** (-0.5)
     half_keys = scene_here // QPARTS
-    both_here = jnp.stack(
-        [
-            scene_keys.reshape(QPARTS, half_keys, heads_total, head_width),
-            scene_values.reshape(QPARTS, half_keys, heads_total, head_width),
-        ],
-        axis=3,
-    ).transpose(2, 0, 1, 3, 4)
-    mine = lax.all_to_all(
-        both_here.reshape(seq_devices, half_keys, 2 * head_width), "seq", 0, 0, tiled=True
-    )
+    key_halves, value_halves = seq_gather(scene_keys, scene_values, seq_devices, head_width, 4)
+    key_group = key_halves.transpose(1, 0, 2, 3).reshape(group_keys, 1, head_width)
+    value_group = value_halves.transpose(1, 0, 2, 3).reshape(group_keys, 1, head_width)
     pairs = [(2 * h + c, 2 * h + 1 - c) for h in range(seq_devices // 2) for c in range(2)]
-    other = lax.ppermute(mine, "seq", pairs)
     core = lax.rem(lax.axis_index("seq"), 2)
-    both_group = jnp.where(
-        core == 0, jnp.stack([mine, other], axis=1), jnp.stack([other, mine], axis=1)
-    ).reshape(group_keys, 2 * head_width)
-    key_group = both_group[:, None, :head_width]
-    value_group = both_group[:, None, head_width:]
     part_accum, stats = forward_item(
         queries[0],
         key_group[:, 0, :],

time: 169 us -> 168 us (level); the launches traced: 168 us -> 165 us
  Pallas kernels: 111 us -> 138 us
  blocking collectives: 26.8 us -> 0 us
  local copies, waits for them, and re-layouts: 10.1 us -> 8.05 us
    pallas_call x0 -> x1, Pallas kernels: none -> 31 us  [seq_gather(): pl.pallas_call(gather_kernel, out_shape=(out, out), in_specs=[vmem, vmem]...]
    all_to_all x1 -> x0, blocking collectives: 26.8 us -> none  [per_device(): lax.all_to_all(both_here.reshape(seq_devices, half_keys, 2 * head_width),...]
    pallas_call x1, Pallas kernels: 55.3 us -> 51.5 us  [grp_combine(): pl.pallas_call(combine_kernel, out_shape=(jax.ShapeDtypeStruct(accum.shap...]
    transpose x1 -> x2, local copies, waits for them, and re-layouts: 1.08 us -> 3.48 us  [the longest x1 2.38 us: per_device(): key_halves.transpose(1, 0, 2, 3).reshape(group_keys, 1, head_width)]
    ppermute x1 -> x0, starting transfers between devices: 2.29 us -> none  [per_device(): other = lax.ppermute(mine, 'seq', pairs)]
    unnamed x10, local copies, waits for them, and re-layouts: 3.71 us -> 1.42 us
    pallas_call x1, Pallas kernels: 42.7 us -> 44.8 us  [grp_reduce(): pl.pallas_call(reduce_kernel, out_shape=jax.ShapeDtypeStruct(x.shape, x.d...]
    ppermute x1, starting transfers between devices: 2.51 us -> 4.3 us  [per_device(): lax.ppermute(given, 'seq', pairs).astype(jnp.float32)]
  transfers between devices with their start and end apart: 3 -> 2, of which waited for: 2 -> 1; matrix products, arithmetic and copies ran while one was open for 0% -> 0% of each run, Pallas kernels for 25% -> 27%
where the time goes in v11:
time: 168 us; the launch traced here: 165 us
  Pallas kernels  138 us (82%)
  starting transfers between devices  10.8 us (6%)
  local copies, waits for them, and re-layouts  8.05 us (5%)
  other arithmetic  4.33 us (3%)
  waiting for transfers between devices  2.39 us (1%)
    pallas_call x1, Pallas kernels, grp_combine(): pl.pallas_call(combine_kernel, out_shape=(jax.ShapeDtypeStruct(accum.shap...  51.5 us
    pallas_call x1, Pallas kernels, grp_reduce(): pl.pallas_call(reduce_kernel, out_shape=jax.ShapeDtypeStruct(x.shape, x.d...  44.8 us
    pallas_call x1, Pallas kernels, seq_gather(): pl.pallas_call(gather_kernel, out_shape=(out, out), in_specs=[vmem, vmem]...  31 us
    all_to_all x1, starting transfers between devices, per_device(): both_back = lax.all_to_all(summed, 'seq', 0, 0, tiled=True)  6.47 us
    pallas_call x1, Pallas kernels, backward_item(): pl.pallas_call(lambda *refs: backward_kernel(softmax_scale, *refs), out_s...  6.24 us
    pallas_call x1, Pallas kernels, forward_item(): pl.pallas_call(lambda *refs: forward_kernel(softmax_scale, *refs), out_sh...  4.88 us
    ppermute x1, starting transfers between devices, per_device(): lax.ppermute(given, 'seq', pairs).astype(jnp.float32)  4.3 us
  transfers between devices with their start and end apart: 2, of which 1 were waited for; matrix products, arithmetic and copies ran while one was open for 0% of the time, Pallas kernels for 27%

profile of v11, /device:TPU:1, one launch (start us, length us, event | category | flops | bytes accessed | tf_op | source)
XLA Modules:
  0.0 165.4 jit_solution(17142613279779788197)
XLA Ops:
  0.6 31.0 %shard_map.93 = (bf16[2,32,64,128]{3,2,1,0:T(8,128)(2,1)}, bf16[2,32,64,128]{3,2,1,0:T(8,128)(2,1)}) custom-call(bf16[128,2048]{1,0:T(8,128)(2,1)} %k_ref.1, bf16[128,2048]{1,0:T(8,128)(2,1)} %v_ref.1), custom_call_target="tpu_custom_call" | custom-call | tf_op jit(solution)/shard_map/pallas_call | solution.py:427
  31.6 0.0 copy-start.1
  31.6 0.0 copy-start.3
  31.7 2.4 %copy.10 = bf16[32,2,64,128]{3,2,1,0:T(8,128)(2,1)} copy(bf16[32,2,64,128]{3,2,0,1:T(8,128)(2,1)} %bitcast.45) | data formatting | bytes 2097152 | tf_op jit(solution)/shard_map/transpose | solution.py:468
  34.0 1.1 copy.11
  35.1 0.7 copy.12.refs_0_
  36.5 4.9 %shard_map.94 = (bf16[16,64,128]{2,1,0:T(8,128)(2,1)}, f32[16,8,128]{2,1,0:T(8,128)}) custom-call(s32[9,2]{1,0:T(8,128)} %copy.12.refs_0_, s32[1]{0:T(128)} %bitcast.30.refs_1_, bf16[1024,128]{1,0:T(8,128)(2,1)} %bitcast.47, bf16[4096,128]{1,0:T(8,128)(2,1)} %bitcast.32, bf16[4096,128]{1,0:T(8,128)(2,1)} %bitcast.34), custom_call_target="tpu_custom_call" | custom-call | tf_op jit(solution)/shard_map/pallas_call | solution.py:74
  41.4 51.5 %shard_map.95 = (bf16[16,64,128]{2,1,0:T(8,128)(2,1)}, f32[16,8,128]{2,1,0:T(8,128)}) custom-call(bf16[16,64,128]{2,1,0:T(8,128)(2,1)} %get-tuple-element.15.acc_in, f32[16,8,128]{2,1,0:T(8,128)} %get-tuple-element.16.stats_in), custom_call_target="tpu_custom_call" | custom-call | tf_op jit(solution)/shard_map/pallas_call | solution.py:357
  92.9 6.2 %shard_map.96 = (bf16[1024,128]{1,0:T(8,128)(2,1)}, bf16[4096,128]{1,0:T(8,128)(2,1)}, bf16[4096,128]{1,0:T(8,128)(2,1)}) custom-call(s32[9,2]{1,0:T(8,128)} %copy.12.refs_0_, s32[1]{0:T(128)} %bitcast.31.refs_1_, bf16[1024,128]{1,0:T(8,128)(2,1)} %bitcast.48, bf16[4096,128]{1,0:T(8,128)(2,1)} %bitcast.33, bf16[4096,128]{1,0:T(8,128)(2,1)} %bitcast.35, ...), custom_call_target="tpu_custom_call" | custom-call | tf_op jit(solution)/shard_map/pallas_call | solution.py:155
  99.1 1.8 %pad_maximum_fusion = bf16[4096,256]{1,0:T(8,128)(2,1)S(1)} fusion(bf16[4096,128]{1,0:T(8,128)(2,1)} %get-tuple-element.21, bf16[4096,128]{1,0:T(8,128)(2,1)} %get-tuple-element.20), kind=kLoop, calls=%fused_computation | loop fusion | flops 4194304 | bytes 4194304 | tf_op jit(solution)/shard_map/concatenate | solution.py:494
  100.9 0.1 dynamic-slice_bitcast_fusion
  101.0 4.3 %collective-permute-start = (bf16[32,64,256]{2,1,0:T(8,128)(2,1)S(1)}, bf16[32,64,256]{2,1,0:T(8,128)(2,1)}, u32[]{:S(2)}, u32[]{:S(2)}) collective-permute-start(bf16[32,64,256]{2,1,0:T(8,128)(2,1)S(1)} %dynamic-slice_bitcast_fusion), channel_id=1, source_target_pairs={{0,1},{1,0},{2,3},{3,2},{4,5},{5,4},{6,7},{7,6},{8,9},{9,8},{10,11... | collective-permute-start | bytes 3145736 | tf_op jit(solution)/shard_map/ppermute | solution.py:499
  105.3 2.4 %collective-permute-done = bf16[32,64,256]{2,1,0:T(8,128)(2,1)} collective-permute-done((bf16[32,64,256]{2,1,0:T(8,128)(2,1)S(1)}, bf16[32,64,256]{2,1,0:T(8,128)(2,1)}, u32[]{:S(2)}, u32[]{:S(2)}) %collective-permute-start) | collective-permute-done | bytes 1048608 | tf_op jit(solution)/shard_map/ppermute | solution.py:499
  107.7 2.6 %fusion = bf16[32,64,256]{2,1,0:T(8,128)(2,1)} fusion(bf16[32,64,256]{2,1,0:T(8,128)(2,1)} %collective-permute-done, bf16[32,2,64,256]{3,2,1,0:T(8,128)(2,1)S(1)} %bitcast.37, s32[]{:T(128)S(6)} %select_n.7), kind=kLoop, calls=%fused_computation.2 | loop fusion | flops 2097152 | bytes 3145732 | tf_op jit(solution)/shard_map/convert_element_type | solution.py:499
  110.3 6.5 %all-to-all-start = ((bf16[32,64,256]{2,1,0:T(8,128)(2,1)}), bf16[32,64,256]{2,1,0:T(8,128)(2,1)S(1)}, u32[]{:S(2)}, u32[]{:S(2)}) async-start(bf16[32,64,256]{2,1,0:T(8,128)(2,1)} %fusion), calls=%async_computation | async-start | bytes 2097152 | tf_op jit(solution)/shard_map/all_to_all | solution.py:502
  116.8 44.8 %shard_map.97 = bf16[16,64,128]{2,1,0:T(8,128)(2,1)} custom-call(bf16[16,64,128]{2,1,0:T(8,128)(2,1)} %bitcast.50), custom_call_target="tpu_custom_call" | custom-call | tf_op jit(solution)/shard_map/pallas_call | solution.py:273
  161.5 0.0 all-to-all-done
  161.6 0.3 reshape.32
  161.9 0.7 copy.14
  162.6 0.2 fusion.1
  162.8 1.2 copy_bitcast_fusion
  164.0 0.0 copy-done
  164.0 0.7 copy.22
  164.7 0.7 copy.23
  (5 shorter events, 0.0 us)
Async XLA Ops:
  31.6 2.4 %copy-start.1 = (bf16[2,32,64,128]{3,2,1,0:T(8,128)(2,1)S(1)}, bf16[2,32,64,128]{3,2,1,0:T(8,128)(2,1)}, u32[]{:S(2)}) copy-start(bf16[2,32,64,128]{3,2,1,0:T(8,128)(2,1)} %get-tuple-element.14) | copy-start | bytes 3145732
  31.6 3.5 %copy-start.3 = (s32[1,1,9,2]{2,3,1,0:T(2,128)S(1)}, s32[1,1,9,2]{2,3,1,0:T(2,128)}, u32[]{:S(2)}) copy-start(s32[1,1,9,2]{2,3,1,0:T(2,128)} %param.10) | copy-start | bytes 220
  101.0 6.7 %collective-permute-start = (bf16[32,64,256]{2,1,0:T(8,128)(2,1)S(1)}, bf16[32,64,256]{2,1,0:T(8,128)(2,1)}, u32[]{:S(2)}, u32[]{:S(2)}) collective-permute-start(bf16[32,64,256]{2,1,0:T(8,128)(2,1)S(1)} %dynamic-slice_bitcast_fusion), channel_id=1, source_target_pairs={{0,1},{1,0},{2,3},{3,2},{4,5},{5,4},{6,7},{7,6},{8,9},{9,8},{10,11... | collective-permute-start | bytes 3145736 | tf_op jit(solution)/shard_map/ppermute | solution.py:499
  110.3 51.3 %all-to-all-start = ((bf16[32,64,256]{2,1,0:T(8,128)(2,1)}), bf16[32,64,256]{2,1,0:T(8,128)(2,1)S(1)}, u32[]{:S(2)}, u32[]{:S(2)}) async-start(bf16[32,64,256]{2,1,0:T(8,128)(2,1)} %fusion), calls=%async_computation | async-start | bytes 2097152 | tf_op jit(solution)/shard_map/all_to_all | solution.py:502
  162.5 1.4 copy-start
  162.6 2.1 %copy-start.2 = (bf16[16,64,128]{2,1,0:T(8,128)(2,1)S(1)}, bf16[16,64,128]{2,1,0:T(8,128)(2,1)}, u32[]{:S(2)}) copy-start(bf16[16,64,128]{2,1,0:T(8,128)(2,1)} %shard_map.97) | copy-start | bytes 786436

commit v12 on v9

--- a/solution.py
+++ b/solution.py
@@ -368,6 +368,111 @@
     )(accum, stats)
 
 
+def back_kernel(
+    dq_in, dk_in, dv_in, dq_out, gk_out, gv_out, part_ref, recv_k, recv_v,
+    send_sem, recv_sem, back_send, back_recv, kv_send, kv_recv,
+):
+    groups = dq_out.shape[0]
+    sources, block, head_width = recv_k.shape
+    me = lax.axis_index("grp")
+    lane = lax.axis_index("seq")
+    mesh_ids = pl.DeviceIdType.MESH
+    barrier = pltpu.get_barrier_semaphore()
+    for step in range(1, groups):
+        pl.semaphore_signal(
+            barrier, inc=1, device_id=(lax.rem(me + step, groups), lane), device_id_type=mesh_ids
+        )
+    for step in range(1, sources):
+        pl.semaphore_signal(
+            barrier, inc=1, device_id=(me, lax.rem(lane + step, sources)), device_id_type=mesh_ids
+        )
+    pl.semaphore_wait(barrier, groups - 1 + sources - 1)
+    returns = []
+    for step in range(1, sources):
+        target = lax.rem(lane + step, sources)
+        rows = pl.ds(pl.multiple_of(target * block, block), block)
+        for index, (source, landing) in enumerate(((dk_in, recv_k), (dv_in, recv_v))):
+            copy = pltpu.make_async_remote_copy(
+                src_ref=source.at[rows],
+                dst_ref=landing.at[lane],
+                send_sem=kv_send.at[index, step],
+                recv_sem=kv_recv.at[index, step],
+                device_id=(me, target),
+                device_id_type=mesh_ids,
+            )
+            copy.start()
+            returns.append(copy)
+    copies = []
+    for step in range(1, groups):
+        target = lax.rem(me + step, groups)
+        copy = pltpu.make_async_remote_copy(
+            src_ref=dq_in.at[target],
+            dst_ref=part_ref.at[me],
+            send_sem=send_sem.at[step],
+            recv_sem=recv_sem.at[step],
+            device_id=(target, lane),
+            device_id_type=mesh_ids,
+        )
+        copy.start()
+        copies.append(copy)
+    own_rows = pl.ds(pl.multiple_of(lane * block, block), block)
+    recv_k[lane] = dk_in[own_rows, :]
+    recv_v[lane] = dv_in[own_rows, :]
+    part_ref[me] = dq_in[me]
+    for copy in copies:
+        copy.wait()
+    dq_out[me] = jnp.sum(part_ref[...].astype(jnp.float32), axis=0).astype(dq_out.dtype)
+    copies = []
+    for step in range(1, groups):
+        target = lax.rem(me + step, groups)
+        copy = pltpu.make_async_remote_copy(
+            src_ref=dq_out.at[me],
+            dst_ref=dq_out.at[me],
+            send_sem=back_send.at[step],
+            recv_sem=back_recv.at[step],
+            device_id=(target, lane),
+            device_id_type=mesh_ids,
+        )
+        copy.start()
+        copies.append(copy)
+    for copy in returns:
+        copy.wait()
+    for head in range(sources // 2):
+        cols = pl.ds(head * head_width, head_width)
+        for landing, out_ref in ((recv_k, gk_out), (recv_v, gv_out)):
+            out_ref[:, cols] = (
+                landing[2 * head].astype(jnp.float32) + landing[2 * head + 1].astype(jnp.float32)
+            ).astype(out_ref.dtype)
+    for copy in copies:
+        copy.wait()
+
+
+def back_exchange(query_grad, key_grad, value_grad, groups, sources, collective):
+    head_width = query_grad.shape[-1]
+    block = key_grad.shape[0] // sources
+    vmem = pl.BlockSpec(memory_space=pltpu.VMEM)
+    grad_shape = jax.ShapeDtypeStruct((block, sources // 2 * head_width), key_grad.dtype)
+    sems = pltpu.SemaphoreType.DMA((groups,))
+    return pl.pallas_call(
+        back_kernel,
+        out_shape=(jax.ShapeDtypeStruct(query_grad.shape, query_grad.dtype), grad_shape, grad_shape),
+        in_specs=[vmem, vmem, vmem],
+        out_specs=(vmem, vmem, vmem),
+        scratch_shapes=[
+            pltpu.VMEM(query_grad.shape, query_grad.dtype),
+            pltpu.VMEM((sources, block, head_width), key_grad.dtype),
+            pltpu.VMEM((sources, block, head_width), key_grad.dtype),
+            sems,
+            sems,
+            sems,
+            sems,
+            pltpu.SemaphoreType.DMA((2, sources)),
+            pltpu.SemaphoreType.DMA((2, sources)),
+        ],
+        compiler_params=pltpu.CompilerParams(collective_id=collective, has_side_effects=True),
+    )(query_grad, key_grad, value_grad)
+
+
 def scatter_rows(rows, parts, collective):
     return grp_exchange(
         rows.reshape(parts, rows.shape[0] // parts, rows.shape[1]), parts, False, collective
@@ -433,22 +538,10 @@
         tile_counts[0, 0],
         softmax_scale,
     )
-    both_parts = jnp.concatenate([key_grad, value_grad], axis=1).reshape(
-        seq_devices, QPARTS, half_keys, 2 * head_width
-    )
-    kept = lax.dynamic_index_in_dim(both_parts, core, axis=1, keepdims=False)
-    given = lax.dynamic_index_in_dim(both_parts, 1 - core, axis=1, keepdims=False)
-    summed = (kept.astype(jnp.float32) + lax.ppermute(given, "seq", pairs).astype(jnp.float32)).astype(
-        jnp.bfloat16
-    )
-    both_back = lax.all_to_all(summed, "seq", 0, 0, tiled=True)
-    both_back = both_back.reshape(heads_total, QPARTS, half_keys, 2, head_width).transpose(1, 2, 0, 3, 4)
-    both_back = both_back.reshape(scene_here, heads_total, 2, head_width)
-    grad_keys = both_back[:, :, 0, :].reshape(scene_here, -1)
-    grad_values = both_back[:, :, 1, :].reshape(scene_here, -1)
-    grad_queries = grp_reduce(
-        query_grad.reshape(groups, chunk_rows, head_width), groups, 2
-    ).reshape(1, query_rows, head_width)
+    grad_queries, grad_keys, grad_values = back_exchange(
+        query_grad.reshape(groups, chunk_rows, head_width), key_grad, value_grad, groups, seq_devices, 2
+    )
+    grad_queries = grad_queries.reshape(1, query_rows, head_width)
     return (attended, grad_queries, grad_keys, grad_values)
 
 

time: 169 us -> 157 us (0.929)
  starting transfers between devices: 10.4 us -> 2.29 us
  other arithmetic: 4.62 us -> 0.29 us
  waiting for transfers between devices: 3.3 us -> 0.91 us
  Pallas kernels: 111 us -> 113 us
    all_to_all x1 -> x0, starting transfers between devices: 5.61 us -> none  [per_device(): both_back = lax.all_to_all(summed, 'seq', 0, 0, tiled=True)]
    pallas_call x1, Pallas kernels: 55.3 us -> 51 us  [grp_combine(): pl.pallas_call(combine_kernel, out_shape=(jax.ShapeDtypeStruct(accum.shap...]
    pallas_call x1, Pallas kernels: 42.7 us -> 46.8 us  [back_exchange(): pl.pallas_call(back_kernel, out_shape=(jax.ShapeDtypeStruct(query_grad.sh...]
    unnamed x10 -> x12, local copies, waits for them, and re-layouts: 3.71 us -> 7.35 us
    convert_element_type x1 -> x0, other arithmetic: 2.56 us -> none  [per_device(): (kept.astype(jnp.float32) + lax.ppermute(given, 'seq', pairs).astype(jnp....]
    ppermute x1 -> x0, starting transfers between devices: 2.51 us -> none  [per_device(): lax.ppermute(given, 'seq', pairs).astype(jnp.float32)]
    ppermute x1 -> x0, waiting for transfers between devices: 2.39 us -> none  [per_device(): lax.ppermute(given, 'seq', pairs).astype(jnp.float32)]
    concatenate x1 -> x0, other arithmetic: 1.77 us -> none  [per_device(): jnp.concatenate([key_grad, value_grad], axis=1)]
  transfers between devices with their start and end apart: 3 -> 1, of which waited for: 2 -> 1; matrix products, arithmetic and copies ran while one was open for 0% -> 0% of each run, Pallas kernels for 25% -> 0%
where the time goes in v12:
time: 157 us; the launch traced here: 156 us
  Pallas kernels  113 us (72%)
  blocking collectives  26.8 us (17%)
  local copies, waits for them, and re-layouts  11.3 us (7%)
  starting transfers between devices  2.29 us (1%)
    pallas_call x1, Pallas kernels, grp_combine(): pl.pallas_call(combine_kernel, out_shape=(jax.ShapeDtypeStruct(accum.shap...  51 us
    pallas_call x1, Pallas kernels, back_exchange(): pl.pallas_call(back_kernel, out_shape=(jax.ShapeDtypeStruct(query_grad.sh...  46.8 us
    all_to_all x1, blocking collectives, per_device(): lax.all_to_all(both_here.reshape(seq_devices, half_keys, 2 * head_width),...  26.8 us
    pallas_call x1, Pallas kernels, backward_item(): pl.pallas_call(lambda *refs: backward_kernel(softmax_scale, *refs), out_s...  8.51 us
    unnamed x12, local copies, waits for them, and re-layouts  7.35 us
    pallas_call x1, Pallas kernels, forward_item(): pl.pallas_call(lambda *refs: forward_kernel(softmax_scale, *refs), out_sh...  7.05 us
  transfers between devices with their start and end apart: 1, of which 1 were waited for; matrix products, arithmetic and copies ran while one was open for 0% of the time, Pallas kernels for 0%

profile of v12, /device:TPU:1, one launch (start us, length us, event | category | flops | bytes accessed | tf_op | source)
XLA Modules:
  0.0 156.4 jit_solution(11912960473508758546)
XLA Ops:
  0.6 1.1 copy.13
  1.8 1.1 copy.14
  2.9 0.1 maximum_bitcast_fusion
  3.0 1.1 copy.10
  4.1 0.0 copy-start.2
  4.1 0.7 reshape.25
  4.9 26.8 %all_to_all.5 = bf16[32,64,256]{2,1,0:T(8,128)(2,1)S(1)} all-to-all(bf16[32,64,256]{2,1,0:T(8,128)(2,1)S(1)} %reshape.25), channel_id=1, replica_groups=mesh['grp'=16,'seq'=32] {'seq'}, dimensions={0} | all-to-all | bytes 2097152 | tf_op jit(solution)/shard_map/all_to_all | solution.py:508
  31.7 2.3 %collective-permute-start = (bf16[32,64,256]{2,1,0:T(8,128)(2,1)S(1)}, bf16[32,64,256]{2,1,0:T(8,128)(2,1)S(1)}, u32[]{:S(2)}, u32[]{:S(2)}) collective-permute-start(bf16[32,64,256]{2,1,0:T(8,128)(2,1)S(1)} %all_to_all.5), channel_id=1, source_target_pairs={{0,1},{1,0},{2,3},{3,2},{4,5},{5,4},{6,7},{7,6},{8,9},{9,8},{10,11... | collective-permute-start | bytes 3145736 | tf_op jit(solution)/shard_map/ppermute | solution.py:512
  34.6 0.0 copy-done.2
  34.7 0.7 copy.11.refs_0_
  35.3 0.9 collective-permute-done
  36.3 0.2 maximum_select_fusion
  36.4 1.4 fusion
  37.9 7.1 %shard_map.93 = (bf16[16,64,128]{2,1,0:T(8,128)(2,1)}, f32[16,8,128]{2,1,0:T(8,128)}) custom-call(s32[9,2]{1,0:T(8,128)} %copy.11.refs_0_, s32[1]{0:T(128)} %bitcast.21.refs_1_, bf16[1024,128]{1,0:T(8,128)(2,1)} %bitcast.30, bf16[4096,128]{1,0:T(8,128)(2,1)} %get-tuple-element.25.refs_3_, bf16[4096,128]{1,0:T(8,128)(2,1)} %get-tuple-element.24.refs_4_), custom_call_target="tpu_custom_call" | custom-call | tf_op jit(solution)/shard_map/pallas_call | solution.py:74
  44.9 51.0 %shard_map.94 = (bf16[16,64,128]{2,1,0:T(8,128)(2,1)}, f32[16,8,128]{2,1,0:T(8,128)}) custom-call(bf16[16,64,128]{2,1,0:T(8,128)(2,1)} %get-tuple-element.14.acc_in, f32[16,8,128]{2,1,0:T(8,128)} %get-tuple-element.15.stats_in), custom_call_target="tpu_custom_call" | custom-call | tf_op jit(solution)/shard_map/pallas_call | solution.py:357
  96.0 0.0 copy-start
  96.0 8.5 %shard_map.95 = (bf16[1024,128]{1,0:T(8,128)(2,1)}, bf16[4096,128]{1,0:T(8,128)(2,1)}, bf16[4096,128]{1,0:T(8,128)(2,1)}) custom-call(s32[9,2]{1,0:T(8,128)} %copy.11.refs_0_, s32[1]{0:T(128)} %bitcast.22.refs_1_, bf16[1024,128]{1,0:T(8,128)(2,1)} %bitcast.31, bf16[4096,128]{1,0:T(8,128)(2,1)} %get-tuple-element.25.refs_3_, ...), custom_call_target="tpu_custom_call" | custom-call | tf_op jit(solution)/shard_map/pallas_call | solution.py:155
  104.5 46.8 %shard_map.96 = (bf16[16,64,128]{2,1,0:T(8,128)(2,1)}, bf16[128,2048]{1,0:T(8,128)(2,1)}, bf16[128,2048]{1,0:T(8,128)(2,1)}) custom-call(bf16[16,64,128]{2,1,0:T(8,128)(2,1)} %bitcast.35, bf16[4096,128]{1,0:T(8,128)(2,1)} %get-tuple-element.19.dk_in, bf16[4096,128]{1,0:T(8,128)(2,1)} %get-tuple-element.20.dv_in), custom_call_target="tpu_custom_call" | custom-call | tf_op jit(solution)/shard_map/pallas_call | solution.py:456
  151.3 0.0 copy-start.1
  151.3 0.0 copy-done
  151.3 0.7 copy.20
  152.0 1.7 %copy.21 = bf16[1,1024,128]{2,1,0:T(8,128)(2,1)} copy(bf16[1,1024,128]{2,1,0:T(8,128)(2,1)} %bitcast.36) | data formatting | bytes 524288
  153.7 1.9 %copy.22 = bf16[128,2048]{1,0:T(8,128)(2,1)} copy(bf16[128,2048]{1,0:T(8,128)(2,1)} %get-tuple-element.32) | data formatting | bytes 1048576
  155.6 0.8 copy.23
  (1 shorter events, 0.0 us)
Async XLA Ops:
  4.1 30.5 %copy-start.2 = (s32[1,1,9,2]{2,3,1,0:T(2,128)S(1)}, s32[1,1,9,2]{2,3,1,0:T(2,128)}, u32[]{:S(2)}) copy-start(s32[1,1,9,2]{2,3,1,0:T(2,128)} %param.10) | copy-start | bytes 220
  31.7 4.6 %collective-permute-start = (bf16[32,64,256]{2,1,0:T(8,128)(2,1)S(1)}, bf16[32,64,256]{2,1,0:T(8,128)(2,1)S(1)}, u32[]{:S(2)}, u32[]{:S(2)}) collective-permute-start(bf16[32,64,256]{2,1,0:T(8,128)(2,1)S(1)} %all_to_all.5), channel_id=1, source_target_pairs={{0,1},{1,0},{2,3},{3,2},{4,5},{5,4},{6,7},{7,6},{8,9},{9,8},{10,11... | collective-permute-start | bytes 3145736 | tf_op jit(solution)/shard_map/ppermute | solution.py:512
  96.0 55.3 %copy-start = (bf16[16,64,128]{2,1,0:T(8,128)(2,1)S(1)}, bf16[16,64,128]{2,1,0:T(8,128)(2,1)}, u32[]{:S(2)}) copy-start(bf16[16,64,128]{2,1,0:T(8,128)(2,1)} %get-tuple-element.16) | copy-start | bytes 786436
  151.3 4.3 %copy-start.1 = (bf16[128,2048]{1,0:T(8,128)(2,1)S(1)}, bf16[128,2048]{1,0:T(8,128)(2,1)}, u32[]{:S(2)}) copy-start(bf16[128,2048]{1,0:T(8,128)(2,1)} %get-tuple-element.33) | copy-start | bytes 1572868

commit v13 on v12

--- a/solution.py
+++ b/solution.py
@@ -473,6 +473,77 @@
     )(query_grad, key_grad, value_grad)
 
 
+def gather_kernel(k_ref, v_ref, k_out, v_out, send_sem, recv_sem, pair_send, pair_recv):
+    sources, halves, half, head_width = k_out.shape
+    me = lax.axis_index("seq")
+    grp_here = lax.axis_index("grp")
+    mine = lax.rem(me, 2)
+    partner = me + 1 - 2 * mine
+    head = me // 2
+    mesh_ids = pl.DeviceIdType.MESH
+    barrier = pltpu.get_barrier_semaphore()
+    for step in range(1, sources):
+        pl.semaphore_signal(
+            barrier, inc=1, device_id=(grp_here, lax.rem(me + step, sources)), device_id_type=mesh_ids
+        )
+    pl.semaphore_wait(barrier, sources - 1)
+    copies = []
+    for step in range(1, sources):
+        target = lax.rem(me + step, sources)
+        rows = pl.ds(pl.multiple_of(lax.rem(target, 2) * half, half), half)
+        cols = pl.ds(pl.multiple_of((target // 2) * head_width, head_width), head_width)
+        for index, (source, landing) in enumerate(((k_ref, k_out), (v_ref, v_out))):
+            copy = pltpu.make_async_remote_copy(
+                src_ref=source.at[rows, cols],
+                dst_ref=landing.at[me, lax.rem(target, 2)],
+                send_sem=send_sem.at[index, step],
+                recv_sem=recv_sem.at[index, step],
+                device_id=(grp_here, target),
+                device_id_type=mesh_ids,
+            )
+            copy.start()
+            copies.append(copy)
+    own_rows = pl.ds(pl.multiple_of(mine * half, half), half)
+    own_cols = pl.ds(pl.multiple_of(head * head_width, head_width), head_width)
+    k_out[me, mine] = k_ref[own_rows, own_cols]
+    v_out[me, mine] = v_ref[own_rows, own_cols]
+    for copy in copies:
+        copy.wait()
+    copies = []
+    for index, landing in enumerate((k_out, v_out)):
+        copy = pltpu.make_async_remote_copy(
+            src_ref=landing.at[:, mine],
+            dst_ref=landing.at[:, mine],
+            send_sem=pair_send.at[index],
+            recv_sem=pair_recv.at[index],
+            device_id=(grp_here, partner),
+            device_id_type=mesh_ids,
+        )
+        copy.start()
+        copies.append(copy)
+    for copy in copies:
+        copy.wait()
+
+
+def seq_gather(scene_keys, scene_values, sources, head_width, collective):
+    half = scene_keys.shape[0] // QPARTS
+    vmem = pl.BlockSpec(memory_space=pltpu.VMEM)
+    out = jax.ShapeDtypeStruct((sources, QPARTS, half, head_width), scene_keys.dtype)
+    return pl.pallas_call(
+        gather_kernel,
+        out_shape=(out, out),
+        in_specs=[vmem, vmem],
+        out_specs=(vmem, vmem),
+        scratch_shapes=[
+            pltpu.SemaphoreType.DMA((2, sources)),
+            pltpu.SemaphoreType.DMA((2, sources)),
+            pltpu.SemaphoreType.DMA((2,)),
+            pltpu.SemaphoreType.DMA((2,)),
+        ],
+        compiler_params=pltpu.CompilerParams(collective_id=collective, has_side_effects=True),
+    )(scene_keys, scene_values)
+
+
 def scatter_rows(rows, parts, collective):
     return grp_exchange(
         rows.reshape(parts, rows.shape[0] // parts, rows.shape[1]), parts, False, collective
@@ -498,24 +569,9 @@
     heads_here = max(1, items_here // QPARTS)
     softmax_scale = head_width ** (-0.5)
     half_keys = scene_here // QPARTS
-    both_here = jnp.stack(
-        [
-            scene_keys.reshape(QPARTS, half_keys, heads_total, head_width),
-            scene_values.reshape(QPARTS, half_keys, heads_total, head_width),
-        ],
-        axis=3,
-    ).transpose(2, 0, 1, 3, 4)
-    mine = lax.all_to_all(
-        both_here.reshape(seq_devices, half_keys, 2 * head_width), "seq", 0, 0, tiled=True
-    )
-    pairs = [(2 * h + c, 2 * h + 1 - c) for h in range(seq_devices // 2) for c in range(2)]
-    other = lax.ppermute(mine, "seq", pairs)
-    core = lax.rem(lax.axis_index("seq"), 2)
-    both_group = jnp.where(
-        core == 0, jnp.stack([mine, other], axis=1), jnp.stack([other, mine], axis=1)
-    ).reshape(group_keys, 2 * head_width)
-    key_group = both_group[:, None, :head_width]
-    value_group = both_group[:, None, head_width:]
+    key_halves, value_halves = seq_gather(scene_keys, scene_values, seq_devices, head_width, 4)
+    key_group = key_halves.reshape(group_keys, 1, head_width)
+    value_group = value_halves.reshape(group_keys, 1, head_width)
     part_accum, stats = forward_item(
         queries[0],
         key_group[:, 0, :],

time: 157 us -> 150 us (0.955)
  Pallas kernels: 113 us -> 143 us
  blocking collectives: 26.8 us -> 0 us
  local copies, waits for them, and re-layouts: 11.3 us -> 5.08 us
  starting transfers between devices: 2.29 us -> 0 us
    pallas_call x0 -> x1, Pallas kernels: none -> 31 us  [seq_gather(): pl.pallas_call(gather_kernel, out_shape=(out, out), in_specs=[vmem, vmem]...]
    all_to_all x1 -> x0, blocking collectives: 26.8 us -> none  [per_device(): lax.all_to_all(both_here.reshape(seq_devices, half_keys, 2 * head_width),...]
    unnamed x12 -> x14, local copies, waits for them, and re-layouts: 7.35 us -> 4.4 us
    pallas_call x1, Pallas kernels: 46.8 us -> 49.7 us  [back_exchange(): pl.pallas_call(back_kernel, out_shape=(jax.ShapeDtypeStruct(query_grad.sh...]
    pallas_call x1, Pallas kernels: 51 us -> 48.7 us  [grp_combine(): pl.pallas_call(combine_kernel, out_shape=(jax.ShapeDtypeStruct(accum.shap...]
    ppermute x1 -> x0, starting transfers between devices: 2.29 us -> none  [per_device(): other = lax.ppermute(mine, 'seq', pairs)]
  transfers between devices with their start and end apart: 1 -> 0, of which waited for: 1 -> 0; matrix products, arithmetic and copies ran while one was open for 0% -> 0% of each run, Pallas kernels for 0% -> 0%
where the time goes in v13:
time: 150 us; the launch traced here: 149 us
  Pallas kernels  143 us (95%)
  local copies, waits for them, and re-layouts  5.08 us (3%)
    pallas_call x1, Pallas kernels, back_exchange(): pl.pallas_call(back_kernel, out_shape=(jax.ShapeDtypeStruct(query_grad.sh...  49.7 us
    pallas_call x1, Pallas kernels, grp_combine(): pl.pallas_call(combine_kernel, out_shape=(jax.ShapeDtypeStruct(accum.shap...  48.7 us
    pallas_call x1, Pallas kernels, seq_gather(): pl.pallas_call(gather_kernel, out_shape=(out, out), in_specs=[vmem, vmem]...  31 us
    pallas_call x1, Pallas kernels, backward_item(): pl.pallas_call(lambda *refs: backward_kernel(softmax_scale, *refs), out_s...  7.37 us
    pallas_call x1, Pallas kernels, forward_item(): pl.pallas_call(lambda *refs: forward_kernel(softmax_scale, *refs), out_sh...  5.97 us
    unnamed x14, local copies, waits for them, and re-layouts  4.4 us

profile of v13, /device:TPU:1, one launch (start us, length us, event | category | flops | bytes accessed | tf_op | source)
XLA Modules:
  0.0 149.1 jit_solution(6720485358522317860)
XLA Ops:
  1.3 0.0 copy-start.4
  1.3 0.7 copy-done.4
  2.0 0.7 copy.10.refs_0_
  2.6 31.0 %shard_map.93 = (bf16[32,2,64,128]{3,2,1,0:T(8,128)(2,1)}, bf16[32,2,64,128]{3,2,1,0:T(8,128)(2,1)}) custom-call(bf16[128,2048]{1,0:T(8,128)(2,1)} %k_ref.1, bf16[128,2048]{1,0:T(8,128)(2,1)} %v_ref.1), custom_call_target="tpu_custom_call" | custom-call | tf_op jit(solution)/shard_map/pallas_call | solution.py:532
  33.7 6.0 %shard_map.94 = (bf16[16,64,128]{2,1,0:T(8,128)(2,1)}, f32[16,8,128]{2,1,0:T(8,128)}) custom-call(s32[9,2]{1,0:T(8,128)} %copy.10.refs_0_, s32[1]{0:T(128)} %bitcast.10.refs_1_, bf16[1024,128]{1,0:T(8,128)(2,1)} %bitcast.18, bf16[4096,128]{1,0:T(8,128)(2,1)} %bitcast.12, bf16[4096,128]{1,0:T(8,128)(2,1)} %bitcast.14), custom_call_target="tpu_custom_call" | custom-call | tf_op jit(solution)/shard_map/pallas_call | solution.py:74
  39.6 48.7 %shard_map.95 = (bf16[16,64,128]{2,1,0:T(8,128)(2,1)}, f32[16,8,128]{2,1,0:T(8,128)}) custom-call(bf16[16,64,128]{2,1,0:T(8,128)(2,1)} %get-tuple-element.18.acc_in, f32[16,8,128]{2,1,0:T(8,128)} %get-tuple-element.19.stats_in), custom_call_target="tpu_custom_call" | custom-call | tf_op jit(solution)/shard_map/pallas_call | solution.py:357
  88.3 7.4 %shard_map.96 = (bf16[1024,128]{1,0:T(8,128)(2,1)}, bf16[4096,128]{1,0:T(8,128)(2,1)}, bf16[4096,128]{1,0:T(8,128)(2,1)}) custom-call(s32[9,2]{1,0:T(8,128)} %copy.10.refs_0_, s32[1]{0:T(128)} %bitcast.11.refs_1_, bf16[1024,128]{1,0:T(8,128)(2,1)} %bitcast.19, bf16[4096,128]{1,0:T(8,128)(2,1)} %bitcast.13, bf16[4096,128]{1,0:T(8,128)(2,1)} %bitcast.15, ...), custom_call_target="tpu_custom_call" | custom-call | tf_op jit(solution)/shard_map/pallas_call | solution.py:155
  95.7 0.0 copy-start
  95.7 49.7 %shard_map.97 = (bf16[16,64,128]{2,1,0:T(8,128)(2,1)}, bf16[128,2048]{1,0:T(8,128)(2,1)}, bf16[128,2048]{1,0:T(8,128)(2,1)}) custom-call(bf16[16,64,128]{2,1,0:T(8,128)(2,1)} %bitcast.21, bf16[4096,128]{1,0:T(8,128)(2,1)} %get-tuple-element.23.dk_in, bf16[4096,128]{1,0:T(8,128)(2,1)} %get-tuple-element.24.dv_in), custom_call_target="tpu_custom_call" | custom-call | tf_op jit(solution)/shard_map/pallas_call | solution.py:456
  145.4 0.0 copy-start.3
  145.4 0.0 copy-done
  145.4 0.0 copy-start.2
  145.4 0.7 copy.17
  146.1 0.3 copy-done.3
  146.4 0.7 copy.18
  147.1 0.0 copy-done.2
  147.1 0.0 copy-start.1
  147.1 0.8 copy.19
  147.9 0.4 copy-done.1
  148.4 0.8 copy.20
Async XLA Ops:
  1.3 0.7 copy-start.4
  95.7 49.7 %copy-start = (bf16[16,64,128]{2,1,0:T(8,128)(2,1)S(1)}, bf16[16,64,128]{2,1,0:T(8,128)(2,1)}, u32[]{:S(2)}) copy-start(bf16[16,64,128]{2,1,0:T(8,128)(2,1)} %get-tuple-element.20) | copy-start | bytes 786436
  145.4 1.0 copy-start.3
  145.4 1.7 %copy-start.2 = (bf16[128,2048]{1,0:T(8,128)(2,1)S(1)}, bf16[128,2048]{1,0:T(8,128)(2,1)}, u32[]{:S(2)}) copy-start(bf16[128,2048]{1,0:T(8,128)(2,1)} %get-tuple-element.34) | copy-start | bytes 1572868
  147.1 1.2 copy-start.1

commit v14 on v13

--- a/solution.py
+++ b/solution.py
@@ -369,7 +369,7 @@
 
 
 def back_kernel(
-    dq_in, dk_in, dv_in, dq_out, gk_out, gv_out, part_ref, recv_k, recv_v,
+    dq_in, dk_in, dv_in, dq_out, recv_k, recv_v, part_ref,
     send_sem, recv_sem, back_send, back_recv, kv_send, kv_recv,
 ):
     groups = dq_out.shape[0]
@@ -437,14 +437,18 @@
         copies.append(copy)
     for copy in returns:
         copy.wait()
-    for head in range(sources // 2):
+    for copy in copies:
+        copy.wait()
+
+
+def head_sum_kernel(recv_k, recv_v, gk_out, gv_out):
+    head_width = recv_k.shape[2]
+    for head in range(recv_k.shape[0] // 2):
         cols = pl.ds(head * head_width, head_width)
         for landing, out_ref in ((recv_k, gk_out), (recv_v, gv_out)):
             out_ref[:, cols] = (
                 landing[2 * head].astype(jnp.float32) + landing[2 * head + 1].astype(jnp.float32)
             ).astype(out_ref.dtype)
-    for copy in copies:
-        copy.wait()
 
 
 def back_exchange(query_grad, key_grad, value_grad, groups, sources, collective):
@@ -452,16 +456,15 @@
     block = key_grad.shape[0] // sources
     vmem = pl.BlockSpec(memory_space=pltpu.VMEM)
     grad_shape = jax.ShapeDtypeStruct((block, sources // 2 * head_width), key_grad.dtype)
+    landing = jax.ShapeDtypeStruct((sources, block, head_width), key_grad.dtype)
     sems = pltpu.SemaphoreType.DMA((groups,))
-    return pl.pallas_call(
+    grad_queries, recv_k, recv_v = pl.pallas_call(
         back_kernel,
-        out_shape=(jax.ShapeDtypeStruct(query_grad.shape, query_grad.dtype), grad_shape, grad_shape),
+        out_shape=(jax.ShapeDtypeStruct(query_grad.shape, query_grad.dtype), landing, landing),
         in_specs=[vmem, vmem, vmem],
         out_specs=(vmem, vmem, vmem),
         scratch_shapes=[
             pltpu.VMEM(query_grad.shape, query_grad.dtype),
-            pltpu.VMEM((sources, block, head_width), key_grad.dtype),
-            pltpu.VMEM((sources, block, head_width), key_grad.dtype),
             sems,
             sems,
             sems,
@@ -471,6 +474,13 @@
         ],
         compiler_params=pltpu.CompilerParams(collective_id=collective, has_side_effects=True),
     )(query_grad, key_grad, value_grad)
+    grad_keys, grad_values = pl.pallas_call(
+        head_sum_kernel,
+        out_shape=(grad_shape, grad_shape),
+        in_specs=[vmem, vmem],
+        out_specs=(vmem, vmem),
+    )(recv_k, recv_v)
+    return grad_queries, grad_keys, grad_values
 
 
 def gather_kernel(k_ref, v_ref, k_out, v_out, send_sem, recv_sem, pair_send, pair_recv):

time: 150 us -> 148 us (0.987); the launches traced: 149 us -> 145 us
  Pallas kernels: 143 us -> 141 us
  local copies, waits for them, and re-layouts: 5.08 us -> 3.11 us
    pallas_call x1, Pallas kernels: 49.7 us -> 45.6 us  [back_exchange(): pl.pallas_call(back_kernel, out_shape=(jax.ShapeDtypeStruct(query_grad.sh...]
    pallas_call x0 -> x1, Pallas kernels: none -> 2.86 us  [back_exchange(): pl.pallas_call(head_sum_kernel, out_shape=(grad_shape, grad_shape), in_sp...]
    unnamed x14 -> x8, local copies, waits for them, and re-layouts: 4.4 us -> 2.42 us
    pallas_call x1, Pallas kernels: 48.7 us -> 50.5 us  [grp_combine(): pl.pallas_call(combine_kernel, out_shape=(jax.ShapeDtypeStruct(accum.shap...]
where the time goes in v14:
time: 148 us; the launch traced here: 145 us
  Pallas kernels  141 us (95%)
  local copies, waits for them, and re-layouts  3.11 us (2%)
    pallas_call x1, Pallas kernels, grp_combine(): pl.pallas_call(combine_kernel, out_shape=(jax.ShapeDtypeStruct(accum.shap...  50.5 us
    pallas_call x1, Pallas kernels, back_exchange(): pl.pallas_call(back_kernel, out_shape=(jax.ShapeDtypeStruct(query_grad.sh...  45.6 us
    pallas_call x1, Pallas kernels, seq_gather(): pl.pallas_call(gather_kernel, out_shape=(out, out), in_specs=[vmem, vmem]...  31 us
    pallas_call x1, Pallas kernels, backward_item(): pl.pallas_call(lambda *refs: backward_kernel(softmax_scale, *refs), out_s...  6.27 us
    pallas_call x1, Pallas kernels, forward_item(): pl.pallas_call(lambda *refs: forward_kernel(softmax_scale, *refs), out_sh...  4.88 us

profile of v14, /device:TPU:1, one launch (start us, length us, event | category | flops | bytes accessed | tf_op | source)
XLA Modules:
  0.0 145.5 jit_solution(16987572921597352705)
XLA Ops:
  1.3 0.0 copy-start.2
  1.3 0.7 copy-done.2
  2.0 0.7 copy.10.refs_0_
  2.6 31.0 %shard_map.93 = (bf16[32,2,64,128]{3,2,1,0:T(8,128)(2,1)}, bf16[32,2,64,128]{3,2,1,0:T(8,128)(2,1)}) custom-call(bf16[128,2048]{1,0:T(8,128)(2,1)} %k_ref.1, bf16[128,2048]{1,0:T(8,128)(2,1)} %v_ref.1), custom_call_target="tpu_custom_call" | custom-call | tf_op jit(solution)/shard_map/pallas_call | solution.py:542
  33.6 4.9 %shard_map.94 = (bf16[16,64,128]{2,1,0:T(8,128)(2,1)}, f32[16,8,128]{2,1,0:T(8,128)}) custom-call(s32[9,2]{1,0:T(8,128)} %copy.10.refs_0_, s32[1]{0:T(128)} %bitcast.10.refs_1_, bf16[1024,128]{1,0:T(8,128)(2,1)} %bitcast.18, bf16[4096,128]{1,0:T(8,128)(2,1)} %bitcast.12, bf16[4096,128]{1,0:T(8,128)(2,1)} %bitcast.14), custom_call_target="tpu_custom_call" | custom-call | tf_op jit(solution)/shard_map/pallas_call | solution.py:74
  38.5 50.5 %shard_map.95 = (bf16[16,64,128]{2,1,0:T(8,128)(2,1)}, f32[16,8,128]{2,1,0:T(8,128)}) custom-call(bf16[16,64,128]{2,1,0:T(8,128)(2,1)} %get-tuple-element.20.acc_in, f32[16,8,128]{2,1,0:T(8,128)} %get-tuple-element.21.stats_in), custom_call_target="tpu_custom_call" | custom-call | tf_op jit(solution)/shard_map/pallas_call | solution.py:357
  89.0 6.3 %shard_map.96 = (bf16[1024,128]{1,0:T(8,128)(2,1)}, bf16[4096,128]{1,0:T(8,128)(2,1)}, bf16[4096,128]{1,0:T(8,128)(2,1)}) custom-call(s32[9,2]{1,0:T(8,128)} %copy.10.refs_0_, s32[1]{0:T(128)} %bitcast.11.refs_1_, bf16[1024,128]{1,0:T(8,128)(2,1)} %bitcast.19, bf16[4096,128]{1,0:T(8,128)(2,1)} %bitcast.13, bf16[4096,128]{1,0:T(8,128)(2,1)} %bitcast.15, ...), custom_call_target="tpu_custom_call" | custom-call | tf_op jit(solution)/shard_map/pallas_call | solution.py:155
  95.3 45.6 %shard_map.97 = (bf16[16,64,128]{2,1,0:T(8,128)(2,1)}, bf16[32,128,128]{2,1,0:T(8,128)(2,1)}, bf16[32,128,128]{2,1,0:T(8,128)(2,1)}) custom-call(bf16[16,64,128]{2,1,0:T(8,128)(2,1)} %bitcast.21, bf16[4096,128]{1,0:T(8,128)(2,1)} %get-tuple-element.25.dk_in, bf16[4096,128]{1,0:T(8,128)(2,1)} %get-tuple-element.26.dv_in), custom_call_target="tpu_custom_call" | custom-call | tf_op jit(solution)/shard_map/pallas_call | solution.py:461
  140.8 0.0 copy-start
  140.9 2.9 %shard_map.98 = (bf16[128,2048]{1,0:T(8,128)(2,1)}, bf16[128,2048]{1,0:T(8,128)(2,1)}) custom-call(bf16[32,128,128]{2,1,0:T(8,128)(2,1)} %get-tuple-element.28.recv_k, bf16[32,128,128]{2,1,0:T(8,128)(2,1)} %get-tuple-element.29.recv_v), custom_call_target="tpu_custom_call" | custom-call | tf_op jit(solution)/shard_map/pallas_call | solution.py:477
  143.7 0.0 copy-done
  143.7 0.0 copy-start.1
  143.7 0.7 copy.15
  144.4 0.3 copy-done.1
  144.8 0.7 copy.16
Async XLA Ops:
  1.3 0.7 copy-start.2
  140.8 2.9 %copy-start = (bf16[16,64,128]{2,1,0:T(8,128)(2,1)S(1)}, bf16[16,64,128]{2,1,0:T(8,128)(2,1)}, u32[]{:S(2)}) copy-start(bf16[16,64,128]{2,1,0:T(8,128)(2,1)} %get-tuple-element.22) | copy-start | bytes 786436
  143.7 1.0 copy-start.1

commit v15 on v13

--- a/solution.py
+++ b/solution.py
@@ -507,21 +507,28 @@
     own_cols = pl.ds(pl.multiple_of(head * head_width, head_width), head_width)
     k_out[me, mine] = k_ref[own_rows, own_cols]
     v_out[me, mine] = v_ref[own_rows, own_cols]
-    for copy in copies:
-        copy.wait()
-    copies = []
-    for index, landing in enumerate((k_out, v_out)):
-        copy = pltpu.make_async_remote_copy(
-            src_ref=landing.at[:, mine],
-            dst_ref=landing.at[:, mine],
-            send_sem=pair_send.at[index],
-            recv_sem=pair_recv.at[index],
-            device_id=(grp_here, partner),
-            device_id_type=mesh_ids,
-        )
-        copy.start()
-        copies.append(copy)
-    for copy in copies:
+    forwards = []
+
+    def forward(step, block, sources_of):
+        for index, (landing, source) in enumerate(zip((k_out, v_out), sources_of)):
+            copy = pltpu.make_async_remote_copy(
+                src_ref=source,
+                dst_ref=landing.at[block, mine],
+                send_sem=pair_send.at[index, step],
+                recv_sem=pair_recv.at[index, step],
+                device_id=(grp_here, partner),
+                device_id_type=mesh_ids,
+            )
+            copy.start()
+            forwards.append(copy)
+
+    forward(0, me, (k_ref.at[own_rows, own_cols], v_ref.at[own_rows, own_cols]))
+    for step in range(1, sources):
+        for copy in copies[2 * (step - 1) : 2 * step]:
+            copy.wait()
+        block = lax.rem(me + sources - step, sources)
+        forward(step, block, (k_out.at[block, mine], v_out.at[block, mine]))
+    for copy in forwards:
         copy.wait()
 
 
@@ -537,8 +544,8 @@
         scratch_shapes=[
             pltpu.SemaphoreType.DMA((2, sources)),
             pltpu.SemaphoreType.DMA((2, sources)),
-            pltpu.SemaphoreType.DMA((2,)),
-            pltpu.SemaphoreType.DMA((2,)),
+            pltpu.SemaphoreType.DMA((2, sources)),
+            pltpu.SemaphoreType.DMA((2, sources)),
         ],
         compiler_params=pltpu.CompilerParams(collective_id=collective, has_side_effects=True),
     )(scene_keys, scene_values)

time: 150 us -> 149 us (level)
  no operation moved by 1% of the time
where the time goes in v15:
time: 149 us
  Pallas kernels  142 us (95%)
  local copies, waits for them, and re-layouts  5.08 us (3%)
    pallas_call x1, Pallas kernels, back_exchange(): pl.pallas_call(back_kernel, out_shape=(jax.ShapeDtypeStruct(query_grad.sh...  49.2 us
    pallas_call x1, Pallas kernels, grp_combine(): pl.pallas_call(combine_kernel, out_shape=(jax.ShapeDtypeStruct(accum.shap...  49.1 us
    pallas_call x1, Pallas kernels, seq_gather(): pl.pallas_call(gather_kernel, out_shape=(out, out), in_specs=[vmem, vmem]...  30.9 us
    pallas_call x1, Pallas kernels, backward_item(): pl.pallas_call(lambda *refs: backward_kernel(softmax_scale, *refs), out_s...  7.36 us
    pallas_call x1, Pallas kernels, forward_item(): pl.pallas_call(lambda *refs: forward_kernel(softmax_scale, *refs), out_sh...  5.97 us
    unnamed x14, local copies, waits for them, and re-layouts  4.4 us

profile of v15, /device:TPU:1, one launch (start us, length us, event | category | flops | bytes accessed | tf_op | source)
XLA Modules:
  0.0 148.9 jit_solution(4389664039583960604)
XLA Ops:
  1.3 0.0 copy-start.4
  1.3 0.7 copy-done.4
  2.0 0.7 copy.10.refs_0_
  2.6 30.9 %shard_map.93 = (bf16[32,2,64,128]{3,2,1,0:T(8,128)(2,1)}, bf16[32,2,64,128]{3,2,1,0:T(8,128)(2,1)}) custom-call(bf16[128,2048]{1,0:T(8,128)(2,1)} %k_ref.1, bf16[128,2048]{1,0:T(8,128)(2,1)} %v_ref.1), custom_call_target="tpu_custom_call" | custom-call | tf_op jit(solution)/shard_map/pallas_call | solution.py:539
  33.5 6.0 %shard_map.94 = (bf16[16,64,128]{2,1,0:T(8,128)(2,1)}, f32[16,8,128]{2,1,0:T(8,128)}) custom-call(s32[9,2]{1,0:T(8,128)} %copy.10.refs_0_, s32[1]{0:T(128)} %bitcast.10.refs_1_, bf16[1024,128]{1,0:T(8,128)(2,1)} %bitcast.18, bf16[4096,128]{1,0:T(8,128)(2,1)} %bitcast.12, bf16[4096,128]{1,0:T(8,128)(2,1)} %bitcast.14), custom_call_target="tpu_custom_call" | custom-call | tf_op jit(solution)/shard_map/pallas_call | solution.py:74
  39.5 49.1 %shard_map.95 = (bf16[16,64,128]{2,1,0:T(8,128)(2,1)}, f32[16,8,128]{2,1,0:T(8,128)}) custom-call(bf16[16,64,128]{2,1,0:T(8,128)(2,1)} %get-tuple-element.18.acc_in, f32[16,8,128]{2,1,0:T(8,128)} %get-tuple-element.19.stats_in), custom_call_target="tpu_custom_call" | custom-call | tf_op jit(solution)/shard_map/pallas_call | solution.py:357
  88.6 7.4 %shard_map.96 = (bf16[1024,128]{1,0:T(8,128)(2,1)}, bf16[4096,128]{1,0:T(8,128)(2,1)}, bf16[4096,128]{1,0:T(8,128)(2,1)}) custom-call(s32[9,2]{1,0:T(8,128)} %copy.10.refs_0_, s32[1]{0:T(128)} %bitcast.11.refs_1_, bf16[1024,128]{1,0:T(8,128)(2,1)} %bitcast.19, bf16[4096,128]{1,0:T(8,128)(2,1)} %bitcast.13, bf16[4096,128]{1,0:T(8,128)(2,1)} %bitcast.15, ...), custom_call_target="tpu_custom_call" | custom-call | tf_op jit(solution)/shard_map/pallas_call | solution.py:155
  95.9 0.0 copy-start
  95.9 49.2 %shard_map.97 = (bf16[16,64,128]{2,1,0:T(8,128)(2,1)}, bf16[128,2048]{1,0:T(8,128)(2,1)}, bf16[128,2048]{1,0:T(8,128)(2,1)}) custom-call(bf16[16,64,128]{2,1,0:T(8,128)(2,1)} %bitcast.21, bf16[4096,128]{1,0:T(8,128)(2,1)} %get-tuple-element.23.dk_in, bf16[4096,128]{1,0:T(8,128)(2,1)} %get-tuple-element.24.dv_in), custom_call_target="tpu_custom_call" | custom-call | tf_op jit(solution)/shard_map/pallas_call | solution.py:456
  145.1 0.0 copy-start.3
  145.1 0.0 copy-done
  145.1 0.0 copy-start.2
  145.1 0.7 copy.17
  145.8 0.3 copy-done.3
  146.1 0.7 copy.18
  146.8 0.0 copy-done.2
  146.8 0.0 copy-start.1
  146.8 0.8 copy.19
  147.6 0.4 copy-done.1
  148.1 0.8 copy.20
Async XLA Ops:
  1.3 0.7 copy-start.4
  95.9 49.2 %copy-start = (bf16[16,64,128]{2,1,0:T(8,128)(2,1)S(1)}, bf16[16,64,128]{2,1,0:T(8,128)(2,1)}, u32[]{:S(2)}) copy-start(bf16[16,64,128]{2,1,0:T(8,128)(2,1)} %get-tuple-element.20) | copy-start | bytes 786436
  145.1 1.0 copy-start.3
  145.1 1.7 %copy-start.2 = (bf16[128,2048]{1,0:T(8,128)(2,1)S(1)}, bf16[128,2048]{1,0:T(8,128)(2,1)}, u32[]{:S(2)}) copy-start(bf16[128,2048]{1,0:T(8,128)(2,1)} %get-tuple-element.34) | copy-start | bytes 1572868
  146.8 1.2 copy-start.1

commit v16 on v15

--- a/solution.py
+++ b/solution.py
@@ -387,6 +387,19 @@
             barrier, inc=1, device_id=(me, lax.rem(lane + step, sources)), device_id_type=mesh_ids
         )
     pl.semaphore_wait(barrier, groups - 1 + sources - 1)
+    copies = []
+    for step in range(1, groups):
+        target = lax.rem(me + step, groups)
+        copy = pltpu.make_async_remote_copy(
+            src_ref=dq_in.at[target],
+            dst_ref=part_ref.at[me],
+            send_sem=send_sem.at[step],
+            recv_sem=recv_sem.at[step],
+            device_id=(target, lane),
+            device_id_type=mesh_ids,
+        )
+        copy.start()
+        copies.append(copy)
     returns = []
     for step in range(1, sources):
         target = lax.rem(lane + step, sources)
@@ -402,19 +415,6 @@
             )
             copy.start()
             returns.append(copy)
-    copies = []
-    for step in range(1, groups):
-        target = lax.rem(me + step, groups)
-        copy = pltpu.make_async_remote_copy(
-            src_ref=dq_in.at[target],
-            dst_ref=part_ref.at[me],
-            send_sem=send_sem.at[step],
-            recv_sem=recv_sem.at[step],
-            device_id=(target, lane),
-            device_id_type=mesh_ids,
-        )
-        copy.start()
-        copies.append(copy)
     own_rows = pl.ds(pl.multiple_of(lane * block, block), block)
     recv_k[lane] = dk_in[own_rows, :]
     recv_v[lane] = dv_in[own_rows, :]

time: 149 us -> 146 us (0.980); the launches traced: 149 us -> 144 us
  Pallas kernels: 142 us -> 138 us
    pallas_call x1, Pallas kernels: 49.2 us -> 43.5 us  [back_exchange(): pl.pallas_call(back_kernel, out_shape=(jax.ShapeDtypeStruct(query_grad.sh...]
    pallas_call x1, Pallas kernels: 49.1 us -> 52.2 us  [grp_combine(): pl.pallas_call(combine_kernel, out_shape=(jax.ShapeDtypeStruct(accum.shap...]
where the time goes in v16:
time: 146 us; the launch traced here: 144 us
  Pallas kernels  138 us (95%)
  local copies, waits for them, and re-layouts  5.08 us (3%)
    pallas_call x1, Pallas kernels, grp_combine(): pl.pallas_call(combine_kernel, out_shape=(jax.ShapeDtypeStruct(accum.shap...  52.2 us
    pallas_call x1, Pallas kernels, back_exchange(): pl.pallas_call(back_kernel, out_shape=(jax.ShapeDtypeStruct(query_grad.sh...  43.5 us
    pallas_call x1, Pallas kernels, seq_gather(): pl.pallas_call(gather_kernel, out_shape=(out, out), in_specs=[vmem, vmem]...  30.9 us
    pallas_call x1, Pallas kernels, backward_item(): pl.pallas_call(lambda *refs: backward_kernel(softmax_scale, *refs), out_s...  6.26 us
    pallas_call x1, Pallas kernels, forward_item(): pl.pallas_call(lambda *refs: forward_kernel(softmax_scale, *refs), out_sh...  4.88 us
    unnamed x14, local copies, waits for them, and re-layouts  4.4 us

profile of v16, /device:TPU:1, one launch (start us, length us, event | category | flops | bytes accessed | tf_op | source)
XLA Modules:
  0.0 144.1 jit_solution(11690034487630712941)
XLA Ops:
  1.3 0.0 copy-start.4
  1.3 0.7 copy-done.4
  2.0 0.7 copy.10.refs_0_
  2.6 30.9 %shard_map.93 = (bf16[32,2,64,128]{3,2,1,0:T(8,128)(2,1)}, bf16[32,2,64,128]{3,2,1,0:T(8,128)(2,1)}) custom-call(bf16[128,2048]{1,0:T(8,128)(2,1)} %k_ref.1, bf16[128,2048]{1,0:T(8,128)(2,1)} %v_ref.1), custom_call_target="tpu_custom_call" | custom-call | tf_op jit(solution)/shard_map/pallas_call | solution.py:539
  33.5 4.9 %shard_map.94 = (bf16[16,64,128]{2,1,0:T(8,128)(2,1)}, f32[16,8,128]{2,1,0:T(8,128)}) custom-call(s32[9,2]{1,0:T(8,128)} %copy.10.refs_0_, s32[1]{0:T(128)} %bitcast.10.refs_1_, bf16[1024,128]{1,0:T(8,128)(2,1)} %bitcast.18, bf16[4096,128]{1,0:T(8,128)(2,1)} %bitcast.12, bf16[4096,128]{1,0:T(8,128)(2,1)} %bitcast.14), custom_call_target="tpu_custom_call" | custom-call | tf_op jit(solution)/shard_map/pallas_call | solution.py:74
  38.4 52.2 %shard_map.95 = (bf16[16,64,128]{2,1,0:T(8,128)(2,1)}, f32[16,8,128]{2,1,0:T(8,128)}) custom-call(bf16[16,64,128]{2,1,0:T(8,128)(2,1)} %get-tuple-element.18.acc_in, f32[16,8,128]{2,1,0:T(8,128)} %get-tuple-element.19.stats_in), custom_call_target="tpu_custom_call" | custom-call | tf_op jit(solution)/shard_map/pallas_call | solution.py:357
  90.6 6.3 %shard_map.96 = (bf16[1024,128]{1,0:T(8,128)(2,1)}, bf16[4096,128]{1,0:T(8,128)(2,1)}, bf16[4096,128]{1,0:T(8,128)(2,1)}) custom-call(s32[9,2]{1,0:T(8,128)} %copy.10.refs_0_, s32[1]{0:T(128)} %bitcast.11.refs_1_, bf16[1024,128]{1,0:T(8,128)(2,1)} %bitcast.19, bf16[4096,128]{1,0:T(8,128)(2,1)} %bitcast.13, bf16[4096,128]{1,0:T(8,128)(2,1)} %bitcast.15, ...), custom_call_target="tpu_custom_call" | custom-call | tf_op jit(solution)/shard_map/pallas_call | solution.py:155
  96.9 0.0 copy-start
  96.9 43.5 %shard_map.97 = (bf16[16,64,128]{2,1,0:T(8,128)(2,1)}, bf16[128,2048]{1,0:T(8,128)(2,1)}, bf16[128,2048]{1,0:T(8,128)(2,1)}) custom-call(bf16[16,64,128]{2,1,0:T(8,128)(2,1)} %bitcast.21, bf16[4096,128]{1,0:T(8,128)(2,1)} %get-tuple-element.23.dk_in, bf16[4096,128]{1,0:T(8,128)(2,1)} %get-tuple-element.24.dv_in), custom_call_target="tpu_custom_call" | custom-call | tf_op jit(solution)/shard_map/pallas_call | solution.py:456
  140.4 0.0 copy-start.3
  140.4 0.0 copy-done
  140.4 0.0 copy-start.2
  140.4 0.7 copy.17
  141.1 0.3 copy-done.3
  141.4 0.7 copy.18
  142.1 0.0 copy-done.2
  142.1 0.0 copy-start.1
  142.1 0.8 copy.19
  142.9 0.4 copy-done.1
  143.3 0.8 copy.20
Async XLA Ops:
  1.3 0.7 copy-start.4
  96.9 43.5 %copy-start = (bf16[16,64,128]{2,1,0:T(8,128)(2,1)S(1)}, bf16[16,64,128]{2,1,0:T(8,128)(2,1)}, u32[]{:S(2)}) copy-start(bf16[16,64,128]{2,1,0:T(8,128)(2,1)} %get-tuple-element.20) | copy-start | bytes 786436
  140.4 1.0 copy-start.3
  140.4 1.7 %copy-start.2 = (bf16[128,2048]{1,0:T(8,128)(2,1)S(1)}, bf16[128,2048]{1,0:T(8,128)(2,1)}, u32[]{:S(2)}) copy-start(bf16[128,2048]{1,0:T(8,128)(2,1)} %get-tuple-element.34) | copy-start | bytes 1572868
  142.1 1.2 copy-start.1

commit v17 on v15

--- a/solution.py
+++ b/solution.py
@@ -473,7 +473,7 @@
     )(query_grad, key_grad, value_grad)
 
 
-def gather_kernel(k_ref, v_ref, k_out, v_out, send_sem, recv_sem, pair_send, pair_recv):
+def gather_kernel(k_ref, v_ref, k_out, v_out, send_sem, recv_sem, pair_send, pair_recv, own_sem):
     sources, halves, half, head_width = k_out.shape
     me = lax.axis_index("seq")
     grp_here = lax.axis_index("grp")
@@ -505,8 +505,11 @@
             copies.append(copy)
     own_rows = pl.ds(pl.multiple_of(mine * half, half), half)
     own_cols = pl.ds(pl.multiple_of(head * head_width, head_width), head_width)
-    k_out[me, mine] = k_ref[own_rows, own_cols]
-    v_out[me, mine] = v_ref[own_rows, own_cols]
+    own = []
+    for index, (source, landing) in enumerate(((k_ref, k_out), (v_ref, v_out))):
+        copy = pltpu.make_async_copy(source.at[own_rows, own_cols], landing.at[me, mine], own_sem.at[index])
+        copy.start()
+        own.append(copy)
     forwards = []
 
     def forward(step, block, sources_of):
@@ -528,7 +531,7 @@
             copy.wait()
         block = lax.rem(me + sources - step, sources)
         forward(step, block, (k_out.at[block, mine], v_out.at[block, mine]))
-    for copy in forwards:
+    for copy in forwards + own:
         copy.wait()
 
 
@@ -539,13 +542,14 @@
     return pl.pallas_call(
         gather_kernel,
         out_shape=(out, out),
-        in_specs=[vmem, vmem],
+        in_specs=[pl.BlockSpec(memory_space=pl.ANY)] * 2,
         out_specs=(vmem, vmem),
         scratch_shapes=[
             pltpu.SemaphoreType.DMA((2, sources)),
             pltpu.SemaphoreType.DMA((2, sources)),
             pltpu.SemaphoreType.DMA((2, sources)),
             pltpu.SemaphoreType.DMA((2, sources)),
+            pltpu.SemaphoreType.DMA((2,)),
         ],
         compiler_params=pltpu.CompilerParams(collective_id=collective, has_side_effects=True),
     )(scene_keys, scene_values)

time: 149 us -> 151 us (1.013)
  Pallas kernels: 142 us -> 144 us
    pallas_call x1, Pallas kernels: 49.1 us -> 51.3 us  [grp_combine(): pl.pallas_call(combine_kernel, out_shape=(jax.ShapeDtypeStruct(accum.shap...]
    pallas_call x1, Pallas kernels: 49.2 us -> 47.4 us  [back_exchange(): pl.pallas_call(back_kernel, out_shape=(jax.ShapeDtypeStruct(query_grad.sh...]
where the time goes in v17:
time: 151 us
  Pallas kernels  144 us (95%)
  local copies, waits for them, and re-layouts  5.08 us (3%)
    pallas_call x1, Pallas kernels, grp_combine(): pl.pallas_call(combine_kernel, out_shape=(jax.ShapeDtypeStruct(accum.shap...  51.3 us
    pallas_call x1, Pallas kernels, back_exchange(): pl.pallas_call(back_kernel, out_shape=(jax.ShapeDtypeStruct(query_grad.sh...  47.4 us
    pallas_call x1, Pallas kernels, seq_gather(): pl.pallas_call(gather_kernel, out_shape=(out, out), in_specs=[pl.BlockSpe...  30 us
    pallas_call x1, Pallas kernels, backward_item(): pl.pallas_call(lambda *refs: backward_kernel(softmax_scale, *refs), out_s...  8.46 us
    pallas_call x1, Pallas kernels, forward_item(): pl.pallas_call(lambda *refs: forward_kernel(softmax_scale, *refs), out_sh...  7.05 us
    unnamed x14, local copies, waits for them, and re-layouts  4.4 us

profile of v17, /device:TPU:1, one launch (start us, length us, event | category | flops | bytes accessed | tf_op | source)
XLA Modules:
  0.0 150.7 jit_solution(10801045012649362911)
XLA Ops:
  1.3 0.0 copy-start.4
  1.3 0.7 copy-done.4
  2.0 0.7 copy.10.refs_0_
  2.6 30.0 %shard_map.93 = (bf16[32,2,64,128]{3,2,1,0:T(8,128)(2,1)}, bf16[32,2,64,128]{3,2,1,0:T(8,128)(2,1)}) custom-call(bf16[128,2048]{1,0:T(8,128)(2,1)} %k_ref.1, bf16[128,2048]{1,0:T(8,128)(2,1)} %v_ref.1), custom_call_target="tpu_custom_call" | custom-call | tf_op jit(solution)/shard_map/pallas_call | solution.py:542
  32.6 7.1 %shard_map.94 = (bf16[16,64,128]{2,1,0:T(8,128)(2,1)}, f32[16,8,128]{2,1,0:T(8,128)}) custom-call(s32[9,2]{1,0:T(8,128)} %copy.10.refs_0_, s32[1]{0:T(128)} %bitcast.10.refs_1_, bf16[1024,128]{1,0:T(8,128)(2,1)} %bitcast.18, bf16[4096,128]{1,0:T(8,128)(2,1)} %bitcast.12, bf16[4096,128]{1,0:T(8,128)(2,1)} %bitcast.14), custom_call_target="tpu_custom_call" | custom-call | tf_op jit(solution)/shard_map/pallas_call | solution.py:74
  39.7 51.3 %shard_map.95 = (bf16[16,64,128]{2,1,0:T(8,128)(2,1)}, f32[16,8,128]{2,1,0:T(8,128)}) custom-call(bf16[16,64,128]{2,1,0:T(8,128)(2,1)} %get-tuple-element.18.acc_in, f32[16,8,128]{2,1,0:T(8,128)} %get-tuple-element.19.stats_in), custom_call_target="tpu_custom_call" | custom-call | tf_op jit(solution)/shard_map/pallas_call | solution.py:357
  91.0 8.5 %shard_map.96 = (bf16[1024,128]{1,0:T(8,128)(2,1)}, bf16[4096,128]{1,0:T(8,128)(2,1)}, bf16[4096,128]{1,0:T(8,128)(2,1)}) custom-call(s32[9,2]{1,0:T(8,128)} %copy.10.refs_0_, s32[1]{0:T(128)} %bitcast.11.refs_1_, bf16[1024,128]{1,0:T(8,128)(2,1)} %bitcast.19, bf16[4096,128]{1,0:T(8,128)(2,1)} %bitcast.13, bf16[4096,128]{1,0:T(8,128)(2,1)} %bitcast.15, ...), custom_call_target="tpu_custom_call" | custom-call | tf_op jit(solution)/shard_map/pallas_call | solution.py:155
  99.5 0.0 copy-start
  99.5 47.4 %shard_map.97 = (bf16[16,64,128]{2,1,0:T(8,128)(2,1)}, bf16[128,2048]{1,0:T(8,128)(2,1)}, bf16[128,2048]{1,0:T(8,128)(2,1)}) custom-call(bf16[16,64,128]{2,1,0:T(8,128)(2,1)} %bitcast.21, bf16[4096,128]{1,0:T(8,128)(2,1)} %get-tuple-element.23.dk_in, bf16[4096,128]{1,0:T(8,128)(2,1)} %get-tuple-element.24.dv_in), custom_call_target="tpu_custom_call" | custom-call | tf_op jit(solution)/shard_map/pallas_call | solution.py:456
  146.9 0.0 copy-start.3
  146.9 0.0 copy-done
  146.9 0.0 copy-start.2
  147.0 0.7 copy.17
  147.7 0.3 copy-done.3
  148.0 0.7 copy.18
  148.7 0.0 copy-done.2
  148.7 0.0 copy-start.1
  148.7 0.8 copy.19
  149.5 0.4 copy-done.1
  149.9 0.8 copy.20
Async XLA Ops:
  1.3 0.7 copy-start.4
  99.5 47.4 %copy-start = (bf16[16,64,128]{2,1,0:T(8,128)(2,1)S(1)}, bf16[16,64,128]{2,1,0:T(8,128)(2,1)}, u32[]{:S(2)}) copy-start(bf16[16,64,128]{2,1,0:T(8,128)(2,1)} %get-tuple-element.20) | copy-start | bytes 786436
  146.9 1.0 copy-start.3
  146.9 1.7 %copy-start.2 = (bf16[128,2048]{1,0:T(8,128)(2,1)S(1)}, bf16[128,2048]{1,0:T(8,128)(2,1)}, u32[]{:S(2)}) copy-start(bf16[128,2048]{1,0:T(8,128)(2,1)} %get-tuple-element.34) | copy-start | bytes 1572868
  148.7 1.2 copy-start.1

commit v18 on v15

--- a/solution.py
+++ b/solution.py
@@ -311,22 +311,25 @@
             )
             copy.start()
             copies.append(copy)
-    acc_part[me] = acc_in[me]
-    stats_part[me] = stats_in[me]
-    for copy in copies:
-        copy.wait()
-    columns = jnp.transpose(stats_part[...].reshape(groups * 8, 128))
-    maxima = [columns[:chunk_rows, 8 * g : 8 * g + 1] for g in range(groups)]
-    totals = [columns[chunk_rows:, 8 * g : 8 * g + 1] for g in range(groups)]
-    top = maxima[0]
-    for g in range(1, groups):
-        top = jnp.maximum(top, maxima[g])
-    row_total = jnp.zeros_like(top)
-    row_accum = jnp.zeros((chunk_rows, head_width), jnp.float32)
-    for g in range(groups):
-        shrink = jnp.exp(maxima[g] - top)
-        row_total = row_total + totals[g] * shrink
-        row_accum = row_accum + acc_part[g].astype(jnp.float32) * shrink
+
+    def columns_of(stats_block):
+        spread_row = jnp.broadcast_to(stats_block[0:1, :], (2 * chunk_rows, 2 * chunk_rows))
+        columns = jnp.transpose(spread_row)
+        return columns[:chunk_rows, 0:1], columns[chunk_rows:, 0:1]
+
+    top, row_total = columns_of(stats_in[me])
+    row_accum = acc_in[me].astype(jnp.float32)
+    for step in range(1, groups):
+        for copy in copies[2 * (step - 1) : 2 * step]:
+            copy.wait()
+        sender = lax.rem(me + groups - step, groups)
+        their_max, their_total = columns_of(stats_part[sender])
+        new_top = jnp.maximum(top, their_max)
+        keep = jnp.exp(top - new_top)
+        take = jnp.exp(their_max - new_top)
+        row_total = row_total * keep + their_total * take
+        row_accum = row_accum * keep + acc_part[sender].astype(jnp.float32) * take
+        top = new_top
     out_ref[me] = (row_accum / row_total).astype(out_ref.dtype)
     spread = jnp.concatenate(
         [jnp.broadcast_to(top, (chunk_rows, 128)), jnp.broadcast_to(row_total, (chunk_rows, 128))], axis=0

time: 149 us -> 150 us (level)
    pallas_call x1, Pallas kernels: 49.2 us -> 51.1 us  [back_exchange(): pl.pallas_call(back_kernel, out_shape=(jax.ShapeDtypeStruct(query_grad.sh...]
where the time goes in v18:
time: 150 us
  Pallas kernels  143 us (95%)
  local copies, waits for them, and re-layouts  5.08 us (3%)
    pallas_call x1, Pallas kernels, back_exchange(): pl.pallas_call(back_kernel, out_shape=(jax.ShapeDtypeStruct(query_grad.sh...  51.1 us
    pallas_call x1, Pallas kernels, grp_combine(): pl.pallas_call(combine_kernel, out_shape=(jax.ShapeDtypeStruct(accum.shap...  48 us
    pallas_call x1, Pallas kernels, seq_gather(): pl.pallas_call(gather_kernel, out_shape=(out, out), in_specs=[vmem, vmem]...  30.9 us
    pallas_call x1, Pallas kernels, backward_item(): pl.pallas_call(lambda *refs: backward_kernel(softmax_scale, *refs), out_s...  7.37 us
    pallas_call x1, Pallas kernels, forward_item(): pl.pallas_call(lambda *refs: forward_kernel(softmax_scale, *refs), out_sh...  5.97 us
    unnamed x14, local copies, waits for them, and re-layouts  4.4 us

profile of v18, /device:TPU:1, one launch (start us, length us, event | category | flops | bytes accessed | tf_op | source)
XLA Modules:
  0.0 149.7 jit_solution(3325123239955298129)
XLA Ops:
  1.3 0.0 copy-start.4
  1.3 0.7 copy-done.4
  2.0 0.7 copy.10.refs_0_
  2.6 30.9 %shard_map.93 = (bf16[32,2,64,128]{3,2,1,0:T(8,128)(2,1)}, bf16[32,2,64,128]{3,2,1,0:T(8,128)(2,1)}) custom-call(bf16[128,2048]{1,0:T(8,128)(2,1)} %k_ref.1, bf16[128,2048]{1,0:T(8,128)(2,1)} %v_ref.1), custom_call_target="tpu_custom_call" | custom-call | tf_op jit(solution)/shard_map/pallas_call | solution.py:542
  33.5 6.0 %shard_map.94 = (bf16[16,64,128]{2,1,0:T(8,128)(2,1)}, f32[16,8,128]{2,1,0:T(8,128)}) custom-call(s32[9,2]{1,0:T(8,128)} %copy.10.refs_0_, s32[1]{0:T(128)} %bitcast.10.refs_1_, bf16[1024,128]{1,0:T(8,128)(2,1)} %bitcast.18, bf16[4096,128]{1,0:T(8,128)(2,1)} %bitcast.12, bf16[4096,128]{1,0:T(8,128)(2,1)} %bitcast.14), custom_call_target="tpu_custom_call" | custom-call | tf_op jit(solution)/shard_map/pallas_call | solution.py:74
  39.5 48.0 %shard_map.95 = (bf16[16,64,128]{2,1,0:T(8,128)(2,1)}, f32[16,8,128]{2,1,0:T(8,128)}) custom-call(bf16[16,64,128]{2,1,0:T(8,128)(2,1)} %get-tuple-element.18.acc_in, f32[16,8,128]{2,1,0:T(8,128)} %get-tuple-element.19.stats_in), custom_call_target="tpu_custom_call" | custom-call | tf_op jit(solution)/shard_map/pallas_call | solution.py:360
  87.5 7.4 %shard_map.96 = (bf16[1024,128]{1,0:T(8,128)(2,1)}, bf16[4096,128]{1,0:T(8,128)(2,1)}, bf16[4096,128]{1,0:T(8,128)(2,1)}) custom-call(s32[9,2]{1,0:T(8,128)} %copy.10.refs_0_, s32[1]{0:T(128)} %bitcast.11.refs_1_, bf16[1024,128]{1,0:T(8,128)(2,1)} %bitcast.19, bf16[4096,128]{1,0:T(8,128)(2,1)} %bitcast.13, bf16[4096,128]{1,0:T(8,128)(2,1)} %bitcast.15, ...), custom_call_target="tpu_custom_call" | custom-call | tf_op jit(solution)/shard_map/pallas_call | solution.py:155
  94.8 0.0 copy-start
  94.8 51.1 %shard_map.97 = (bf16[16,64,128]{2,1,0:T(8,128)(2,1)}, bf16[128,2048]{1,0:T(8,128)(2,1)}, bf16[128,2048]{1,0:T(8,128)(2,1)}) custom-call(bf16[16,64,128]{2,1,0:T(8,128)(2,1)} %bitcast.21, bf16[4096,128]{1,0:T(8,128)(2,1)} %get-tuple-element.23.dk_in, bf16[4096,128]{1,0:T(8,128)(2,1)} %get-tuple-element.24.dv_in), custom_call_target="tpu_custom_call" | custom-call | tf_op jit(solution)/shard_map/pallas_call | solution.py:459
  145.9 0.0 copy-start.3
  145.9 0.0 copy-done
  145.9 0.0 copy-start.2
  146.0 0.7 copy.17
  146.7 0.3 copy-done.3
  146.9 0.7 copy.18
  147.7 0.0 copy-done.2
  147.7 0.0 copy-start.1
  147.7 0.8 copy.19
  148.4 0.4 copy-done.1
  148.9 0.8 copy.20
Async XLA Ops:
  1.3 0.7 copy-start.4
  94.8 51.1 %copy-start = (bf16[16,64,128]{2,1,0:T(8,128)(2,1)S(1)}, bf16[16,64,128]{2,1,0:T(8,128)(2,1)}, u32[]{:S(2)}) copy-start(bf16[16,64,128]{2,1,0:T(8,128)(2,1)} %get-tuple-element.20) | copy-start | bytes 786436
  145.9 1.0 copy-start.3
  145.9 1.7 %copy-start.2 = (bf16[128,2048]{1,0:T(8,128)(2,1)S(1)}, bf16[128,2048]{1,0:T(8,128)(2,1)}, u32[]{:S(2)}) copy-start(bf16[128,2048]{1,0:T(8,128)(2,1)} %get-tuple-element.34) | copy-start | bytes 1572868
  147.7 1.2 copy-start.1

commit v19 on v15

--- a/solution.py
+++ b/solution.py
@@ -301,9 +301,10 @@
             (acc_in, acc_part, send_acc, recv_acc),
             (stats_in, stats_part, send_stats, recv_stats),
         ):
+            rows = pl.ds(0, 1) if source is stats_in else pl.ds(0, source.shape[1])
             copy = pltpu.make_async_remote_copy(
-                src_ref=source.at[target],
-                dst_ref=landing.at[me],
+                src_ref=source.at[target, rows],
+                dst_ref=landing.at[me, rows],
                 send_sem=sent.at[step],
                 recv_sem=got.at[step],
                 device_id=(target, lane),
@@ -336,9 +337,10 @@
     for step in range(1, groups):
         target = lax.rem(me + step, groups)
         for source, sent, got in ((out_ref, back_send, back_recv), (stats_out, stat_send, stat_recv)):
+            rows = pl.ds(0, 1) if source is stats_out else pl.ds(0, source.shape[1])
             copy = pltpu.make_async_remote_copy(
-                src_ref=source.at[me],
-                dst_ref=source.at[me],
+                src_ref=source.at[me, rows],
+                dst_ref=source.at[me, rows],
                 send_sem=sent.at[step],
                 recv_sem=got.at[step],
                 device_id=(target, lane),

time: 149 us -> 145 us (0.973); the launches traced: 149 us -> 142 us
  Pallas kernels: 142 us -> 136 us
    pallas_call x1, Pallas kernels: 49.1 us -> 43.7 us  [grp_combine(): pl.pallas_call(combine_kernel, out_shape=(jax.ShapeDtypeStruct(accum.shap...]
where the time goes in v19:
time: 145 us; the launch traced here: 142 us
  Pallas kernels  136 us (94%)
  local copies, waits for them, and re-layouts  5.08 us (4%)
    pallas_call x1, Pallas kernels, back_exchange(): pl.pallas_call(back_kernel, out_shape=(jax.ShapeDtypeStruct(query_grad.sh...  48 us
    pallas_call x1, Pallas kernels, grp_combine(): pl.pallas_call(combine_kernel, out_shape=(jax.ShapeDtypeStruct(accum.shap...  43.7 us
    pallas_call x1, Pallas kernels, seq_gather(): pl.pallas_call(gather_kernel, out_shape=(out, out), in_specs=[vmem, vmem]...  30.9 us
    pallas_call x1, Pallas kernels, backward_item(): pl.pallas_call(lambda *refs: backward_kernel(softmax_scale, *refs), out_s...  7.36 us
    pallas_call x1, Pallas kernels, forward_item(): pl.pallas_call(lambda *refs: forward_kernel(softmax_scale, *refs), out_sh...  5.97 us
    unnamed x14, local copies, waits for them, and re-layouts  4.4 us

profile of v19, /device:TPU:1, one launch (start us, length us, event | category | flops | bytes accessed | tf_op | source)
XLA Modules:
  0.0 142.2 jit_solution(9661568625702546968)
XLA Ops:
  1.3 0.0 copy-start.4
  1.3 0.7 copy-done.4
  2.0 0.7 copy.10.refs_0_
  2.6 30.9 %shard_map.93 = (bf16[32,2,64,128]{3,2,1,0:T(8,128)(2,1)}, bf16[32,2,64,128]{3,2,1,0:T(8,128)(2,1)}) custom-call(bf16[128,2048]{1,0:T(8,128)(2,1)} %k_ref.1, bf16[128,2048]{1,0:T(8,128)(2,1)} %v_ref.1), custom_call_target="tpu_custom_call" | custom-call | tf_op jit(solution)/shard_map/pallas_call | solution.py:541
  33.5 6.0 %shard_map.94 = (bf16[16,64,128]{2,1,0:T(8,128)(2,1)}, f32[16,8,128]{2,1,0:T(8,128)}) custom-call(s32[9,2]{1,0:T(8,128)} %copy.10.refs_0_, s32[1]{0:T(128)} %bitcast.10.refs_1_, bf16[1024,128]{1,0:T(8,128)(2,1)} %bitcast.18, bf16[4096,128]{1,0:T(8,128)(2,1)} %bitcast.12, bf16[4096,128]{1,0:T(8,128)(2,1)} %bitcast.14), custom_call_target="tpu_custom_call" | custom-call | tf_op jit(solution)/shard_map/pallas_call | solution.py:74
  39.5 43.7 %shard_map.95 = (bf16[16,64,128]{2,1,0:T(8,128)(2,1)}, f32[16,8,128]{2,1,0:T(8,128)}) custom-call(bf16[16,64,128]{2,1,0:T(8,128)(2,1)} %get-tuple-element.18.acc_in, f32[16,8,128]{2,1,0:T(8,128)} %get-tuple-element.19.stats_in), custom_call_target="tpu_custom_call" | custom-call | tf_op jit(solution)/shard_map/pallas_call | solution.py:359
  83.2 7.4 %shard_map.96 = (bf16[1024,128]{1,0:T(8,128)(2,1)}, bf16[4096,128]{1,0:T(8,128)(2,1)}, bf16[4096,128]{1,0:T(8,128)(2,1)}) custom-call(s32[9,2]{1,0:T(8,128)} %copy.10.refs_0_, s32[1]{0:T(128)} %bitcast.11.refs_1_, bf16[1024,128]{1,0:T(8,128)(2,1)} %bitcast.19, bf16[4096,128]{1,0:T(8,128)(2,1)} %bitcast.13, bf16[4096,128]{1,0:T(8,128)(2,1)} %bitcast.15, ...), custom_call_target="tpu_custom_call" | custom-call | tf_op jit(solution)/shard_map/pallas_call | solution.py:155
  90.5 0.0 copy-start
  90.5 48.0 %shard_map.97 = (bf16[16,64,128]{2,1,0:T(8,128)(2,1)}, bf16[128,2048]{1,0:T(8,128)(2,1)}, bf16[128,2048]{1,0:T(8,128)(2,1)}) custom-call(bf16[16,64,128]{2,1,0:T(8,128)(2,1)} %bitcast.21, bf16[4096,128]{1,0:T(8,128)(2,1)} %get-tuple-element.23.dk_in, bf16[4096,128]{1,0:T(8,128)(2,1)} %get-tuple-element.24.dv_in), custom_call_target="tpu_custom_call" | custom-call | tf_op jit(solution)/shard_map/pallas_call | solution.py:458
  138.5 0.0 copy-start.3
  138.5 0.0 copy-done
  138.5 0.0 copy-start.2
  138.5 0.7 copy.17
  139.2 0.3 copy-done.3
  139.5 0.7 copy.18
  140.2 0.0 copy-done.2
  140.2 0.0 copy-start.1
  140.2 0.8 copy.19
  141.0 0.4 copy-done.1
  141.4 0.8 copy.20
Async XLA Ops:
  1.3 0.7 copy-start.4
  90.5 48.0 %copy-start = (bf16[16,64,128]{2,1,0:T(8,128)(2,1)S(1)}, bf16[16,64,128]{2,1,0:T(8,128)(2,1)}, u32[]{:S(2)}) copy-start(bf16[16,64,128]{2,1,0:T(8,128)(2,1)} %get-tuple-element.20) | copy-start | bytes 786436
  138.5 1.0 copy-start.3
  138.5 1.7 %copy-start.2 = (bf16[128,2048]{1,0:T(8,128)(2,1)S(1)}, bf16[128,2048]{1,0:T(8,128)(2,1)}, u32[]{:S(2)}) copy-start(bf16[128,2048]{1,0:T(8,128)(2,1)} %get-tuple-element.34) | copy-start | bytes 1572868
  140.2 1.2 copy-start.1
